TPU v7x, 128 devices: a whole 4x4x4 slice. The times are simulated.
128 devices in a mesh: expert: 32 (over y, z, core), hidden: 4 (over x).
Axes of the slice: x: 4, y: 4, z: 4, core: 2. Of those that a mesh axis runs over, the one named last changes fastest.
Arguments:
- tokens: bfloat16 [4096, 2048], P('expert', 'hidden'), may hold values from -6 to 6
- cotangent: bfloat16 [4096, 2048], P('expert', 'hidden'), may hold values from -6 to 6
- gate_weight: bfloat16 [64, 2048, 1408], P('expert', 'hidden'), may hold values from -0.125 to 0.125
- up_weight: bfloat16 [64, 2048, 1408], P('expert', 'hidden'), may hold values from -0.125 to 0.125
- down_weight: bfloat16 [64, 2048, 1408], P('expert', 'hidden'), may hold values from -0.15625 to 0.15625
- routing: int32 [4096, 6], P('expert'), may hold values from 0 to 63, all different within a row; in each aligned block of 128 rows (0 to 127, 128 to 255, ...) at most 16 rows name the same one
- route_weight: float32 [4096, 6], P('expert'), may hold values from 0.05 to 1
- merge_source: int32 [16], replicated, may hold values from 2 to 61, as said below
- merge_target: int32 [16], replicated, may hold values from 0 to 63, as said below
- neuron_perm: int32 [16, 1408], replicated, may hold values from 0 to 1407, as said below
Outputs:
- mixed: bfloat16 [4096, 2048], P('expert', 'hidden')
- grad_gate: bfloat16 [64, 2048, 1408], P('expert', 'hidden')
- grad_up: bfloat16 [64, 2048, 1408], P('expert', 'hidden')
- grad_down: bfloat16 [64, 2048, 1408], P('expert', 'hidden')
Inputs may be any that keep to these rules, and one draw needn't show every extreme that they name: `routing`: in each aligned block of 128 tokens no expert is named more than 16 times, a bound that some block reaches. `merge_source`: 16 distinct experts, always including expert 2 and expert 64 - 3; merge_source and merge_target together hold exactly one expert of each aligned group of 2 consecutive expert numbers. `merge_target`: distinct experts, none of them a source, always including expert 0 and expert 64 - 1; see merge_source. `neuron_perm`: each row is a permutation of 0 to 1407.
All inputs are finite; a program needn't handle non-finite values.
Results may differ from a plain program's by a relative error of at most 0.019.
Values may be sent and summed in bfloat16 or wider, within the bound.
A program may use at most 128 MiB of HBM per device.

v0:
```python
import jax
import jax.numpy as jnp
from jax import lax
from jax.sharding import PartitionSpec as P


def silu_parts(values):
    sigma = jax.nn.sigmoid(values)
    return (values * sigma, sigma * (1.0 + values * (1.0 - sigma)))


def shards(
    tokens,
    cotangent,
    gate_weight,
    up_weight,
    down_weight,
    routing,
    route_weight,
    merge_source,
    merge_target,
    neuron_perm,
):
    devices_n = lax.axis_size("expert")
    my_index = lax.axis_index("expert")
    exp_local, width_local, neurons = gate_weight.shape
    experts = exp_local * devices_n
    groups = exp_local + 1
    tok_local, top_count = routing.shape
    slot_depth = max(2, tok_local * top_count * 4 // (3 * experts))
    group_rows = devices_n * slot_depth
    slot_total = groups * group_rows
    assign_n = tok_local * top_count
    expert_ids = jnp.arange(experts, dtype=jnp.int32)
    source_hit = merge_source[:, None] == expert_ids[None, :]
    is_source = jnp.any(source_hit, axis=0)
    mapped = jnp.where(
        is_source, jnp.sum(jnp.where(source_hit, merge_target[:, None], 0), axis=0), expert_ids
    )
    group_of = jnp.where(is_source, exp_local, mapped % exp_local)
    slot_base = group_of * group_rows + mapped // exp_local * slot_depth
    flat_ids = routing.reshape(-1)
    flat_weight = route_weight.reshape(-1)
    expert_hot = (flat_ids[:, None] == expert_ids[None, :]).astype(jnp.int32)
    rank_in = jnp.sum(jnp.cumsum(expert_hot, axis=0) * expert_hot, axis=1) - 1
    slot_index = jnp.sum(expert_hot * slot_base[None, :], axis=1) + rank_in
    slot_hot = jnp.arange(slot_total, dtype=jnp.int32)[:, None] == slot_index[None, :]
    token_hot = (
        jnp.arange(assign_n, dtype=jnp.int32)[:, None] // top_count
        == jnp.arange(tok_local, dtype=jnp.int32)[None, :]
    )
    placing = jnp.dot(
        slot_hot.astype(jnp.bfloat16),
        token_hot.astype(jnp.bfloat16),
        preferred_element_type=jnp.float32,
    ).astype(jnp.bfloat16)
    slot_weight = jnp.sum(jnp.where(slot_hot, flat_weight[None, :], 0.0), axis=1)
    send_tokens = jnp.dot(placing, tokens, preferred_element_type=jnp.float32).astype(jnp.bfloat16)
    placed_grads = jnp.dot(placing, cotangent, preferred_element_type=jnp.float32)
    send_grads = (placed_grads * slot_weight[:, None]).astype(jnp.bfloat16)
    slot_shape = (groups, devices_n, slot_depth, width_local)
    inputs_x, inputs_dy = (
        lax.all_to_all(
            send_tokens.reshape(slot_shape), "expert", split_axis=1, concat_axis=1, tiled=True
        ),
        lax.all_to_all(
            send_grads.reshape(slot_shape), "expert", split_axis=1, concat_axis=1, tiled=True
        ),
    )
    inputs_x = inputs_x.reshape(groups, group_rows, width_local)
    inputs_dy = inputs_dy.reshape(groups, group_rows, width_local)
    source_dev = merge_source // exp_local
    target_dev = merge_target // exp_local
    source_slot = jnp.sum(jnp.where(source_dev == my_index, merge_source % exp_local, 0))
    piece_shape = (devices_n, width_local // devices_n, neurons)
    out_gate = lax.dynamic_index_in_dim(gate_weight, source_slot, 0, keepdims=False).reshape(
        piece_shape
    )
    out_up = lax.dynamic_index_in_dim(up_weight, source_slot, 0, keepdims=False).reshape(
        piece_shape
    )
    out_down = lax.dynamic_index_in_dim(down_weight, source_slot, 0, keepdims=False).reshape(
        piece_shape
    )
    spread_gate, spread_up, spread_down = (
        lax.all_to_all(out_gate, "expert", split_axis=0, concat_axis=0, tiled=True),
        lax.all_to_all(out_up, "expert", split_axis=0, concat_axis=0, tiled=True),
        lax.all_to_all(out_down, "expert", split_axis=0, concat_axis=0, tiled=True),
    )
    device_ids = jnp.arange(devices_n, dtype=jnp.int32)
    pair_hit = target_dev[:, None] == device_ids[None, :]
    source_for = jnp.sum(jnp.where(pair_hit, source_dev[:, None], 0), axis=0)
    relay_gate = jnp.take(spread_gate, source_for, axis=0)
    relay_up = jnp.take(spread_up, source_for, axis=0)
    relay_down = jnp.take(spread_down, source_for, axis=0)
    got_gate, got_up, got_down = (
        lax.all_to_all(relay_gate, "expert", split_axis=0, concat_axis=0, tiled=True),
        lax.all_to_all(relay_up, "expert", split_axis=0, concat_axis=0, tiled=True),
        lax.all_to_all(relay_down, "expert", split_axis=0, concat_axis=0, tiled=True),
    )
    own_target = target_dev == my_index
    has_target = jnp.any(own_target)
    target_slot = jnp.sum(jnp.where(own_target, merge_target % exp_local, 0))
    order_perm = jnp.sum(jnp.where(own_target[:, None], neuron_perm, 0), axis=0)

    def merged_groups(weight, arrived):
        local_one = lax.dynamic_index_in_dim(weight, target_slot, 0, keepdims=False)
        permuted = jnp.take(arrived.reshape(width_local, neurons), order_perm, axis=1)
        blended = (0.5 * (local_one.astype(jnp.float32) + permuted.astype(jnp.float32))).astype(
            jnp.bfloat16
        )
        chosen = jnp.where(has_target, blended, local_one)
        updated = lax.dynamic_update_index_in_dim(weight, chosen, target_slot, 0)
        return jnp.concatenate([updated, chosen[None]], axis=0)

    group_gate = merged_groups(gate_weight, got_gate)
    group_up = merged_groups(up_weight, got_up)
    group_down = merged_groups(down_weight, got_down)
    gate_part = jnp.einsum("grd,gdf->grf", inputs_x, group_gate, preferred_element_type=jnp.float32)
    up_part = jnp.einsum("grd,gdf->grf", inputs_x, group_up, preferred_element_type=jnp.float32)
    gate_sum, up_sum = (
        lax.psum(gate_part.astype(jnp.bfloat16), "hidden").astype(jnp.float32),
        lax.psum(up_part.astype(jnp.bfloat16), "hidden").astype(jnp.float32),
    )
    active, slope = silu_parts(gate_sum)
    hidden_act = (active * up_sum).astype(jnp.bfloat16)
    outputs_y = jnp.einsum(
        "grf,gdf->grd", hidden_act, group_down, preferred_element_type=jnp.float32
    ).astype(jnp.bfloat16)
    returned = lax.all_to_all(
        outputs_y.reshape(slot_shape), "expert", split_axis=1, concat_axis=1, tiled=True
    )
    picked = (
        jnp.take(returned.reshape(slot_total, width_local), slot_index, axis=0).astype(jnp.float32)
        * flat_weight[:, None]
    )
    mixed = jnp.sum(picked.reshape(tok_local, top_count, width_local), axis=1).astype(jnp.bfloat16)
    grad_down = jnp.einsum(
        "grd,grf->gdf", inputs_dy, hidden_act, preferred_element_type=jnp.float32
    )
    back_part = jnp.einsum(
        "grd,gdf->grf", inputs_dy, group_down, preferred_element_type=jnp.float32
    )
    back_sum = lax.psum(back_part.astype(jnp.bfloat16), "hidden").astype(jnp.float32)
    grad_gate_act = (back_sum * up_sum * slope).astype(jnp.bfloat16)
    grad_up_act = (back_sum * active).astype(jnp.bfloat16)
    grad_gate = jnp.einsum(
        "grd,grf->gdf", inputs_x, grad_gate_act, preferred_element_type=jnp.float32
    )
    grad_up = jnp.einsum("grd,grf->gdf", inputs_x, grad_up_act, preferred_element_type=jnp.float32)

    def fold(grad):
        base = grad[:exp_local]
        extra = lax.dynamic_index_in_dim(base, target_slot, 0, keepdims=False) + grad[exp_local]
        return lax.dynamic_update_index_in_dim(base, extra, target_slot, 0).astype(jnp.bfloat16)

    return (mixed, fold(grad_gate), fold(grad_up), fold(grad_down))


def solution(mesh):
    placed = (
        P("expert", "hidden"),
        P("expert", "hidden"),
        P("expert", "hidden", None),
        P("expert", "hidden", None),
        P("expert", "hidden", None),
        P("expert", None),
        P("expert", None),
        P(),
        P(),
        P(),
    )
    return jax.shard_map(
        shards,
        mesh=mesh,
        in_specs=placed,
        out_specs=(
            P("expert", "hidden"),
            P("expert", "hidden", None),
            P("expert", "hidden", None),
            P("expert", "hidden", None),
        ),
        check_vma=False,
    )
```

profile of v0, /device:TPU:1, one launch (start us, length us, event | category | flops | bytes accessed | tf_op | source)
XLA Modules:
  0.0 576.4 jit_solution(17776151516587490401)
XLA Ops:
  19.2 9.9 %all-to-all-start.5 = ((bf16[32,16,1408]{2,1,0:T(8,128)(2,1)}), bf16[32,16,1408]{2,1,0:T(8,128)(2,1)}, u32[]{:S(2)}, u32[]{:S(2)}) async-start(bf16[32,16,1408]{2,1,0:T(8,128)(2,1)} %bitcast.77), calls=%async_computation.5 | async-start | bytes 2883584 | tf_op jit(solution)/shard_map/all_to_all | solution.py:88
  30.4 20.0 %all-to-all-done.5 = bf16[32,16,1408]{2,1,0:T(8,128)(2,1)} async-done(((bf16[32,16,1408]{2,1,0:T(8,128)(2,1)}), bf16[32,16,1408]{2,1,0:T(8,128)(2,1)}, u32[]{:S(2)}, u32[]{:S(2)}) %all-to-all-start.5) | async-done | bytes 1441824 | tf_op jit(solution)/shard_map/all_to_all | solution.py:88
  50.4 4.6 all-to-all-start.3
  58.5 17.9 %all-to-all-done.3 = bf16[32,16,1408]{2,1,0:T(8,128)(2,1)} async-done(((bf16[32,16,1408]{2,1,0:T(8,128)(2,1)}), bf16[32,16,1408]{2,1,0:T(8,128)(2,1)}, u32[]{:S(2)}, u32[]{:S(2)}) %all-to-all-start.3) | async-done | bytes 1441824 | tf_op jit(solution)/shard_map/all_to_all | solution.py:87
  84.0 17.8 %all-to-all-done.1 = bf16[32,16,1408]{2,1,0:T(8,128)(2,1)S(1)} async-done(((bf16[32,16,1408]{2,1,0:T(8,128)(2,1)}), bf16[32,16,1408]{2,1,0:T(8,128)(2,1)S(1)}, u32[]{:S(2)}, u32[]{:S(2)}) %all-to-all-start.1) | async-done | bytes 1441824 | tf_op jit(solution)/shard_map/all_to_all | solution.py:86
  109.5 20.1 %all-to-all-done = bf16[3,32,16,512]{3,2,0,1:T(8,128)(2,1)S(1)} async-done(((bf16[3,32,16,512]{3,2,0,1:T(8,128)(2,1)}), bf16[3,32,16,512]{3,2,0,1:T(8,128)(2,1)S(1)}, u32[]{:S(2)}, u32[]{:S(2)}) %all-to-all-start) | async-done | bytes 1572896 | tf_op jit(solution)/shard_map/all_to_all | solution.py:63
  129.6 4.2 all-to-all-start.8
  144.1 4.6 broadcast_select_fusion
  148.8 7.8 %all-to-all-done.8 = bf16[3,32,16,512]{3,2,0,1:T(8,128)(2,1)S(1)} async-done(((bf16[3,32,16,512]{3,2,0,1:T(8,128)(2,1)}), bf16[3,32,16,512]{3,2,0,1:T(8,128)(2,1)S(1)}, u32[]{:S(2)}, u32[]{:S(2)}) %all-to-all-start.8) | async-done | bytes 1572896 | tf_op jit(solution)/shard_map/all_to_all | solution.py:66
  156.5 26.6 %all_to_all.45 = bf16[32,16,1408]{2,1,0:T(8,128)(2,1)} all-to-all(bf16[32,16,1408]{2,1,0:T(8,128)(2,1)} %get-tuple-element.22), channel_id=1, replica_groups=mesh['expert'=32,'hidden'=4] {'expert'}, dimensions={0} | all-to-all | bytes 2883584 | tf_op jit(solution)/shard_map/all_to_all | solution.py:99
  183.1 25.1 %all_to_all.46 = bf16[32,16,1408]{2,1,0:T(8,128)(2,1)} all-to-all(bf16[32,16,1408]{2,1,0:T(8,128)(2,1)S(1)} %copy-done.13), channel_id=1, replica_groups=mesh['expert'=32,'hidden'=4] {'expert'}, dimensions={0} | all-to-all | bytes 2883584 | tf_op jit(solution)/shard_map/all_to_all | solution.py:98
  208.2 4.5 all-to-all-start.2
  220.0 5.4 gather_fusion.6
  228.7 5.0 gather_fusion.4
  236.9 5.0 gather_fusion.2
  247.1 5.4 constant_dynamic-update-slice_fusion
  252.5 7.1 %convolution_convert_fusion.2 = bf16[3,512,1408]{2,1,0:T(8,128)(2,1)} fusion(bf16[3,512,512]{2,1,0:T(8,128)(2,1)S(1)} %bitcast.78, bf16[1,512,1408]{2,1,0:T(8,128)(2,1)S(1)} %fusion.33, bf16[2,512,1408]{2,1,0:T(8,128)(2,1)} %get-tuple-element.27), kind=kOutput, calls=%fused_computation.27 | convolution fusion | flops 2218917888 | bytes 10223616 | tf_op jit(solution)/shard_map/grd,gdf->grf/dot_general | solution.py:119
  259.6 4.7 convolution_convert_fusion.1
  264.4 4.7 convolution_convert_fusion
  269.3 234.9 %all-reduce.3.cloned.1.call-done = (bf16[3,512,1408]{2,1,0:T(8,128)(2,1)}, bf16[3,512,1408]{2,1,0:T(8,128)(2,1)}, bf16[3,512,1408]{2,1,0:T(8,128)(2,1)}) async-done(((bf16[3,512,1408]{2,1,0:T(8,128)(2,1)}, bf16[3,512,1408]{2,1,0:T(8,128)(2,1)}, bf16[3,512,1408]{2,1,0:T(8,128)(2,1)}), (bf16[3,512,1408]{2,1,0:T(8,128)(2,1)}, bf16[3,512,1408]{2,1,0:T(8,128)(2,1)}, ...) | async-done | bytes 12976144 | tf_op jit(solution)/shard_map/psum | solution.py:123
  504.2 5.2 fusion
  511.3 11.6 %fusion.18 = f32[3,512,1408]{2,1,0:T(8,128)} fusion(bf16[3,512,512]{2,1,0:T(8,128)(2,1)S(1)} %bitcast.80, bf16[3,512,1408]{2,1,0:T(8,128)(2,1)S(1)} %copy-done.15, bf16[3,512,1408]{2,1,0:T(8,128)(2,1)} %get-tuple-element.10, bf16[3,512,1408]{2,1,0:T(8,128)(2,1)S(1)} %copy-done.14), kind=kOutput, calls=%fused_computation.36 | convolution fusion | flops 2242707456 | bytes 23199744 | tf_op jit(solution)/shard_map/grd,grf->gdf/dot_general | solution.py:147
  522.9 6.8 %fusion.10 = f32[3,512,1408]{2,1,0:T(8,128)} fusion(bf16[3,512,512]{2,1,0:T(8,128)(2,1)S(1)} %bitcast.81, bf16[3,512,1408]{2,1,0:T(8,128)(2,1)S(1)} %bitcast.85, bf16[3,512,1408]{2,1,0:T(8,128)(2,1)S(1)} %copy-done.14), kind=kOutput, calls=%fused_computation.28 | convolution fusion | flops 2231894016 | bytes 18874368 | tf_op jit(solution)/shard_map/grd,grf->gdf/dot_general | solution.py:150
  533.8 8.3 %all-to-all-start.7 = ((bf16[3,32,16,512]{3,2,0,1:T(8,128)(2,1)}), bf16[3,32,16,512]{3,2,0,1:T(8,128)(2,1)S(1)}, u32[]{:S(2)}, u32[]{:S(2)}) async-start(bf16[3,32,16,512]{3,2,0,1:T(8,128)(2,1)} %copy.66), calls=%async_computation.7 | async-start | bytes 3145728 | tf_op jit(solution)/shard_map/all_to_all | solution.py:130
  (150 shorter events, 90.8 us)
Async XLA Ops:
  7.2 75.0 %copy-start = (bf16[128,512]{1,0:T(8,128)(2,1)S(1)}, bf16[128,512]{1,0:T(8,128)(2,1)}, u32[]{:S(2)}) copy-start(bf16[128,512]{1,0:T(8,128)(2,1)} %param.14) | copy-start | bytes 393220
  9.9 8.1 %copy-start.3 = (bf16[2,512,1408]{2,1,0:T(8,128)(2,1)}, bf16[2,512,1408]{2,1,0:T(8,128)(2,1)S(1)}, u32[]{:S(2)}) copy-start(bf16[2,512,1408]{2,1,0:T(8,128)(2,1)S(1)} %copy.94) | copy-start | bytes 8650756
  19.2 9.9 %copy-start.5 = (bf16[2,512,1408]{2,1,0:T(8,128)(2,1)S(1)}, bf16[2,512,1408]{2,1,0:T(8,128)(2,1)}, u32[]{:S(2)}) copy-start(bf16[2,512,1408]{2,1,0:T(8,128)(2,1)} %copy.93) | copy-start | bytes 8650756
  19.2 31.2 %all-to-all-start.5 = ((bf16[32,16,1408]{2,1,0:T(8,128)(2,1)}), bf16[32,16,1408]{2,1,0:T(8,128)(2,1)}, u32[]{:S(2)}, u32[]{:S(2)}) async-start(bf16[32,16,1408]{2,1,0:T(8,128)(2,1)} %bitcast.77), calls=%async_computation.5 | async-start | bytes 2883584 | tf_op jit(solution)/shard_map/all_to_all | solution.py:88
  29.1 25.9 %copy-start.24 = (s32[128,6]{0,1:T(8,128)S(1)}, s32[128,6]{0,1:T(8,128)}, u32[]{:S(2)}) copy-start(s32[128,6]{0,1:T(8,128)} %param.19) | copy-start | bytes 9220
  30.4 26.9 %copy-start.7 = (bf16[2,512,1408]{2,1,0:T(8,128)(2,1)S(1)}, bf16[2,512,1408]{2,1,0:T(8,128)(2,1)}, u32[]{:S(2)}) copy-start(bf16[2,512,1408]{2,1,0:T(8,128)(2,1)} %copy.92) | copy-start | bytes 8650756
  50.4 26.0 %all-to-all-start.3 = ((bf16[32,16,1408]{2,1,0:T(8,128)(2,1)}), bf16[32,16,1408]{2,1,0:T(8,128)(2,1)}, u32[]{:S(2)}, u32[]{:S(2)}) async-start(bf16[32,16,1408]{2,1,0:T(8,128)(2,1)} %bitcast.76), calls=%async_computation.3 | async-start | bytes 2883584 | tf_op jit(solution)/shard_map/all_to_all | solution.py:87
  57.3 23.5 %copy-start.26 = (s32[16]{0:T(128)S(1)}, s32[16]{0:T(128)}, u32[]{:S(2)}) copy-start(s32[16]{0:T(128)} %param.22) | copy-start | bytes 196
  76.4 25.3 %all-to-all-start.1 = ((bf16[32,16,1408]{2,1,0:T(8,128)(2,1)}), bf16[32,16,1408]{2,1,0:T(8,128)(2,1)S(1)}, u32[]{:S(2)}, u32[]{:S(2)}) async-start(bf16[32,16,1408]{2,1,0:T(8,128)(2,1)} %bitcast.73), calls=%async_computation.1 | async-start | bytes 2883584 | tf_op jit(solution)/shard_map/all_to_all | solution.py:86
  82.7 24.2 %copy-start.25 = (f32[128,6]{0,1:T(8,128)S(1)}, f32[128,6]{0,1:T(8,128)}, u32[]{:S(2)}) copy-start(f32[128,6]{0,1:T(8,128)} %param.20) | copy-start | bytes 9220
  82.7 25.0 %copy-start.22 = (bf16[128,512]{1,0:T(8,128)(2,1)S(1)}, bf16[128,512]{1,0:T(8,128)(2,1)}, u32[]{:S(2)}) copy-start(bf16[128,512]{1,0:T(8,128)(2,1)} %param.15) | copy-start | bytes 393220
  102.9 26.8 %all-to-all-start = ((bf16[3,32,16,512]{3,2,0,1:T(8,128)(2,1)}), bf16[3,32,16,512]{3,2,0,1:T(8,128)(2,1)S(1)}, u32[]{:S(2)}, u32[]{:S(2)}) async-start(bf16[3,32,16,512]{3,2,0,1:T(8,128)(2,1)} %copy.58), calls=%async_computation | async-start | bytes 3145728 | tf_op jit(solution)/shard_map/all_to_all | solution.py:63
  129.6 26.9 %all-to-all-start.8 = ((bf16[3,32,16,512]{3,2,0,1:T(8,128)(2,1)}), bf16[3,32,16,512]{3,2,0,1:T(8,128)(2,1)S(1)}, u32[]{:S(2)}, u32[]{:S(2)}) async-start(bf16[3,32,16,512]{3,2,0,1:T(8,128)(2,1)} %copy.70), calls=%async_computation.8 | async-start | bytes 3145728 | tf_op jit(solution)/shard_map/all_to_all | solution.py:66
  156.5 26.6 %copy-start.13 = (bf16[32,16,1408]{2,1,0:T(8,128)(2,1)S(1)}, bf16[32,16,1408]{2,1,0:T(8,128)(2,1)}, u32[]{:S(2)}) copy-start(bf16[32,16,1408]{2,1,0:T(8,128)(2,1)} %get-tuple-element.23) | copy-start | bytes 4325380
  183.1 32.4 %copy-start.23 = (s32[16,1408]{1,0:T(8,128)S(1)}, s32[16,1408]{1,0:T(8,128)}, u32[]{:S(2)}) copy-start(s32[16,1408]{1,0:T(8,128)} %param.23) | copy-start | bytes 270340
  208.2 27.0 %all-to-all-start.2 = ((bf16[32,16,1408]{2,1,0:T(8,128)(2,1)}), bf16[32,16,1408]{2,1,0:T(8,128)(2,1)}, u32[]{:S(2)}, u32[]{:S(2)}) async-start(bf16[32,16,1408]{2,1,0:T(8,128)(2,1)} %get-tuple-element.24), calls=%async_computation.2 | async-start | bytes 2883584 | tf_op jit(solution)/shard_map/all_to_all | solution.py:97
  212.7 291.5 %all-reduce.3.cloned.1.call-start = ((), (), s32[]{:S(2)}) async-start(), calls=%async_computation.9 | async-start | bytes 25952256 | tf_op jit(solution)/shard_map/psum | solution.py:123
  252.5 11.9 %copy-start.20 = (bf16[1,512,1408]{2,1,0:T(8,128)(2,1)}, bf16[1,512,1408]{2,1,0:T(8,128)(2,1)S(1)}, u32[]{:S(2)}) copy-start(bf16[1,512,1408]{2,1,0:T(8,128)(2,1)S(1)} %get-tuple-element.12) | copy-start | bytes 4325380
  504.2 7.1 %copy-start.19 = (bf16[3,32,16,512]{3,2,1,0:T(8,128)(2,1)S(1)}, bf16[3,32,16,512]{3,2,1,0:T(8,128)(2,1)}, u32[]{:S(2)}) copy-start(bf16[3,32,16,512]{3,2,1,0:T(8,128)(2,1)} %copy.59) | copy-start | bytes 4718596
  504.2 18.7 %slice-start.7 = ((s8[4325376]{0:T(1024)(128)(4,1)}), s8[4194304]{0:T(1024)(128)(4,1)S(1)}, s32[]{:S(2)}) async-start(s8[4325376]{0:T(1024)(128)(4,1)} %bitcast.84), calls=%async_computation.17 | async-start | bytes 8388608
  509.4 20.3 %copy-start.2 = (bf16[3,512,1408]{2,1,0:T(8,128)(2,1)}, bf16[3,512,1408]{2,1,0:T(8,128)(2,1)S(1)}, u32[]{:S(2)}) copy-start(bf16[3,512,1408]{2,1,0:T(8,128)(2,1)S(1)} %fusion) | copy-start | bytes 12976132
  511.3 11.6 %slice-start.8 = ((s8[4325376]{0:T(1024)(128)(4,1)}), s8[131072]{0:T(1024)(128)(4,1)S(1)}, s32[]{:S(2)}) async-start(s8[4325376]{0:T(1024)(128)(4,1)} %bitcast.84), calls=%async_computation.18 | async-start | bytes 262144
  533.8 13.7 %slice-start.1 = ((s8[8650752]{0:T(1024)(128)(4,1)}), s8[262144]{0:T(1024)(128)(4,1)S(1)}, s32[]{:S(2)}) async-start(s8[8650752]{0:T(1024)(128)(4,1)} %bitcast.65), calls=%async_computation.11 | async-start | bytes 524288
  533.8 30.9 %all-to-all-start.7 = ((bf16[3,32,16,512]{3,2,0,1:T(8,128)(2,1)}), bf16[3,32,16,512]{3,2,0,1:T(8,128)(2,1)S(1)}, u32[]{:S(2)}, u32[]{:S(2)}) async-start(bf16[3,32,16,512]{3,2,0,1:T(8,128)(2,1)} %copy.66), calls=%async_computation.7 | async-start | bytes 3145728 | tf_op jit(solution)/shard_map/all_to_all | solution.py:130
  (21 other events, 82.2 us)
Sparse Core Ops, SparseCore 0:
  269.2 234.9 all-reduce.2
where the time goes:
time: 584 us; the launch traced here: 576 us
  waiting for transfers between devices  322 us (55%)
  local copies, waits for them, and re-layouts  67.4 us (12%)
  blocking collectives  51.7 us (9%)
  matrix products  42.4 us (7%)
  starting transfers between devices  40 us (7%)
  other arithmetic  34.6 us (6%)
  between operations  18.4 us (3%)
    psum x1, waiting for transfers between devices, shards(): lax.psum(up_part.astype(jnp.bfloat16), 'hidden').astype(jnp.float32)  235 us
    all_to_all x1, blocking collectives, shards(): lax.all_to_all(relay_down, 'expert', split_axis=0, concat_axis=0, tiled=T...  26.6 us
    all_to_all x1, blocking collectives, shards(): lax.all_to_all(relay_up, 'expert', split_axis=0, concat_axis=0, tiled=True)  25.1 us
    gather x6, local copies, waits for them, and re-layouts, merged_groups(): jnp.take(arrived.reshape(width_local, neurons), order_perm, axis=1)  21.1 us
    all_to_all x1, waiting for transfers between devices, shards(): lax.all_to_all(send_tokens.reshape(slot_shape), 'expert', split_axis=1, c...  20.1 us
    all_to_all x1, waiting for transfers between devices, shards(): lax.all_to_all(out_down, 'expert', split_axis=0, concat_axis=0, tiled=True)  20 us
    all_to_all x1, waiting for transfers between devices, shards(): lax.all_to_all(out_up, 'expert', split_axis=0, concat_axis=0, tiled=True)  17.9 us
    all_to_all x1, waiting for transfers between devices, shards(): lax.all_to_all(out_gate, 'expert', split_axis=0, concat_axis=0, tiled=True)  17.8 us
  transfers between devices with their start and end apart: 8, of which 7 were waited for; matrix products, arithmetic and copies ran while one was open for 10% of the time, Pallas kernels for 0%

commit v1 on v0

v1 whole, which is shorter than its diff:
```python
import jax
import jax.numpy as jnp
from jax import lax
from jax.sharding import PartitionSpec as P

BF = jnp.bfloat16
F32 = jnp.float32


def silu_parts(values):
    sigma = jax.nn.sigmoid(values)
    return (values * sigma, sigma * (1.0 + values * (1.0 - sigma)))


def mm(a, b):
    return jnp.dot(a, b, preferred_element_type=F32)


def mm_nt(a, b):
    return lax.dot_general(a, b, (((1,), (1,)), ((), ())), preferred_element_type=F32)


def mm_tn(a, b):
    return lax.dot_general(a, b, (((0,), (0,)), ((), ())), preferred_element_type=F32)


def exchange(values):
    return lax.all_to_all(values, "expert", split_axis=0, concat_axis=0, tiled=True)


def reduced(part):
    return lax.psum_scatter(part.astype(BF), "hidden", scatter_dimension=0, tiled=True).astype(F32)


def spread(values):
    return lax.all_gather(values, "hidden", axis=0, tiled=True)


def shards(
    tokens,
    cotangent,
    gate_weight,
    up_weight,
    down_weight,
    routing,
    route_weight,
    merge_source,
    merge_target,
    neuron_perm,
):
    devices_n = lax.axis_size("expert")
    me = lax.axis_index("expert")
    exp_local, width, neurons = gate_weight.shape
    experts = exp_local * devices_n
    half = neurons // 2
    tok_local, top_count = routing.shape
    depth = max(2, tok_local * top_count * 4 // (3 * experts))
    expert_ids = jnp.arange(experts, dtype=jnp.int32)
    device_ids = jnp.arange(devices_n, dtype=jnp.int32)

    src_hit = (merge_source[:, None] // exp_local) == device_ids[None, :]
    tgt_hit = (merge_target[:, None] // exp_local) == device_ids[None, :]
    any_hit = src_hit | tgt_hit

    def pick(hit, values):
        return jnp.sum(jnp.where(hit, values[:, None], 0), axis=0)

    source_of = pick(any_hit, merge_source)
    target_of = pick(any_hit, merge_target)
    is_src = jnp.any(src_hit, axis=0)
    own_merge = jnp.where(is_src, source_of, target_of)
    partner_dev = jnp.where(is_src, target_of, source_of) // exp_local
    plain_of = device_ids * exp_local * 2 + (exp_local - 1) - own_merge
    i_am_src = jnp.any((merge_source // exp_local) == me)
    merge_slot = jnp.sum(jnp.where(device_ids == me, own_merge, 0)) - me * exp_local
    plain_slot = 1 - merge_slot

    mine = ((merge_source // exp_local) == me) | ((merge_target // exp_local) == me)
    perm = jnp.sum(jnp.where(mine[:, None], neuron_perm, 0), axis=0)
    order = jnp.where(i_am_src, perm, jnp.arange(neurons, dtype=jnp.int32))
    hot = (order[None, :] == jnp.arange(neurons, dtype=jnp.int32)[:, None]).astype(BF)

    def one(weight, slot):
        return lax.dynamic_index_in_dim(weight, slot, 0, keepdims=False)

    stack = jnp.concatenate([one(w, merge_slot) for w in (gate_weight, up_weight, down_weight)], 0)
    ordered = mm(stack, hot).astype(BF)
    first, second = ordered[:, :half], ordered[:, half:]
    keep = jnp.where(i_am_src, second, first)
    send = jnp.where(i_am_src, first, second)

    def relay(values):
        rows, cols = values.shape
        there = exchange(values.reshape(devices_n, rows // devices_n, cols))
        there = jnp.take(there, partner_dev, axis=0)
        return exchange(there).reshape(rows, cols)

    got = relay(send)
    blended = (0.5 * (keep.astype(F32) + got.astype(F32))).astype(BF)
    merged = blended.reshape(3, width, half)

    slot_expert = jnp.stack([plain_of, target_of, source_of], axis=1).reshape(-1)
    hit = routing.T[None, :, :] == slot_expert[:, None, None]
    chosen = jnp.any(hit, axis=1)
    chosen_w = jnp.sum(jnp.where(hit, route_weight.T[None, :, :], 0.0), axis=1)
    tok_ids = jnp.arange(tok_local, dtype=jnp.int32)
    before = (tok_ids[:, None] < tok_ids[None, :]).astype(BF)
    rank = mm(chosen.astype(BF), before).astype(jnp.int32)
    rank = jnp.where(chosen, rank, -1)
    place = rank[:, None, :] == jnp.arange(depth, dtype=jnp.int32)[None, :, None]
    slot_w = jnp.sum(jnp.where(place, chosen_w[:, None, :], 0.0), axis=2)
    place = place.astype(BF).reshape(devices_n, 3, depth, tok_local)
    slot_w = slot_w.reshape(devices_n, 3, depth)
    place_p = place[:, 0].reshape(-1, tok_local)
    place_m = place[:, 1:].reshape(-1, tok_local)
    w_p = slot_w[:, 0].reshape(-1)
    w_m = slot_w[:, 1:].reshape(-1)

    def dispatch(place, weights):
        rows = place.shape[0]
        x = mm(place, tokens).astype(BF).reshape(devices_n, rows // devices_n, width)
        dy = (mm(place, cotangent) * weights[:, None]).astype(BF)
        dy = dy.reshape(devices_n, rows // devices_n, width)
        return exchange(x).reshape(rows, width), exchange(dy).reshape(rows, width)

    x_p, dy_p = dispatch(place_p, w_p)
    x_m, dy_m = dispatch(place_m, w_m)

    def partials(x, dy, gate, up, down):
        return reduced(mm(x, gate)), reduced(mm(x, up)), reduced(mm(dy, down))

    def acts(g, u, dh):
        active, slope = silu_parts(g)
        h = (active * u).astype(BF)
        dg = (dh * u * slope).astype(BF)
        du = (dh * active).astype(BF)
        return spread(h), spread(dg), spread(du)

    plain_w = [one(w, plain_slot) for w in (gate_weight, up_weight, down_weight)]
    sums_p = partials(x_p, dy_p, *plain_w)
    sums_m = partials(x_m, dy_m, merged[0], merged[1], merged[2])
    h_m, dg_m, du_m = acts(*sums_m)
    h_p, dg_p, du_p = acts(*sums_p)

    def grads(x, dy, h, dg, du):
        return [mm_tn(x, dg).astype(BF), mm_tn(x, du).astype(BF), mm_tn(dy, h).astype(BF)]

    grads_m = jnp.concatenate(grads(x_m, dy_m, h_m, dg_m, du_m), axis=0)
    far = relay(grads_m)
    y_m = mm_nt(h_m, merged[2]).astype(BF)
    back_m = exchange(y_m.reshape(devices_n, -1, width)).reshape(-1, width)
    y_p = mm_nt(h_p, plain_w[2]).astype(BF)
    back_p = exchange(y_p.reshape(devices_n, -1, width)).reshape(-1, width)
    grads_p = grads(x_p, dy_p, h_p, dg_p, du_p)

    def combine(place, weights, back):
        hi = weights.astype(BF)
        lo = (weights - hi.astype(F32)).astype(BF)
        return mm_tn(place * hi[:, None], back) + mm_tn(place * lo[:, None], back)

    mixed = (combine(place_p, w_p, back_p) + combine(place_m, w_m, back_m)).astype(BF)

    outs = []
    for index, plain in enumerate(grads_p):
        rows = slice(index * width, (index + 1) * width)
        full = jnp.concatenate([grads_m[rows], far[rows]], axis=1)
        full = jnp.where(i_am_src, jnp.zeros_like(full), full)
        first_is_merge = merge_slot == 0
        outs.append(
            jnp.stack([jnp.where(first_is_merge, full, plain), jnp.where(first_is_merge, plain, full)])
        )
    return (mixed, *outs)


def solution(mesh):
    placed = (
        P("expert", "hidden"),
        P("expert", "hidden"),
        P("expert", "hidden", None),
        P("expert", "hidden", None),
        P("expert", "hidden", None),
        P("expert", None),
        P("expert", None),
        P(),
        P(),
        P(),
    )
    return jax.shard_map(
        shards,
        mesh=mesh,
        in_specs=placed,
        out_specs=(
            P("expert", "hidden"),
            P("expert", "hidden", None),
            P("expert", "hidden", None),
            P("expert", "hidden", None),
        ),
        check_vma=False,
    )
```

time: 584 us -> 521 us (0.89)
  waiting for transfers between devices: 322 us -> 261 us
  blocking collectives: 51.7 us -> 23.7 us
  matrix products: 42.4 us -> 68.5 us
  starting transfers between devices: 40 us -> 58.2 us
  local copies, waits for them, and re-layouts: 67.4 us -> 50.1 us
  other arithmetic: 34.6 us -> 41.3 us
    psum x1 -> x0, waiting for transfers between devices: 235 us -> none  [shards(): lax.psum(up_part.astype(jnp.bfloat16), 'hidden').astype(jnp.float32)]
    all_gather x0 -> x6, waiting for transfers between devices: none -> 98.3 us  [spread(): return lax.all_gather(values, 'hidden', axis=0, tiled=True)]
    reduce_scatter x0 -> x6, waiting for transfers between devices: none -> 42 us  [reduced(): lax.psum_scatter(part.astype(BF), 'hidden', scatter_dimension=0, tiled=True)]
    all_to_all x7 -> x9, waiting for transfers between devices: 86.9 us -> 118 us  [exchange(): lax.all_to_all(values, 'expert', split_axis=0, concat_axis=0, tiled=True)]
    all_to_all x2 -> x1, blocking collectives: 51.7 us -> 23.7 us  [exchange(): lax.all_to_all(values, 'expert', split_axis=0, concat_axis=0, tiled=True)]
    dot_general x10 -> x24, matrix products: 42.4 us -> 68.5 us  [the longest x12 37.2 us: mm(): return jnp.dot(a, b, preferred_element_type=F32)]
    gather x11 -> x2, local copies, waits for them, and re-layouts: 33.6 us -> 7.66 us  [relay(): there = jnp.take(there, partner_dev, axis=0)]
    all_to_all x7 -> x9, starting transfers between devices: 39.5 us -> 57.3 us  [exchange(): lax.all_to_all(values, 'expert', split_axis=0, concat_axis=0, tiled=True)]
  transfers between devices with their start and end apart: 8 -> 21, of which waited for: 7 -> 13; matrix products, arithmetic and copies ran while one was open for 10% -> 23% of each run, Pallas kernels for 0% -> 0%
where the time goes in v1:
time: 521 us; the launch traced here: 518 us
  waiting for transfers between devices  261 us (50%)
  matrix products  68.5 us (13%)
  starting transfers between devices  58.2 us (11%)
  local copies, waits for them, and re-layouts  50.1 us (10%)
  other arithmetic  41.3 us (8%)
  blocking collectives  23.7 us (5%)
  between operations  15.4 us (3%)
    all_to_all x9, waiting for transfers between devices, exchange(): lax.all_to_all(values, 'expert', split_axis=0, concat_axis=0, tiled=True)  118 us
    all_gather x6, waiting for transfers between devices, spread(): return lax.all_gather(values, 'hidden', axis=0, tiled=True)  98.3 us
    all_to_all x9, starting transfers between devices, exchange(): lax.all_to_all(values, 'expert', split_axis=0, concat_axis=0, tiled=True)  57.3 us
    reduce_scatter x6, waiting for transfers between devices, reduced(): lax.psum_scatter(part.astype(BF), 'hidden', scatter_dimension=0, tiled=True)  42 us
    dot_general x12, matrix products, mm(): return jnp.dot(a, b, preferred_element_type=F32)  37.2 us
    dot_general x10, matrix products, mm_tn(): lax.dot_general(a, b, (((0,), (0,)), ((), ())), preferred_element_type=F32)  24.7 us
    all_to_all x1, blocking collectives, exchange(): lax.all_to_all(values, 'expert', split_axis=0, concat_axis=0, tiled=True)  23.7 us
    unnamed x60, local copies, waits for them, and re-layouts  19.8 us
  transfers between devices with their start and end apart: 21, of which 13 were waited for; matrix products, arithmetic and copies ran while one was open for 23% of the time, Pallas kernels for 0%

profile of v1, /device:TPU:1, one launch (start us, length us, event | category | flops | bytes accessed | tf_op | source)
XLA Modules:
  0.0 518.4 jit_solution(2830530205905219217)
XLA Ops:
  18.7 9.6 %all-to-all-start.9 = ((bf16[32,16,512]{2,1,0:T(8,128)(2,1)}), bf16[32,16,512]{2,1,0:T(8,128)(2,1)}, u32[]{:S(2)}, u32[]{:S(2)}) async-start(bf16[32,16,512]{2,1,0:T(8,128)(2,1)} %bitcast.32), calls=%async_computation.14 | async-start | bytes 1048576 | tf_op jit(solution)/shard_map/all_to_all | solution.py:28
  51.3 10.0 %fusion.1 = bf16[1536,1408]{0,1:T(8,128)(2,1)S(1)} fusion(bf16[512,1408]{1,0:T(8,128)(2,1)S(1)} %copy-done.4, bf16[512,1408]{1,0:T(8,128)(2,1)S(1)} %dynamic-slice_bitcast_fusion.1, bf16[512,1408]{1,0:T(8,128)(2,1)S(1)} %dynamic-slice_bitcast_fusion.2, s32[1408]{0:T(1024)S(1)} %iota_select_fusion), kind=kOutput, calls=%fused_computation.4 | convolution fusion | flops 6107250688 | bytes 8656384 | tf_op jit(solution)/shard_map/dot_general | solution.py:16
  69.8 7.0 %all-to-all-start.3 = ((bf16[32,48,704]{2,1,0:T(8,128)(2,1)}), bf16[32,48,704]{2,1,0:T(8,128)(2,1)}, u32[]{:S(2)}, u32[]{:S(2)}) async-start(bf16[32,48,704]{2,1,0:T(8,128)(2,1)} %bitcast.105), calls=%async_computation.5 | async-start | bytes 4718592 | tf_op jit(solution)/shard_map/all_to_all | solution.py:28
  80.6 27.4 %all-to-all-done.3 = bf16[32,48,704]{2,1,0:T(8,128)(2,1)} async-done(((bf16[32,48,704]{2,1,0:T(8,128)(2,1)}), bf16[32,48,704]{2,1,0:T(8,128)(2,1)}, u32[]{:S(2)}, u32[]{:S(2)}) %all-to-all-start.3) | async-done | bytes 2162720 | tf_op jit(solution)/shard_map/all_to_all | solution.py:28
  115.2 5.2 %all-to-all-start.4 = ((bf16[32,48,704]{2,1,0:T(8,128)(2,1)}), bf16[32,48,704]{2,1,0:T(8,128)(2,1)}, u32[]{:S(2)}, u32[]{:S(2)}) async-start(bf16[32,48,704]{2,1,0:T(8,128)(2,1)} %broadcast_select_fusion.1), calls=%async_computation.6 | async-start | bytes 4718592 | tf_op jit(solution)/shard_map/all_to_all | solution.py:28
  126.6 25.1 %all-to-all-done.4 = bf16[32,48,704]{2,1,0:T(8,128)(2,1)} async-done(((bf16[32,48,704]{2,1,0:T(8,128)(2,1)}), bf16[32,48,704]{2,1,0:T(8,128)(2,1)}, u32[]{:S(2)}, u32[]{:S(2)}) %all-to-all-start.4) | async-done | bytes 2162720 | tf_op jit(solution)/shard_map/all_to_all | solution.py:28
  151.7 5.1 all-to-all-start.2
  161.1 5.9 %copy.36 = f32[1536,704]{0,1:T(8,128)} copy(f32[1536,704]{1,0:T(8,128)} %bitcast_convert_fusion) | data formatting | bytes 8650752 | tf_op jit(solution)/shard_map/convert_element_type | solution.py:99
  167.0 6.5 %multiply_convert_fusion = bf16[1536,704]{0,1:T(8,128)(2,1)} fusion(f32[1536,704]{0,1:T(8,128)} %copy.36, pred[]{:T(512)} %compare_reduce_fusion.1, bf16[1536,1408]{0,1:T(8,128)(2,1)} %copy-done.2), kind=kLoop, calls=%fused_computation.10 | loop fusion | flops 5406720 | bytes 10813441 | tf_op jit(solution)/shard_map/convert_element_type | solution.py:99
  181.6 23.7 %all_to_all.50 = bf16[32,32,512]{2,1,0:T(8,128)(2,1)S(1)} all-to-all(bf16[32,32,512]{2,1,0:T(8,128)(2,1)S(1)} %bitcast.110), channel_id=1, replica_groups=mesh['expert'=32,'hidden'=4] {'expert'}, dimensions={0} | all-to-all | bytes 2097152 | tf_op jit(solution)/shard_map/all_to_all | solution.py:28
  216.0 15.0 %reduce-scatter.15.cloned.1.call-done = bf16[256,704]{0,1:T(8,128)(2,1)} async-done(((bf16[1024,704]{0,1:T(8,128)(2,1)}), bf16[256,704]{0,1:T(8,128)(2,1)}) %reduce-scatter.15.cloned.1.call-update) | async-done | bytes 360464 | tf_op jit(solution)/shard_map/reduce_scatter | solution.py:32
  230.9 26.9 %reduce-scatter.11.cloned.1.call-done = bf16[256,704]{0,1:T(8,128)(2,1)} async-done(((bf16[1024,704]{0,1:T(8,128)(2,1)}), bf16[256,704]{0,1:T(8,128)(2,1)}) %reduce-scatter.11.cloned.1.call-update) | async-done | bytes 360464 | tf_op jit(solution)/shard_map/reduce_scatter | solution.py:32
  261.8 24.0 %all-gather.7.cloned.1.call-done = bf16[512,1408]{1,0:T(8,128)(2,1)} async-done(((bf16[128,1408]{1,0:T(8,128)(2,1)}), bf16[512,1408]{1,0:T(8,128)(2,1)}) %all-gather.7.cloned.1.call-update) | async-done | bytes 1441808 | tf_op jit(solution)/shard_map/all_gather | solution.py:36
  289.0 7.9 %all-to-all-start.1 = ((bf16[32,16,512]{2,1,0:T(8,128)(2,1)}), bf16[32,16,512]{2,1,0:T(8,128)(2,1)S(1)}, u32[]{:S(2)}, u32[]{:S(2)}) async-start(bf16[32,16,512]{2,1,0:T(8,128)(2,1)} %bitcast.122), calls=%async_computation.3 | async-start | bytes 1048576 | tf_op jit(solution)/shard_map/all_to_all | solution.py:28
  296.9 18.3 %all-gather.9.cloned.1.call-done = bf16[1024,704]{0,1:T(8,128)(2,1)} async-done(((bf16[256,704]{0,1:T(8,128)(2,1)}), bf16[1024,704]{0,1:T(8,128)(2,1)}) %all-gather.9.cloned.1.call-update) | async-done | bytes 1441808 | tf_op jit(solution)/shard_map/all_gather | solution.py:36
  318.7 27.7 %all-gather.13.cloned.1.call-done = bf16[1024,704]{0,1:T(8,128)(2,1)} async-done(((bf16[256,704]{0,1:T(8,128)(2,1)}), bf16[1024,704]{0,1:T(8,128)(2,1)}) %all-gather.13.cloned.1.call-update) | async-done | bytes 1441808 | tf_op jit(solution)/shard_map/all_gather | solution.py:36
  349.8 28.2 %all-gather.11.cloned.1.call-done = bf16[1024,704]{0,1:T(8,128)(2,1)} async-done(((bf16[256,704]{0,1:T(8,128)(2,1)}), bf16[1024,704]{0,1:T(8,128)(2,1)}) %all-gather.11.cloned.1.call-update) | async-done | bytes 1441808 | tf_op jit(solution)/shard_map/all_gather | solution.py:36
  384.1 9.1 %all-to-all-start.7 = ((bf16[32,48,704]{2,1,0:T(8,128)(2,1)}), bf16[32,48,704]{2,1,0:T(8,128)(2,1)S(1)}, u32[]{:S(2)}, u32[]{:S(2)}) async-start(bf16[32,48,704]{2,1,0:T(8,128)(2,1)} %bitcast.106), calls=%async_computation.12 | async-start | bytes 4718592 | tf_op jit(solution)/shard_map/all_to_all | solution.py:28
  397.5 26.9 %all-to-all-done.7 = bf16[32,48,704]{2,1,0:T(8,128)(2,1)S(1)} async-done(((bf16[32,48,704]{2,1,0:T(8,128)(2,1)}), bf16[32,48,704]{2,1,0:T(8,128)(2,1)S(1)}, u32[]{:S(2)}, u32[]{:S(2)}) %all-to-all-start.7) | async-done | bytes 2162720 | tf_op jit(solution)/shard_map/all_to_all | solution.py:28
  437.4 9.7 %all-to-all-done.5 = bf16[32,32,512]{2,1,0:T(8,128)(2,1)S(1)} async-done(((bf16[32,32,512]{2,1,0:T(8,128)(2,1)}), bf16[32,32,512]{2,1,0:T(8,128)(2,1)S(1)}, u32[]{:S(2)}, u32[]{:S(2)}) %all-to-all-start.5) | async-done | bytes 1048608 | tf_op jit(solution)/shard_map/all_to_all | solution.py:28
  447.2 4.6 all-to-all-start.8
  458.4 24.6 %all-to-all-done.8 = bf16[32,48,704]{2,1,0:T(8,128)(2,1)} async-done(((bf16[32,48,704]{2,1,0:T(8,128)(2,1)}), bf16[32,48,704]{2,1,0:T(8,128)(2,1)}, u32[]{:S(2)}, u32[]{:S(2)}) %all-to-all-start.8) | async-done | bytes 2162720 | tf_op jit(solution)/shard_map/all_to_all | solution.py:28
  486.2 6.2 %select_bitcast_fusion.3 = (bf16[1,512,1408]{1,2,0:T(8,128)(2,1)}, bf16[1,512,1408]{1,2,0:T(8,128)(2,1)}, bf16[1,512,1408]{1,2,0:T(8,128)(2,1)S(1)}, bf16[1,512,1408]{1,2,0:T(8,128)(2,1)S(1)}) fusion(bf16[512,1408]{0,1:T(8,128)(2,1)} %convolution_convert_fusion.1, pred[]{:T(512)S(6)} %eq.125, bf16[512,704]{0,1:T(8,128)(2,1)S(1)} %copy.51, ...), kind=kOutput, calls=%fused_computation.43 | convolution fusion | flops 749010944 | bytes 12058626 | tf_op jit(solution)/shard_map/dot_general | solution.py:24
  506.9 4.6 copy.46
  (163 shorter events, 143.7 us)
Async XLA Ops:
  7.2 27.4 %copy-start = (bf16[2,512,1408]{2,1,0:T(8,128)(2,1)S(1)}, bf16[2,512,1408]{2,1,0:T(8,128)(2,1)}, u32[]{:S(2)}) copy-start(bf16[2,512,1408]{2,1,0:T(8,128)(2,1)} %param.16) | copy-start | bytes 8650756
  18.7 21.3 %all-to-all-start.9 = ((bf16[32,16,512]{2,1,0:T(8,128)(2,1)}), bf16[32,16,512]{2,1,0:T(8,128)(2,1)}, u32[]{:S(2)}, u32[]{:S(2)}) async-start(bf16[32,16,512]{2,1,0:T(8,128)(2,1)} %bitcast.32), calls=%async_computation.14 | async-start | bytes 1048576 | tf_op jit(solution)/shard_map/all_to_all | solution.py:28
  40.0 29.9 %all-to-all-start = ((bf16[32,16,512]{2,1,0:T(8,128)(2,1)}), bf16[32,16,512]{2,1,0:T(8,128)(2,1)}, u32[]{:S(2)}, u32[]{:S(2)}) async-start(bf16[32,16,512]{2,1,0:T(8,128)(2,1)} %bitcast.8), calls=%async_computation | async-start | bytes 1048576 | tf_op jit(solution)/shard_map/all_to_all | solution.py:28
  44.4 168.8 %reduce-scatter.17.cloned.1.call-start = ((), (), s32[]{:S(2)}) async-start(), calls=%async_computation.25 | async-start | bytes 1802240 | tf_op jit(solution)/shard_map/reduce_scatter | solution.py:32
  69.8 38.3 %all-to-all-start.3 = ((bf16[32,48,704]{2,1,0:T(8,128)(2,1)}), bf16[32,48,704]{2,1,0:T(8,128)(2,1)}, u32[]{:S(2)}, u32[]{:S(2)}) async-start(bf16[32,48,704]{2,1,0:T(8,128)(2,1)} %bitcast.105), calls=%async_computation.5 | async-start | bytes 4718592 | tf_op jit(solution)/shard_map/all_to_all | solution.py:28
  76.8 136.4 %reduce-scatter.7.cloned.1.call-start = ((), (), s32[]{:S(2)}) async-start(), calls=%async_computation.16 | async-start | bytes 1802240 | tf_op jit(solution)/shard_map/reduce_scatter | solution.py:32
  80.6 31.2 %copy-start.22 = (pred[32]{0:T(512)(128)(4,1)}, pred[32]{0:T(512)(128)(4,1)S(1)}, u32[]{:S(2)}) copy-start(pred[32]{0:T(512)(128)(4,1)S(1)} %get-tuple-element.23) | copy-start | bytes 100
  80.6 31.2 %copy-start.21 = (s32[1024]{0:T(1024)}, s32[1024]{0:T(1024)S(1)}, u32[]{:S(2)}) copy-start(s32[1024]{0:T(1024)S(1)} %pad_clamp_fusion) | copy-start | bytes 12292
  115.2 36.6 %all-to-all-start.4 = ((bf16[32,48,704]{2,1,0:T(8,128)(2,1)}), bf16[32,48,704]{2,1,0:T(8,128)(2,1)}, u32[]{:S(2)}, u32[]{:S(2)}) async-start(bf16[32,48,704]{2,1,0:T(8,128)(2,1)} %broadcast_select_fusion.1), calls=%async_computation.6 | async-start | bytes 4718592 | tf_op jit(solution)/shard_map/all_to_all | solution.py:28
  120.4 92.8 %reduce-scatter.9.cloned.1.call-start = ((), (), s32[]{:S(2)}) async-start(), calls=%async_computation.17 | async-start | bytes 1802240 | tf_op jit(solution)/shard_map/reduce_scatter | solution.py:32
  151.7 22.2 %all-to-all-start.2 = ((bf16[32,32,512]{2,1,0:T(8,128)(2,1)}), bf16[32,32,512]{2,1,0:T(8,128)(2,1)}, u32[]{:S(2)}, u32[]{:S(2)}) async-start(bf16[32,32,512]{2,1,0:T(8,128)(2,1)} %bitcast.109), calls=%async_computation.4 | async-start | bytes 2097152 | tf_op jit(solution)/shard_map/all_to_all | solution.py:28
  156.8 59.1 %reduce-scatter.13.cloned.1.call-start = ((), (), s32[]{:S(2)}) async-start(), calls=%async_computation.20 | async-start | bytes 1802240 | tf_op jit(solution)/shard_map/reduce_scatter | solution.py:32
  177.4 53.5 %reduce-scatter.15.cloned.1.call-start = ((), (), s32[]{:S(2)}) async-start(), calls=%async_computation.22 | async-start | bytes 1802240 | tf_op jit(solution)/shard_map/reduce_scatter | solution.py:32
  209.5 48.3 %reduce-scatter.11.cloned.1.call-start = ((), (), s32[]{:S(2)}) async-start(), calls=%async_computation.19 | async-start | bytes 1802240 | tf_op jit(solution)/shard_map/reduce_scatter | solution.py:32
  213.1 72.7 %all-gather.7.cloned.1.call-start = ((), (), s32[]{:S(2)}) async-start(), calls=%async_computation.18 | async-start | bytes 1802240 | tf_op jit(solution)/shard_map/all_gather | solution.py:36
  215.9 99.3 %all-gather.9.cloned.1.call-start = ((), (), s32[]{:S(2)}) async-start(), calls=%async_computation.21 | async-start | bytes 1802240 | tf_op jit(solution)/shard_map/all_gather | solution.py:36
  260.5 85.9 %all-gather.13.cloned.1.call-start = ((), (), s32[]{:S(2)}) async-start(), calls=%async_computation.24 | async-start | bytes 1802240 | tf_op jit(solution)/shard_map/all_gather | solution.py:36
  261.2 116.8 %all-gather.11.cloned.1.call-start = ((), (), s32[]{:S(2)}) async-start(), calls=%async_computation.23 | async-start | bytes 1802240 | tf_op jit(solution)/shard_map/all_gather | solution.py:36
  289.0 95.1 %all-to-all-start.1 = ((bf16[32,16,512]{2,1,0:T(8,128)(2,1)}), bf16[32,16,512]{2,1,0:T(8,128)(2,1)S(1)}, u32[]{:S(2)}, u32[]{:S(2)}) async-start(bf16[32,16,512]{2,1,0:T(8,128)(2,1)} %bitcast.122), calls=%async_computation.3 | async-start | bytes 1048576 | tf_op jit(solution)/shard_map/all_to_all | solution.py:28
  384.1 40.2 %all-to-all-start.7 = ((bf16[32,48,704]{2,1,0:T(8,128)(2,1)}), bf16[32,48,704]{2,1,0:T(8,128)(2,1)S(1)}, u32[]{:S(2)}, u32[]{:S(2)}) async-start(bf16[32,48,704]{2,1,0:T(8,128)(2,1)} %bitcast.106), calls=%async_computation.12 | async-start | bytes 4718592 | tf_op jit(solution)/shard_map/all_to_all | solution.py:28
  393.2 59.8 %all-gather.17.cloned.1.call-start = ((), (), s32[]{:S(2)}) async-start(), calls=%async_computation.27 | async-start | bytes 1802240 | tf_op jit(solution)/shard_map/all_gather | solution.py:36
  425.8 21.4 %all-to-all-start.5 = ((bf16[32,32,512]{2,1,0:T(8,128)(2,1)}), bf16[32,32,512]{2,1,0:T(8,128)(2,1)S(1)}, u32[]{:S(2)}, u32[]{:S(2)}) async-start(bf16[32,32,512]{2,1,0:T(8,128)(2,1)} %bitcast.116), calls=%async_computation.9 | async-start | bytes 2097152 | tf_op jit(solution)/shard_map/all_to_all | solution.py:28
  447.2 35.8 %all-to-all-start.8 = ((bf16[32,48,704]{2,1,0:T(8,128)(2,1)}), bf16[32,48,704]{2,1,0:T(8,128)(2,1)}, u32[]{:S(2)}, u32[]{:S(2)}) async-start(bf16[32,48,704]{2,1,0:T(8,128)(2,1)} %broadcast_select_fusion), calls=%async_computation.13 | async-start | bytes 4718592 | tf_op jit(solution)/shard_map/all_to_all | solution.py:28
  451.8 34.4 %all-gather.15.cloned.1.call-start = ((), (), s32[]{:S(2)}) async-start(), calls=%async_computation.26 | async-start | bytes 1802240 | tf_op jit(solution)/shard_map/all_gather | solution.py:36
  (24 other events, 106.9 us)
Sparse Core Ops, SparseCore 0:
  47.7 24.4 reduce-scatter.16
  80.7 24.6 reduce-scatter.6
  124.4 24.7 reduce-scatter.8
  177.5 24.3 reduce-scatter.12
  209.7 21.2 reduce-scatter.14
  233.2 24.6 reduce-scatter.10
  259.5 26.2 all-gather.6
  287.5 27.6 all-gather.8
  316.9 29.4 all-gather.12
  348.5 29.4 all-gather.10
  395.7 25.8 all-gather.16
  453.9 25.8 all-gather.14

commit v2 on v1

--- a/solution.py
+++ b/solution.py
@@ -1,10 +1,13 @@
 import jax
 import jax.numpy as jnp
 from jax import lax
+from jax.experimental import pallas as pl
+from jax.experimental.pallas import tpu as pltpu
 from jax.sharding import PartitionSpec as P
 
 BF = jnp.bfloat16
 F32 = jnp.float32
+MESH = pl.DeviceIdType.MESH
 
 
 def silu_parts(values):
@@ -28,12 +31,128 @@
     return lax.all_to_all(values, "expert", split_axis=0, concat_axis=0, tiled=True)
 
 
-def reduced(part):
-    return lax.psum_scatter(part.astype(BF), "hidden", scatter_dimension=0, tiled=True).astype(F32)
-
-
-def spread(values):
-    return lax.all_gather(values, "hidden", axis=0, tiled=True)
+def add_to(ref, other):
+    ref[...] = (ref[...].astype(F32) + other[...].astype(F32)).astype(BF)
+
+
+def hidden_kernel(
+    x_ref, dy_ref, gate_ref, up_ref, down_ref, cover_ref, full, part, in_a, in_b, in_l, in_r, own, sends, recvs
+):
+    n = 4
+    me = lax.axis_index("hidden")
+    right, left, across = lax.rem(me + 1, n), lax.rem(me + 3, n), lax.rem(me + 2, n)
+    chunk = part.shape[2]
+    half = chunk // 2
+
+    barrier = pltpu.get_barrier_semaphore()
+    for peer in (left, right):
+        pl.semaphore_signal(barrier, inc=1, device_id={"hidden": peer}, device_id_type=MESH)
+    pl.semaphore_wait(barrier, 2)
+
+    def send(src, dst, kind, q, peer):
+        copy = pltpu.make_async_remote_copy(
+            src_ref=src,
+            dst_ref=dst,
+            send_sem=sends.at[kind, q],
+            recv_sem=recvs.at[kind, q],
+            device_id={"hidden": peer},
+            device_id_type=MESH,
+        )
+        copy.start()
+        return copy
+
+    pairs = ((x_ref, gate_ref), (x_ref, up_ref), (dy_ref, down_ref))
+
+    def product(q, index):
+        rows, weight = pairs[q]
+        return mm(rows[pl.ds(pl.multiple_of(index * chunk, chunk), chunk), :], weight[...])
+
+    first, second = pl.ds(0, half), pl.ds(half, half)
+    step1, step2, step3, step4 = [], [], [], []
+    for q in range(3):
+        part[q, across] = product(q, across).astype(BF)
+        step1.append(
+            (
+                send(part.at[q, across, first], in_a.at[q], 0, q, right),
+                send(part.at[q, across, second], in_b.at[q], 1, q, left),
+            )
+        )
+    for q in range(3):
+        part[q, right] = product(q, right).astype(BF)
+        part[q, left] = product(q, left).astype(BF)
+        step1[q][0].wait_recv()
+        add_to(part.at[q, right, first], in_a.at[q])
+        a = send(part.at[q, right], in_l.at[q], 2, q, right)
+        step1[q][1].wait_recv()
+        add_to(part.at[q, left, second], in_b.at[q])
+        step2.append((a, send(part.at[q, left], in_r.at[q], 3, q, left)))
+    for q in range(3):
+        own[q] = product(q, me)
+
+    def total(q):
+        step2[q][0].wait_recv()
+        step2[q][1].wait_recv()
+        return own[q].astype(BF).astype(F32) + in_l[q].astype(F32) + in_r[q].astype(F32)
+
+    cover = cover_ref[0:1, :]
+
+    def publish(q, value):
+        full[q, me] = (value * cover).astype(BF)
+        step3.append(
+            (
+                send(full.at[q, me], full.at[q, me], 4, q, right),
+                send(full.at[q, me], full.at[q, me], 5, q, left),
+            )
+        )
+
+    g = total(0)
+    u = total(1)
+    active, slope = silu_parts(g)
+    publish(0, active * u)
+    own[0] = active
+    own[1] = u * slope
+    dh = total(2)
+    publish(1, dh * own[1])
+    publish(2, dh * own[0])
+    for q in range(3):
+        step3[q][0].wait_recv()
+        a = send(full.at[q, left, first], full.at[q, left, first], 6, q, right)
+        step3[q][1].wait_recv()
+        step4.append((a, send(full.at[q, right, second], full.at[q, right, second], 7, q, left)))
+    for q in range(3):
+        for copy in step4[q]:
+            copy.wait_recv()
+    for step in (step1, step2, step3, step4):
+        for copies in step:
+            for copy in copies:
+                copy.wait_send()
+
+
+def hidden_block(x, dy, gate, up, down, cover, ident):
+    rows, cols = x.shape[0], gate.shape[1]
+    chunk = rows // 4
+    vmem = pl.BlockSpec(memory_space=pltpu.VMEM)
+    full = pl.pallas_call(
+        hidden_kernel,
+        out_shape=jax.ShapeDtypeStruct((3, 4, chunk, cols), BF),
+        in_specs=[vmem] * 6,
+        out_specs=vmem,
+        scratch_shapes=[
+            pltpu.VMEM((3, 4, chunk, cols), BF),
+            pltpu.VMEM((3, chunk // 2, cols), BF),
+            pltpu.VMEM((3, chunk // 2, cols), BF),
+            pltpu.VMEM((3, chunk, cols), BF),
+            pltpu.VMEM((3, chunk, cols), BF),
+            pltpu.VMEM((3, chunk, cols), F32),
+            pltpu.SemaphoreType.DMA((8, 3)),
+            pltpu.SemaphoreType.DMA((8, 3)),
+        ],
+        compiler_params=pltpu.CompilerParams(
+            collective_id=ident, has_side_effects=True, vmem_limit_bytes=56 * 1024 * 1024
+        ),
+        cost_estimate=pl.CostEstimate(flops=60_000_000_000, bytes_accessed=200_000_000, transcendentals=0),
+    )(x, dy, gate, up, down, cover)
+    return [full[q].reshape(rows, cols) for q in range(3)]
 
 
 def shards(
@@ -52,7 +171,8 @@
     me = lax.axis_index("expert")
     exp_local, width, neurons = gate_weight.shape
     experts = exp_local * devices_n
-    half = neurons // 2
+    half = -(-neurons // 256) * 128
+    tail = neurons - half
     tok_local, top_count = routing.shape
     depth = max(2, tok_local * top_count * 4 // (3 * experts))
     expert_ids = jnp.arange(experts, dtype=jnp.int32)
@@ -85,7 +205,7 @@
 
     stack = jnp.concatenate([one(w, merge_slot) for w in (gate_weight, up_weight, down_weight)], 0)
     ordered = mm(stack, hot).astype(BF)
-    first, second = ordered[:, :half], ordered[:, half:]
+    first, second = ordered[:, :half], ordered[:, tail:]
     keep = jnp.where(i_am_src, second, first)
     send = jnp.where(i_am_src, first, second)
 
@@ -126,27 +246,19 @@
     x_p, dy_p = dispatch(place_p, w_p)
     x_m, dy_m = dispatch(place_m, w_m)
 
-    def partials(x, dy, gate, up, down):
-        return reduced(mm(x, gate)), reduced(mm(x, up)), reduced(mm(dy, down))
-
-    def acts(g, u, dh):
-        active, slope = silu_parts(g)
-        h = (active * u).astype(BF)
-        dg = (dh * u * slope).astype(BF)
-        du = (dh * active).astype(BF)
-        return spread(h), spread(dg), spread(du)
-
     plain_w = [one(w, plain_slot) for w in (gate_weight, up_weight, down_weight)]
-    sums_p = partials(x_p, dy_p, *plain_w)
-    sums_m = partials(x_m, dy_m, merged[0], merged[1], merged[2])
-    h_m, dg_m, du_m = acts(*sums_m)
-    h_p, dg_p, du_p = acts(*sums_p)
+    overlap = jnp.arange(half, dtype=jnp.int32) < (2 * half - neurons)
+    cover_m = jnp.where(i_am_src & overlap, 0.0, 1.0).astype(F32)
+    cover_m = jnp.broadcast_to(cover_m[None, :], (8, half))
+    cover_p = jnp.ones((8, neurons), F32)
+    h_p, dg_p, du_p = hidden_block(x_p, dy_p, *plain_w, cover_p, 0)
+    h_m, dg_m, du_m = hidden_block(x_m, dy_m, merged[0], merged[1], merged[2], cover_m, 1)
 
     def grads(x, dy, h, dg, du):
         return [mm_tn(x, dg).astype(BF), mm_tn(x, du).astype(BF), mm_tn(dy, h).astype(BF)]
 
     grads_m = jnp.concatenate(grads(x_m, dy_m, h_m, dg_m, du_m), axis=0)
-    far = relay(grads_m)
+    far = relay(grads_m[:, half - tail :])
     y_m = mm_nt(h_m, merged[2]).astype(BF)
     back_m = exchange(y_m.reshape(devices_n, -1, width)).reshape(-1, width)
     y_p = mm_nt(h_p, plain_w[2]).astype(BF)

time: 521 us -> 432 us (0.83)
  Pallas kernels: 0 us -> 163 us
  waiting for transfers between devices: 261 us -> 108 us
  matrix products: 68.5 us -> 41.1 us
  blocking collectives: 23.7 us -> 0 us
  local copies, waits for them, and re-layouts: 50.1 us -> 27.1 us
  between operations: 15.4 us -> 1.78 us
  other arithmetic: 41.3 us -> 31.1 us
    pallas_call x0 -> x2, Pallas kernels: none -> 163 us  [hidden_block(): pl.pallas_call(hidden_kernel, out_shape=jax.ShapeDtypeStruct((3, 4, chunk...]
    all_gather x6 -> x0, waiting for transfers between devices: 98.3 us -> none  [spread(): return lax.all_gather(values, 'hidden', axis=0, tiled=True)]
    reduce_scatter x6 -> x0, waiting for transfers between devices: 42 us -> none  [reduced(): lax.psum_scatter(part.astype(BF), 'hidden', scatter_dimension=0, tiled=True)]
    all_to_all x1 -> x0, blocking collectives: 23.7 us -> none  [exchange(): lax.all_to_all(values, 'expert', split_axis=0, concat_axis=0, tiled=True)]
    dot_general x12 -> x6, matrix products: 37.2 us -> 17.7 us  [mm(): return jnp.dot(a, b, preferred_element_type=F32)]
    unnamed x60 -> x58, local copies, waits for them, and re-layouts: 19.8 us -> 7.52 us
    all_to_all x9 -> x10, waiting for transfers between devices: 118 us -> 108 us  [exchange(): lax.all_to_all(values, 'expert', split_axis=0, concat_axis=0, tiled=True)]
    slice x0 -> x3, local copies, waits for them, and re-layouts: none -> 8.6 us  [the longest x2 7.14 us: hidden_block(): return [full[q].reshape(rows, cols) for q in range(3)]]
  transfers between devices with their start and end apart: 21 -> 10, of which waited for: 13 -> 7; matrix products, arithmetic and copies ran while one was open for 23% -> 18% of each run, Pallas kernels for 0% -> 38%
where the time goes in v2:
time: 432 us; the launch traced here: 430 us
  Pallas kernels  163 us (38%)
  waiting for transfers between devices  108 us (25%)
  starting transfers between devices  58.8 us (14%)
  matrix products  41.1 us (10%)
  other arithmetic  31.1 us (7%)
  local copies, waits for them, and re-layouts  27.1 us (6%)
    pallas_call x2, Pallas kernels, hidden_block(): pl.pallas_call(hidden_kernel, out_shape=jax.ShapeDtypeStruct((3, 4, chunk...  163 us
    all_to_all x10, waiting for transfers between devices, exchange(): lax.all_to_all(values, 'expert', split_axis=0, concat_axis=0, tiled=True)  108 us
    all_to_all x10, starting transfers between devices, exchange(): lax.all_to_all(values, 'expert', split_axis=0, concat_axis=0, tiled=True)  58.8 us
    dot_general x6, matrix products, mm(): return jnp.dot(a, b, preferred_element_type=F32)  17.7 us
    dot_general x10, matrix products, mm_tn(): lax.dot_general(a, b, (((0,), (0,)), ((), ())), preferred_element_type=F32)  16.4 us
  transfers between devices with their start and end apart: 10, of which 7 were waited for; matrix products, arithmetic and copies ran while one was open for 18% of the time, Pallas kernels for 38%

profile of v2, /device:TPU:1, one launch (start us, length us, event | category | flops | bytes accessed | tf_op | source)
XLA Modules:
  0.0 429.9 jit_solution(15962833029081320340)
XLA Ops:
  5.6 9.6 %all-to-all-start = ((bf16[32,16,512]{2,1,0:T(8,128)(2,1)}), bf16[32,16,512]{2,1,0:T(8,128)(2,1)}, u32[]{:S(2)}, u32[]{:S(2)}) async-start(bf16[32,16,512]{2,1,0:T(8,128)(2,1)} %bitcast.8), calls=%async_computation | async-start | bytes 1048576 | tf_op jit(solution)/shard_map/all_to_all | solution.py:31
  24.1 12.6 %fusion.1 = bf16[1536,1408]{1,0:T(8,128)(2,1)} fusion(bf16[512,1408]{1,0:T(8,128)(2,1)S(1)} %get-tuple-element.26, bf16[512,1408]{1,0:T(8,128)(2,1)S(1)} %get-tuple-element.28, bf16[512,1408]{1,0:T(8,128)(2,1)S(1)} %get-tuple-element.30, s32[1408]{0:T(1024)S(1)} %iota_select_fusion), kind=kOutput, calls=%fused_computation.4 | convolution fusion | flops 6107250688 | bytes 8656384 | tf_op jit(solution)/shard_map/dot_general | solution.py:19
  38.9 7.4 %all-to-all-start.1 = ((bf16[32,16,512]{2,1,0:T(8,128)(2,1)}), bf16[32,16,512]{2,1,0:T(8,128)(2,1)S(1)}, u32[]{:S(2)}, u32[]{:S(2)}) async-start(bf16[32,16,512]{2,1,0:T(8,128)(2,1)} %bitcast.10), calls=%async_computation.1 | async-start | bytes 1048576 | tf_op jit(solution)/shard_map/all_to_all | solution.py:31
  46.2 4.7 %broadcast_select_fusion.1 = bf16[1536,768]{1,0:T(8,128)(2,1)} fusion(pred[]{:T(512)} %compare_reduce_fusion.1, bf16[1536,1408]{1,0:T(8,128)(2,1)} %fusion.1), kind=kLoop, calls=%fused_computation.21 | loop fusion | flops 1179648 | bytes 7077889 | tf_op jit(solution)/shard_map/jit(_where)/select_n | solution.py:210
  50.9 6.9 %all-to-all-done.1 = bf16[32,16,512]{2,1,0:T(8,128)(2,1)S(1)} async-done(((bf16[32,16,512]{2,1,0:T(8,128)(2,1)}), bf16[32,16,512]{2,1,0:T(8,128)(2,1)S(1)}, u32[]{:S(2)}, u32[]{:S(2)}) %all-to-all-start.1) | async-done | bytes 524320 | tf_op jit(solution)/shard_map/all_to_all | solution.py:31
  58.7 3.8 all-to-all-start.5
  64.7 28.8 %all-to-all-done.5 = bf16[32,48,768]{2,1,0:T(8,128)(2,1)S(1)} async-done(((bf16[32,48,768]{2,1,0:T(8,128)(2,1)}), bf16[32,48,768]{2,1,0:T(8,128)(2,1)S(1)}, u32[]{:S(2)}, u32[]{:S(2)}) %all-to-all-start.5) | async-done | bytes 2359328 | tf_op jit(solution)/shard_map/all_to_all | solution.py:31
  93.5 5.1 %all-to-all-start.3 = ((bf16[32,32,512]{2,1,0:T(8,128)(2,1)}), bf16[32,32,512]{2,1,0:T(8,128)(2,1)}, u32[]{:S(2)}, u32[]{:S(2)}) async-start(bf16[32,32,512]{2,1,0:T(8,128)(2,1)} %bitcast.21), calls=%async_computation.3 | async-start | bytes 2097152 | tf_op jit(solution)/shard_map/all_to_all | solution.py:31
  106.1 9.5 %all-to-all-done.3 = bf16[32,32,512]{2,1,0:T(8,128)(2,1)} async-done(((bf16[32,32,512]{2,1,0:T(8,128)(2,1)}), bf16[32,32,512]{2,1,0:T(8,128)(2,1)}, u32[]{:S(2)}, u32[]{:S(2)}) %all-to-all-start.3) | async-done | bytes 1048608 | tf_op jit(solution)/shard_map/all_to_all | solution.py:31
  115.6 4.0 all-to-all-start.6
  120.2 78.5 %shard_map.129 = bf16[3,4,128,1408]{3,2,1,0:T(8,128)(2,1)} custom-call(bf16[512,512]{1,0:T(8,128)(2,1)} %bitcast.9.x_ref, bf16[512,512]{1,0:T(8,128)(2,1)} %bitcast.129, bf16[512,1408]{1,0:T(8,128)(2,1)} %get-tuple-element.29.gate_ref, bf16[512,1408]{1,0:T(8,128)(2,1)} %get-tuple-element.27.up_ref, bf16[512,1408]{1,0:T(8,128)(2,1)} %get-tuple-element.25.down_ref, ...), custom_call_target="tpu_custom_call" | custom-call | flops 60000002048 | bytes 200000000 | tf_op jit(solution)/shard_map/pallas_call | solution.py:135
  198.7 4.4 %fusion.26 = (bf16[1,4,128,1408]{3,2,1,0:T(8,128)(2,1)}, bf16[1,4,128,1408]{3,2,1,0:T(8,128)(2,1)}, bf16[1,4,128,1408]{3,2,1,0:T(8,128)(2,1)}) fusion(bf16[3,4,128,1408]{3,2,1,0:T(8,128)(2,1)} %shard_map.129), kind=kLoop, calls=%fused_computation.115 | loop fusion | bytes 8650752 | tf_op jit(solution)/shard_map/slice | solution.py:155
  203.1 8.1 %all-to-all-start.4 = ((bf16[32,32,512]{2,1,0:T(8,128)(2,1)}), bf16[32,32,512]{2,1,0:T(8,128)(2,1)S(1)}, u32[]{:S(2)}, u32[]{:S(2)}) async-start(bf16[32,32,512]{2,1,0:T(8,128)(2,1)} %bitcast.23), calls=%async_computation.4 | async-start | bytes 2097152 | tf_op jit(solution)/shard_map/all_to_all | solution.py:31
  214.8 4.7 %fusion.3 = bf16[1536,768]{1,0:T(8,128)(2,1)S(1)} fusion(bf16[32,48,768]{2,1,0:T(8,128)(2,1)} %copy-done.2, pred[]{:T(512)} %compare_reduce_fusion.1, bf16[1536,1408]{1,0:T(8,128)(2,1)} %fusion.1), kind=kLoop, calls=%fused_computation.7 | loop fusion | flops 7077888 | bytes 9437185 | tf_op jit(solution)/shard_map/convert_element_type | solution.py:219
  221.0 7.1 %all-to-all-done.4 = bf16[32,32,512]{2,1,0:T(8,128)(2,1)S(1)} async-done(((bf16[32,32,512]{2,1,0:T(8,128)(2,1)}), bf16[32,32,512]{2,1,0:T(8,128)(2,1)S(1)}, u32[]{:S(2)}, u32[]{:S(2)}) %all-to-all-start.4) | async-done | bytes 1048608 | tf_op jit(solution)/shard_map/all_to_all | solution.py:31
  229.1 3.9 all-to-all-start.2
  233.6 84.1 %shard_map.130 = bf16[3,4,256,768]{3,2,1,0:T(8,128)(2,1)} custom-call(bf16[1024,512]{1,0:T(8,128)(2,1)} %bitcast.22.x_ref, bf16[1024,512]{1,0:T(8,128)(2,1)} %bitcast.121, bf16[512,768]{1,0:T(8,128)(2,1)} %get-tuple-element.33.gate_ref, bf16[512,768]{1,0:T(8,128)(2,1)} %get-tuple-element.32.up_ref, bf16[512,768]{1,0:T(8,128)(2,1)} %get-tuple-element.31.down_ref, ...), custom_call_target="tpu_custom_call" | custom-call | flops 60000002048 | bytes 200000000 | tf_op jit(solution)/shard_map/pallas_call | solution.py:135
  330.0 8.4 %all-to-all-start.8 = ((bf16[32,48,640]{2,1,0:T(8,128)(2,1)}), bf16[32,48,640]{2,1,0:T(8,128)(2,1)}, u32[]{:S(2)}, u32[]{:S(2)}) async-start(bf16[32,48,640]{2,1,0:T(8,128)(2,1)} %bitcast.107), calls=%async_computation.8 | async-start | bytes 3932160 | tf_op jit(solution)/shard_map/all_to_all | solution.py:31
  341.7 23.6 %all-to-all-done.8 = bf16[32,48,640]{2,1,0:T(8,128)(2,1)} async-done(((bf16[32,48,640]{2,1,0:T(8,128)(2,1)}), bf16[32,48,640]{2,1,0:T(8,128)(2,1)}, u32[]{:S(2)}, u32[]{:S(2)}) %all-to-all-start.8) | async-done | bytes 1966112 | tf_op jit(solution)/shard_map/all_to_all | solution.py:31
  365.3 4.4 %all-to-all-start.7 = ((bf16[32,32,512]{2,1,0:T(8,128)(2,1)}), bf16[32,32,512]{2,1,0:T(8,128)(2,1)S(1)}, u32[]{:S(2)}, u32[]{:S(2)}) async-start(bf16[32,32,512]{2,1,0:T(8,128)(2,1)} %bitcast.123), calls=%async_computation.7 | async-start | bytes 2097152 | tf_op jit(solution)/shard_map/all_to_all | solution.py:31
  373.7 13.0 %all-to-all-done.7 = bf16[32,32,512]{2,1,0:T(8,128)(2,1)S(1)} async-done(((bf16[32,32,512]{2,1,0:T(8,128)(2,1)}), bf16[32,32,512]{2,1,0:T(8,128)(2,1)S(1)}, u32[]{:S(2)}, u32[]{:S(2)}) %all-to-all-start.7) | async-done | bytes 1048608 | tf_op jit(solution)/shard_map/all_to_all | solution.py:31
  386.7 4.1 all-to-all-start.9
  393.3 3.7 convolution_convert_fusion.1
  398.9 18.6 %all-to-all-done.9 = bf16[32,48,640]{2,1,0:T(8,128)(2,1)S(1)} async-done(((bf16[32,48,640]{2,1,0:T(8,128)(2,1)}), bf16[32,48,640]{2,1,0:T(8,128)(2,1)S(1)}, u32[]{:S(2)}, u32[]{:S(2)}) %all-to-all-start.9) | async-done | bytes 1966112 | tf_op jit(solution)/shard_map/all_to_all | solution.py:31
  (122 shorter events, 69.3 us)
Async XLA Ops:
  0.6 3.9 copy-start
  0.6 16.0 %copy-start.26 = (s32[128,6]{0,1:T(8,128)S(1)}, s32[128,6]{0,1:T(8,128)}, u32[]{:S(2)}) copy-start(s32[128,6]{0,1:T(8,128)} %param.15) | copy-start | bytes 9220
  0.7 16.0 %copy-start.27 = (f32[128,6]{0,1:T(8,128)S(1)}, f32[128,6]{0,1:T(8,128)}, u32[]{:S(2)}) copy-start(f32[128,6]{0,1:T(8,128)} %param.16) | copy-start | bytes 9220
  0.7 16.7 %copy-start.5 = (bf16[2,512,1408]{2,1,0:T(8,128)(2,1)S(1)}, bf16[2,512,1408]{2,1,0:T(8,128)(2,1)}, u32[]{:S(2)}) copy-start(bf16[2,512,1408]{2,1,0:T(8,128)(2,1)} %param.14) | copy-start | bytes 8650756
  5.6 33.2 %all-to-all-start = ((bf16[32,16,512]{2,1,0:T(8,128)(2,1)}), bf16[32,16,512]{2,1,0:T(8,128)(2,1)}, u32[]{:S(2)}, u32[]{:S(2)}) async-start(bf16[32,16,512]{2,1,0:T(8,128)(2,1)} %bitcast.8), calls=%async_computation | async-start | bytes 1048576 | tf_op jit(solution)/shard_map/all_to_all | solution.py:31
  17.4 2.3 copy-start.6
  24.1 13.6 %copy-start.22 = (bf16[128,512]{1,0:T(8,128)(2,1)S(1)}, bf16[128,512]{1,0:T(8,128)(2,1)}, u32[]{:S(2)}) copy-start(bf16[128,512]{1,0:T(8,128)(2,1)} %param.11) | copy-start | bytes 393220
  38.9 19.0 %all-to-all-start.1 = ((bf16[32,16,512]{2,1,0:T(8,128)(2,1)}), bf16[32,16,512]{2,1,0:T(8,128)(2,1)S(1)}, u32[]{:S(2)}, u32[]{:S(2)}) async-start(bf16[32,16,512]{2,1,0:T(8,128)(2,1)} %bitcast.10), calls=%async_computation.1 | async-start | bytes 1048576 | tf_op jit(solution)/shard_map/all_to_all | solution.py:31
  58.7 34.8 %all-to-all-start.5 = ((bf16[32,48,768]{2,1,0:T(8,128)(2,1)}), bf16[32,48,768]{2,1,0:T(8,128)(2,1)S(1)}, u32[]{:S(2)}, u32[]{:S(2)}) async-start(bf16[32,48,768]{2,1,0:T(8,128)(2,1)} %bitcast.28), calls=%async_computation.5 | async-start | bytes 4718592 | tf_op jit(solution)/shard_map/all_to_all | solution.py:31
  93.5 22.1 %all-to-all-start.3 = ((bf16[32,32,512]{2,1,0:T(8,128)(2,1)}), bf16[32,32,512]{2,1,0:T(8,128)(2,1)}, u32[]{:S(2)}, u32[]{:S(2)}) async-start(bf16[32,32,512]{2,1,0:T(8,128)(2,1)} %bitcast.21), calls=%async_computation.3 | async-start | bytes 2097152 | tf_op jit(solution)/shard_map/all_to_all | solution.py:31
  115.6 87.5 %all-to-all-start.6 = ((bf16[32,48,768]{2,1,0:T(8,128)(2,1)}), bf16[32,48,768]{2,1,0:T(8,128)(2,1)S(1)}, u32[]{:S(2)}, u32[]{:S(2)}) async-start(bf16[32,48,768]{2,1,0:T(8,128)(2,1)} %broadcast_select_fusion), calls=%async_computation.6 | async-start | bytes 4718592 | tf_op jit(solution)/shard_map/all_to_all | solution.py:31
  203.1 8.1 %copy-start.2 = (bf16[32,48,768]{2,1,0:T(8,128)(2,1)}, bf16[32,48,768]{2,1,0:T(8,128)(2,1)S(1)}, u32[]{:S(2)}) copy-start(bf16[32,48,768]{2,1,0:T(8,128)(2,1)S(1)} %all-to-all-done.6) | copy-start | bytes 7077892
  203.1 25.0 %all-to-all-start.4 = ((bf16[32,32,512]{2,1,0:T(8,128)(2,1)}), bf16[32,32,512]{2,1,0:T(8,128)(2,1)S(1)}, u32[]{:S(2)}, u32[]{:S(2)}) async-start(bf16[32,32,512]{2,1,0:T(8,128)(2,1)} %bitcast.23), calls=%async_computation.4 | async-start | bytes 2097152 | tf_op jit(solution)/shard_map/all_to_all | solution.py:31
  229.1 100.1 %all-to-all-start.2 = ((bf16[32,16,512]{2,1,0:T(8,128)(2,1)}), bf16[32,16,512]{2,1,0:T(8,128)(2,1)S(1)}, u32[]{:S(2)}, u32[]{:S(2)}) async-start(bf16[32,16,512]{2,1,0:T(8,128)(2,1)} %bitcast.131), calls=%async_computation.2 | async-start | bytes 1048576 | tf_op jit(solution)/shard_map/all_to_all | solution.py:31
  317.8 2.8 copy-start.13
  321.7 5.1 %copy-start.18 = (bf16[512,768]{1,0:T(8,128)(2,1)}, bf16[512,768]{1,0:T(8,128)(2,1)S(1)}, u32[]{:S(2)}) copy-start(bf16[512,768]{1,0:T(8,128)(2,1)S(1)} %convolution_convert_fusion.5) | copy-start | bytes 2359300
  324.2 2.6 copy-start.14
  330.0 35.3 %all-to-all-start.8 = ((bf16[32,48,640]{2,1,0:T(8,128)(2,1)}), bf16[32,48,640]{2,1,0:T(8,128)(2,1)}, u32[]{:S(2)}, u32[]{:S(2)}) async-start(bf16[32,48,640]{2,1,0:T(8,128)(2,1)} %bitcast.107), calls=%async_computation.8 | async-start | bytes 3932160 | tf_op jit(solution)/shard_map/all_to_all | solution.py:31
  365.3 21.4 %all-to-all-start.7 = ((bf16[32,32,512]{2,1,0:T(8,128)(2,1)}), bf16[32,32,512]{2,1,0:T(8,128)(2,1)S(1)}, u32[]{:S(2)}, u32[]{:S(2)}) async-start(bf16[32,32,512]{2,1,0:T(8,128)(2,1)} %bitcast.123), calls=%async_computation.7 | async-start | bytes 2097152 | tf_op jit(solution)/shard_map/all_to_all | solution.py:31
  373.7 17.1 %copy-start.25 = (f32[32,1,16]{2,1,0:T(1,128)S(1)}, f32[32,1,16]{2,1,0:T(1,128)}, u32[]{:S(2)}) copy-start(f32[32,1,16]{2,1,0:T(1,128)} %get-tuple-element.42) | copy-start | bytes 6148
  373.7 17.7 %copy-start.9 = (bf16[32,3,16,128]{3,2,1,0:T(8,128)(2,1)S(1)}, bf16[32,3,16,128]{3,2,1,0:T(8,128)(2,1)}, u32[]{:S(2)}) copy-start(bf16[32,3,16,128]{3,2,1,0:T(8,128)(2,1)} %get-tuple-element.45) | copy-start | bytes 1179652
  373.7 18.6 %copy-start.24 = (bf16[32,2,16]{2,1,0:T(2,128)(2,1)S(1)}, bf16[32,2,16]{2,1,0:T(2,128)(2,1)}, u32[]{:S(2)}) copy-start(bf16[32,2,16]{2,1,0:T(2,128)(2,1)} %get-tuple-element.8) | copy-start | bytes 6148
  386.7 30.8 %all-to-all-start.9 = ((bf16[32,48,640]{2,1,0:T(8,128)(2,1)}), bf16[32,48,640]{2,1,0:T(8,128)(2,1)S(1)}, u32[]{:S(2)}, u32[]{:S(2)}) async-start(bf16[32,48,640]{2,1,0:T(8,128)(2,1)} %broadcast_select_fusion.2), calls=%async_computation.9 | async-start | bytes 3932160 | tf_op jit(solution)/shard_map/all_to_all | solution.py:31
  393.3 3.7 copy-start.4
  (15 other events, 22.8 us)

commit v3 on v1

v3 whole, which is shorter than its diff:
```python
import jax
import jax.numpy as jnp
from jax import lax
from jax.experimental import pallas as pl
from jax.experimental.pallas import tpu as pltpu
from jax.sharding import PartitionSpec as P

BF = jnp.bfloat16
F32 = jnp.float32
MESH = pl.DeviceIdType.MESH
N_HID = 4


def silu_parts(values):
    sigma = jax.nn.sigmoid(values)
    return (values * sigma, sigma * (1.0 + values * (1.0 - sigma)))


def mm(a, b):
    return jnp.dot(a, b, preferred_element_type=F32)


def mm_nt(a, b):
    return lax.dot_general(a, b, (((1,), (1,)), ((), ())), preferred_element_type=F32)


def mm_tn(a, b):
    return lax.dot_general(a, b, (((0,), (0,)), ((), ())), preferred_element_type=F32)


def add_to(ref, other):
    ref[...] = (ref[...].astype(F32) + other[...].astype(F32)).astype(BF)


class Ring:
    def __init__(self, part, in_a, in_b, in_l, in_r, full, sends, recvs):
        self.part, self.in_a, self.in_b, self.in_l, self.in_r = part, in_a, in_b, in_l, in_r
        self.full, self.sends, self.recvs = full, sends, recvs
        self.me = lax.axis_index("hidden")
        self.right = lax.rem(self.me + 1, N_HID)
        self.left = lax.rem(self.me + 3, N_HID)
        self.across = lax.rem(self.me + 2, N_HID)
        self.chunk = part.shape[2]
        self.lo = pl.ds(0, self.chunk // 2)
        self.hi = pl.ds(self.chunk // 2, self.chunk // 2)
        self.copies = {}

    def send(self, src, dst, kind, q, peer):
        copy = pltpu.make_async_remote_copy(
            src_ref=src,
            dst_ref=dst,
            send_sem=self.sends.at[kind, q],
            recv_sem=self.recvs.at[kind, q],
            device_id={"hidden": peer},
            device_id_type=MESH,
        )
        copy.start()
        self.copies[kind, q] = copy

    def start(self, q, product):
        part = self.part
        part[q, self.across] = product(self.across).astype(BF)
        self.send(part.at[q, self.across, self.lo], self.in_a.at[q], 0, q, self.right)
        self.send(part.at[q, self.across, self.hi], self.in_b.at[q], 1, q, self.left)

    def rest(self, q, product):
        for index in (self.right, self.left, self.me):
            self.part[q, index] = product(index).astype(BF)

    def second(self, q):
        part = self.part
        self.copies[0, q].wait_recv()
        add_to(part.at[q, self.right, self.lo], self.in_a.at[q])
        self.send(part.at[q, self.right], self.in_l.at[q], 2, q, self.right)
        self.copies[1, q].wait_recv()
        add_to(part.at[q, self.left, self.hi], self.in_b.at[q])
        self.send(part.at[q, self.left], self.in_r.at[q], 3, q, self.left)

    def acts(self, cover):
        for q in range(3):
            self.copies[2, q].wait_recv()
            self.copies[3, q].wait_recv()
        step = 32

        @pl.loop(0, self.chunk // step)
        def _(tile):
            rows = pl.ds(pl.multiple_of(tile * step, step), step)

            def total(q):
                own = self.part[q, self.me, rows].astype(F32)
                return own + self.in_l[q, rows].astype(F32) + self.in_r[q, rows].astype(F32)

            g, u, dh = total(0), total(1), total(2)
            active, slope = silu_parts(g)
            values = (active * u, dh * u * slope, dh * active)
            for q in range(3):
                value = values[q] if cover is None else values[q] * cover
                self.full[q, self.me, rows] = value.astype(BF)

    def publish(self, q):
        mine = self.full.at[q, self.me]
        self.send(mine, mine, 4, q, self.right)
        self.send(mine, mine, 5, q, self.left)

    def forward(self, q):
        self.copies[4, q].wait_recv()
        half = self.full.at[q, self.left, self.lo]
        self.send(half, half, 6, q, self.right)
        self.copies[5, q].wait_recv()
        half = self.full.at[q, self.right, self.hi]
        self.send(half, half, 7, q, self.left)

    def arrived(self, q):
        self.copies[6, q].wait_recv()
        self.copies[7, q].wait_recv()

    def sent(self, kinds):
        for kind in kinds:
            for q in range(3):
                self.copies[kind, q].wait_send()


def mega_kernel(
    table,
    tokens,
    cot,
    place,
    place_hi,
    place_lo,
    gate,
    up,
    down,
    send_ids,
    keep_ids,
    cover_ref,
    mixed,
    out_p,
    out_m,
    out_far,
    hot,
    sx_p,
    sx_m,
    rx_p,
    rx_m,
    w_send,
    w_mid0,
    w_mid1,
    w_mid2,
    w_got,
    w_keep,
    part_p,
    a_p,
    b_p,
    l_p,
    r_p,
    full_p,
    part_m,
    a_m,
    b_m,
    l_m,
    r_m,
    full_m,
    g_mid0,
    g_mid1,
    g_mid2,
    g_far,
    back_p,
    back_m,
    ring_ps,
    ring_pr,
    ring_ms,
    ring_mr,
    a2a_s,
    a2a_r,
    out_s,
):
    n = lax.axis_size("expert")
    me = lax.axis_index("expert")
    slot = table[n]
    weights = (gate, up, down)
    w_mid = (w_mid0, w_mid1, w_mid2)
    g_mid = (g_mid0, g_mid1, g_mid2)
    width = tokens.shape[1]
    neurons = gate.shape[2]
    half = w_keep.shape[2]
    far = g_far.shape[2]
    skip = half - far
    piece = width // n
    rows_p, rows_m = sx_p.shape[1], sx_m.shape[1]
    dp, dm = rows_p // n, rows_m // n
    y_z = n // 2

    def peer(step):
        flip = lax.rem(step, 2)
        shift = lax.div(step, 2)
        core = lax.rem(me, 2)
        node = lax.div(me, 2)
        side = 4 if y_z == 16 else y_z
        hi, lo = lax.div(node, side), lax.rem(node, side)
        dhi, dlo = lax.div(shift, side), lax.rem(shift, side)
        hi = lax.rem(hi + dhi, y_z // side)
        lo = lax.rem(lo + dlo, side)
        return (hi * side + lo) * 2 + lax.rem(core + flip, 2)

    ring_p = Ring(part_p, a_p, b_p, l_p, r_p, full_p, ring_ps, ring_pr)
    ring_m = Ring(part_m, a_m, b_m, l_m, r_m, full_m, ring_ms, ring_mr)

    barrier = pltpu.get_barrier_semaphore()
    for other in (ring_p.left, ring_p.right):
        pl.semaphore_signal(barrier, inc=1, device_id={"hidden": other}, device_id_type=MESH)

    @pl.loop(1, n)
    def _(step):
        pl.semaphore_signal(barrier, inc=1, device_id={"expert": peer(step)}, device_id_type=MESH)

    def scatter(sem, src_of, dst_of):
        @pl.loop(1, n)
        def _(step):
            other = peer(step)
            pltpu.make_async_remote_copy(
                src_ref=src_of(other),
                dst_ref=dst_of(me),
                send_sem=a2a_s.at[sem],
                recv_sem=a2a_r.at[sem],
                device_id={"expert": other},
                device_id_type=MESH,
            ).start()

    def landed(sem, ref):
        pltpu.make_async_copy(ref, ref, a2a_r.at[sem]).wait()

    def left_here(sem, ref):
        pltpu.make_async_copy(ref, ref, a2a_s.at[sem]).wait()

    def block(index, size):
        return pl.ds(pl.multiple_of(index * size, size), size)

    def build(base, rows, out):
        @pl.loop(0, rows // 128)
        def _(tile):
            src = pl.ds(pl.multiple_of(base + tile * 128, 128), 128)
            dst = block(tile, 128)
            out[0, dst] = mm(place[src, :], tokens[...]).astype(BF)
            out[1, dst] = (mm(place_hi[src, :], cot[...]) + mm(place_lo[src, :], cot[...])).astype(BF)

    build(0, rows_p, sx_p)
    pl.semaphore_wait(barrier, n + 1)

    scatter(0, lambda d: sx_p.at[:, block(d, dp)], lambda m: rx_p.at[:, block(m, dp)])
    rx_p[:, block(me, dp)] = sx_p[:, block(me, dp)]

    def ordered(ids, q, out):
        @pl.loop(0, width // 128)
        def _(tile):
            rows = block(tile, 128)
            out[q, rows] = mm(weights[q][slot, rows, :], hot[...]).astype(BF)

    def fill_hot(ids):
        @pl.loop(0, neurons // 128)
        def _(tile):
            rows = lax.broadcasted_iota(jnp.int32, (128, half), 0) + tile * 128
            hot[block(tile, 128)] = jnp.where(rows == ids[0:1, :], 1.0, 0.0).astype(BF)

    fill_hot(send_ids)
    for q in range(3):
        ordered(send_ids, q, w_send)
        scatter(1 + q, lambda d: w_send.at[q, block(d, piece)], lambda m: w_mid[q].at[m])
        w_mid[q][me] = w_send[q, block(me, piece)]

    build(rows_p, rows_m, sx_m)
    scatter(7, lambda d: sx_m.at[0, block(d, dm)], lambda m: rx_m.at[0, block(m, dm)])
    rx_m[0, block(me, dm)] = sx_m[0, block(me, dm)]
    rx_m[1, block(me, dm)] = sx_m[1, block(me, dm)]
    fill_hot(keep_ids)
    for q in range(3):
        ordered(keep_ids, q, w_keep)

    landed(0, rx_p.at[:, pl.ds(0, (n - 1) * dp)])
    lefts = (0, 0, 1)

    def product_p(q):
        def product(index):
            return mm(rx_p[lefts[q], block(index, ring_p.chunk), :], weights[q][1 - slot])

        return product

    def product_m(q):
        def product(index):
            return mm(rx_m[lefts[q], block(index, ring_m.chunk), :], w_keep[q])

        return product

    for q in range(3):
        ring_p.start(q, product_p(q))
    for q in range(3):
        ring_p.rest(q, product_p(q))

    def hop(q, mid, cols, first, then, dst_of):
        landed(first, mid[q].at[pl.ds(0, n - 1)])
        left_here(first, mid[q].at[pl.ds(0, n - 1)])

        @pl.loop(0, n)
        def _(other):
            w_send[q, block(other, piece), cols] = mid[q][table[other]]

        scatter(then, lambda d: w_send.at[q, block(d, piece), cols], dst_of(q))

    every = pl.ds(0, half)
    got_of = lambda q: lambda m: w_got.at[q, block(m, piece)]
    ring_p.second(0)
    hop(0, w_mid, every, 1, 4, got_of)
    w_got[0, block(me, piece)] = w_send[0, block(me, piece)]
    scatter(8, lambda d: sx_m.at[1, block(d, dm)], lambda m: rx_m.at[1, block(m, dm)])
    ring_p.second(1)
    hop(1, w_mid, every, 2, 5, got_of)
    w_got[1, block(me, piece)] = w_send[1, block(me, piece)]
    ring_p.second(2)
    hop(2, w_mid, every, 3, 6, got_of)
    w_got[2, block(me, piece)] = w_send[2, block(me, piece)]

    def blend(q):
        landed(4 + q, w_got.at[q, pl.ds(0, (n - 1) * piece)])

        @pl.loop(0, width // 128)
        def _(tile):
            rows = block(tile, 128)
            both = w_keep[q, rows].astype(F32) + w_got[q, rows].astype(F32)
            w_keep[q, rows] = (0.5 * both).astype(BF)

    landed(7, rx_m.at[0, pl.ds(0, (n - 1) * dm)])
    blend(0)
    ring_m.start(0, product_m(0))
    ring_m.rest(0, product_m(0))
    ring_p.acts(None)
    ring_p.publish(0)
    ring_m.second(0)
    blend(1)
    ring_m.start(1, product_m(1))
    ring_m.rest(1, product_m(1))
    ring_p.forward(0)
    landed(8, rx_m.at[1, pl.ds(0, (n - 1) * dm)])
    blend(2)
    ring_m.start(2, product_m(2))
    ring_m.rest(2, product_m(2))
    ring_m.second(1)
    ring_m.second(2)

    left_here(0, sx_p.at[:, pl.ds(0, (n - 1) * dp)])
    ring_p.arrived(0)
    for index in range(N_HID):
        rows = pl.ds(index * ring_p.chunk, ring_p.chunk)
        sx_p[0, rows] = mm_nt(full_p[0, index], weights[2][1 - slot]).astype(BF)
    scatter(9, lambda d: sx_p.at[0, block(d, dp)], lambda m: back_p.at[block(m, dp)])
    back_p[block(me, dp)] = sx_p[0, block(me, dp)]

    def gradient(left, full, rows, q, store):
        @pl.loop(0, width // 128)
        def _(tile):
            cols = block(tile, 128)
            right = full[q].reshape(rows, full.shape[3])
            store(tile, mm_tn(left[:, cols], right).astype(BF))

    ring_p.sent((0, 1, 2, 3))

    def store_p(q):
        def store(tile, value):
            part_p[q, tile] = value

        return store

    def store_m(q):
        def store(tile, value):
            part_m[q, lax.div(tile, 2), block(lax.rem(tile, 2), 128)] = value

        return store

    def grads_p(q, target):
        gradient(rx_p.at[1 if q == 0 else 0], full_p, rows_p, q, store_p(target))
        pltpu.make_async_copy(part_p.at[target], out_p.at[target], out_s.at[target]).start()

    cover = cover_ref[0:1, :]
    ring_m.acts(cover)
    ring_m.publish(0)
    ring_m.publish(1)
    grads_p(0, 2)
    ring_m.forward(0)
    ring_m.publish(2)
    ring_m.forward(1)
    ring_p.publish(1)
    ring_p.publish(2)

    def grads_m(q, target):
        gradient(rx_m.at[1 if q == 0 else 0], full_m, rows_m, q, store_m(target))
        pltpu.make_async_copy(part_m.at[target, pl.ds(0, 2)], out_m.at[target], out_s.at[3 + target]).start()

        def src(d):
            rows = block(lax.rem(d, n // 2), piece)
            return part_m.at[target, lax.div(d, n // 2), rows, pl.ds(skip, far)]

        scatter(11 + target, src, lambda m: g_mid[target].at[m])
        rows = block(lax.rem(me, n // 2), piece)
        g_mid[target][me] = part_m[target, lax.div(me, n // 2), rows, pl.ds(skip, far)]

    ring_m.arrived(0)
    ring_m.sent((0, 1, 2, 3))
    grads_m(0, 2)
    ring_m.forward(2)
    left_here(7, sx_m.at[0, pl.ds(0, (n - 1) * dm)])
    for index in range(N_HID):
        rows = pl.ds(index * ring_m.chunk, ring_m.chunk)
        sx_m[0, rows] = mm_nt(full_m[0, index], w_keep[2]).astype(BF)
    scatter(10, lambda d: sx_m.at[0, block(d, dm)], lambda m: back_m.at[block(m, dm)])
    back_m[block(me, dm)] = sx_m[0, block(me, dm)]
    ring_m.arrived(1)
    grads_m(1, 0)
    ring_p.forward(1)
    ring_m.arrived(2)
    grads_m(2, 1)
    ring_p.forward(2)

    for q in range(3):
        left_here(4 + q, w_mid[q].at[pl.ds(0, n - 1)])
    some = pl.ds(0, far)
    far_of = lambda q: lambda m: g_far.at[q, block(m, piece)]
    for q in (2, 0, 1):
        hop(q, g_mid, some, 11 + q, 14 + q, far_of)
        g_far[q, block(me, piece)] = w_send[q, block(me, piece), some]

    ring_p.arrived(1)
    grads_p(1, 0)
    ring_p.arrived(2)
    grads_p(2, 1)

    landed(9, back_p.at[pl.ds(0, (n - 1) * dp)])
    landed(10, back_m.at[pl.ds(0, (n - 1) * dm)])
    span_p, span_m = pl.ds(0, rows_p), pl.ds(rows_p, rows_m)
    total = mm_tn(place_hi[span_p, :], back_p[...]) + mm_tn(place_lo[span_p, :], back_p[...])
    total += mm_tn(place_hi[span_m, :], back_m[...]) + mm_tn(place_lo[span_m, :], back_m[...])
    mixed[...] = total.astype(BF)

    for q in (2, 0, 1):
        landed(14 + q, g_far.at[q, pl.ds(0, (n - 1) * piece)])
        pltpu.make_async_copy(g_far.at[q], out_far.at[q], out_s.at[6 + q]).start()

    left_here(8, sx_m.at[1, pl.ds(0, (n - 1) * dm)])
    left_here(9, sx_p.at[0, pl.ds(0, (n - 1) * dp)])
    left_here(10, sx_m.at[0, pl.ds(0, (n - 1) * dm)])
    for q in range(3):
        left_here(14 + q, g_far.at[q, pl.ds(0, (n - 1) * piece)])
        pltpu.make_async_copy(part_p.at[q], out_p.at[q], out_s.at[q]).wait()
        pltpu.make_async_copy(part_m.at[q, pl.ds(0, 2)], out_m.at[q], out_s.at[3 + q]).wait()
        pltpu.make_async_copy(g_far.at[q], out_far.at[q], out_s.at[6 + q]).wait()
    for ring in (ring_p, ring_m):
        ring.sent((4, 5, 6, 7))


def mega(table, tokens, cot, place, place_hi, place_lo, gate, up, down, send_ids, keep_ids, cover, n, depth):
    width, neurons = gate.shape[1], gate.shape[2]
    half = send_ids.shape[1]
    far = neurons - half
    rows_p, rows_m = n * depth, 2 * n * depth
    piece = width // n
    cp, cm = rows_p // N_HID, rows_m // N_HID
    vmem = pl.BlockSpec(memory_space=pltpu.VMEM)
    smem = pl.BlockSpec(memory_space=pltpu.SMEM)
    hbm = pl.BlockSpec(memory_space=pl.ANY)

    def ring(chunk, cols):
        return [
            pltpu.VMEM((3, N_HID, chunk, cols), BF),
            pltpu.VMEM((3, chunk // 2, cols), BF),
            pltpu.VMEM((3, chunk // 2, cols), BF),
            pltpu.VMEM((3, chunk, cols), BF),
            pltpu.VMEM((3, chunk, cols), BF),
            pltpu.VMEM((3, N_HID, chunk, cols), BF),
        ]

    return pl.pallas_call(
        mega_kernel,
        out_shape=(
            jax.ShapeDtypeStruct(tokens.shape, BF),
            jax.ShapeDtypeStruct((3, width // 128, 128, neurons), BF),
            jax.ShapeDtypeStruct((3, 2, width // 2, half), BF),
            jax.ShapeDtypeStruct((3, width, far), BF),
        ),
        in_specs=[smem] + [vmem] * 11,
        out_specs=(vmem, hbm, hbm, hbm),
        scratch_shapes=[
            pltpu.VMEM((neurons, half), BF),
            pltpu.VMEM((2, rows_p, width), BF),
            pltpu.VMEM((2, rows_m, width), BF),
            pltpu.VMEM((2, rows_p, width), BF),
            pltpu.VMEM((2, rows_m, width), BF),
            pltpu.VMEM((3, width, half), BF),
            *[pltpu.VMEM((n, piece, half), BF)] * 3,
            pltpu.VMEM((3, width, half), BF),
            pltpu.VMEM((3, width, half), BF),
            *ring(cp, neurons),
            *ring(cm, half),
            *[pltpu.VMEM((n, piece, far), BF)] * 3,
            pltpu.VMEM((3, width, far), BF),
            pltpu.VMEM((rows_p, width), BF),
            pltpu.VMEM((rows_m, width), BF),
            pltpu.SemaphoreType.DMA((8, 3)),
            pltpu.SemaphoreType.DMA((8, 3)),
            pltpu.SemaphoreType.DMA((8, 3)),
            pltpu.SemaphoreType.DMA((8, 3)),
            pltpu.SemaphoreType.DMA((17,)),
            pltpu.SemaphoreType.DMA((17,)),
            pltpu.SemaphoreType.DMA((9,)),
        ],
        compiler_params=pltpu.CompilerParams(
            collective_id=0, has_side_effects=True, vmem_limit_bytes=67_043_328
        ),
    )(table, tokens, cot, place, place_hi, place_lo, gate, up, down, send_ids, keep_ids, cover)


def shards(
    tokens,
    cotangent,
    gate_weight,
    up_weight,
    down_weight,
    routing,
    route_weight,
    merge_source,
    merge_target,
    neuron_perm,
):
    devices_n = lax.axis_size("expert")
    me = lax.axis_index("expert")
    exp_local, width, neurons = gate_weight.shape
    experts = exp_local * devices_n
    half = -(-neurons // 256) * 128
    tail = neurons - half
    tok_local, top_count = routing.shape
    depth = max(2, tok_local * top_count * 4 // (3 * experts))
    device_ids = jnp.arange(devices_n, dtype=jnp.int32)

    src_hit = (merge_source[:, None] // exp_local) == device_ids[None, :]
    tgt_hit = (merge_target[:, None] // exp_local) == device_ids[None, :]
    any_hit = src_hit | tgt_hit

    def pick(hit, values):
        return jnp.sum(jnp.where(hit, values[:, None], 0), axis=0)

    source_of = pick(any_hit, merge_source)
    target_of = pick(any_hit, merge_target)
    is_src = jnp.any(src_hit, axis=0)
    own_merge = jnp.where(is_src, source_of, target_of)
    partner_dev = jnp.where(is_src, target_of, source_of) // exp_local
    plain_of = device_ids * exp_local * 2 + (exp_local - 1) - own_merge
    i_am_src = jnp.any((merge_source // exp_local) == me)
    merge_slot = jnp.sum(jnp.where(device_ids == me, own_merge, 0)) - me * exp_local
    table = jnp.concatenate([partner_dev, jnp.full((8,), merge_slot, jnp.int32)])

    mine = ((merge_source // exp_local) == me) | ((merge_target // exp_local) == me)
    perm = jnp.sum(jnp.where(mine[:, None], neuron_perm, 0), axis=0)
    ids = jnp.arange(neurons, dtype=jnp.int32)
    send_ids = jnp.where(i_am_src, perm[:half], ids[tail:])
    keep_ids = jnp.where(i_am_src, perm[tail:], ids[:half])
    send_ids = jnp.broadcast_to(send_ids[None, :], (8, half))
    keep_ids = jnp.broadcast_to(keep_ids[None, :], (8, half))
    overlap = jnp.arange(half, dtype=jnp.int32) < (half - tail)
    cover = jnp.broadcast_to(jnp.where(i_am_src & overlap, 0.0, 1.0).astype(F32)[None, :], (8, half))

    def placing(slot_expert):
        hit = routing.T[None, :, :] == slot_expert[:, None, None]
        chosen = jnp.any(hit, axis=1)
        chosen_w = jnp.sum(jnp.where(hit, route_weight.T[None, :, :], 0.0), axis=1)
        tok_ids = jnp.arange(tok_local, dtype=jnp.int32)
        before = (tok_ids[:, None] < tok_ids[None, :]).astype(BF)
        rank = mm(chosen.astype(BF), before).astype(jnp.int32)
        rank = jnp.where(chosen, rank, -1)
        place = rank[:, None, :] == jnp.arange(depth, dtype=jnp.int32)[None, :, None]
        hi = chosen_w.astype(BF)
        lo = (chosen_w - hi.astype(F32)).astype(BF)
        zero = jnp.zeros((), BF)

        def filled(value):
            return jnp.where(place, value, zero).reshape(-1, tok_local)

        return filled(jnp.ones((), BF)), filled(hi[:, None, :]), filled(lo[:, None, :])

    slot_expert = jnp.concatenate([plain_of, jnp.stack([target_of, source_of], axis=1).reshape(-1)])
    place, place_hi, place_lo = placing(slot_expert)

    mixed, grads_p, grads_m, far = mega(
        table,
        tokens,
        cotangent,
        place,
        place_hi,
        place_lo,
        gate_weight,
        up_weight,
        down_weight,
        send_ids,
        keep_ids,
        cover,
        devices_n,
        depth,
    )
    grads_p = grads_p.reshape(3, width, neurons)
    grads_m = grads_m.reshape(3, width, half)

    outs = []
    for q in range(3):
        full = jnp.concatenate([grads_m[q], far[q]], axis=1)
        full = jnp.where(i_am_src, jnp.zeros_like(full), full)
        plain = grads_p[q]
        first_is_merge = merge_slot == 0
        outs.append(
            jnp.stack([jnp.where(first_is_merge, full, plain), jnp.where(first_is_merge, plain, full)])
        )
    return (mixed, *outs)


def solution(mesh):
    placed = (
        P("expert", "hidden"),
        P("expert", "hidden"),
        P("expert", "hidden", None),
        P("expert", "hidden", None),
        P("expert", "hidden", None),
        P("expert", None),
        P("expert", None),
        P(),
        P(),
        P(),
    )
    return jax.shard_map(
        shards,
        mesh=mesh,
        in_specs=placed,
        out_specs=(
            P("expert", "hidden"),
            P("expert", "hidden", None),
            P("expert", "hidden", None),
            P("expert", "hidden", None),
        ),
        check_vma=False,
    )
```

time: 521 us -> 251 us (0.48)
  waiting for transfers between devices: 261 us -> 0 us
  Pallas kernels: 0 us -> 223 us
  matrix products: 68.5 us -> 0.14 us
  starting transfers between devices: 58.2 us -> 0 us
  local copies, waits for them, and re-layouts: 50.1 us -> 8.21 us
  blocking collectives: 23.7 us -> 0 us
  other arithmetic: 41.3 us -> 17.8 us
  between operations: 15.4 us -> 1.39 us
    pallas_call x0 -> x1, Pallas kernels: none -> 223 us  [mega(): pl.pallas_call(mega_kernel, out_shape=(jax.ShapeDtypeStruct(tokens.shape,...]
    all_to_all x9 -> x0, waiting for transfers between devices: 118 us -> none  [exchange(): lax.all_to_all(values, 'expert', split_axis=0, concat_axis=0, tiled=True)]
    all_gather x6 -> x0, waiting for transfers between devices: 98.3 us -> none  [spread(): return lax.all_gather(values, 'hidden', axis=0, tiled=True)]
    all_to_all x9 -> x0, starting transfers between devices: 57.3 us -> none  [exchange(): lax.all_to_all(values, 'expert', split_axis=0, concat_axis=0, tiled=True)]
    reduce_scatter x6 -> x0, waiting for transfers between devices: 42 us -> none  [reduced(): lax.psum_scatter(part.astype(BF), 'hidden', scatter_dimension=0, tiled=True)]
    dot_general x12 -> x1, matrix products: 37.2 us -> 0.14 us  [mm(): return jnp.dot(a, b, preferred_element_type=F32)]
    dot_general x12 -> x0, matrix products: 31.4 us -> none  [the longest x10 24.7 us: mm_tn(): lax.dot_general(a, b, (((0,), (0,)), ((), ())), preferred_element_type=F32)]
    all_to_all x1 -> x0, blocking collectives: 23.7 us -> none  [exchange(): lax.all_to_all(values, 'expert', split_axis=0, concat_axis=0, tiled=True)]
  transfers between devices with their start and end apart: 21 -> 0, of which waited for: 13 -> 0; matrix products, arithmetic and copies ran while one was open for 23% -> 0% of each run, Pallas kernels for 0% -> 0%
where the time goes in v3:
time: 251 us
  Pallas kernels  223 us (89%)
  other arithmetic  17.8 us (7%)
  local copies, waits for them, and re-layouts  8.21 us (3%)
    pallas_call x1, Pallas kernels, mega(): pl.pallas_call(mega_kernel, out_shape=(jax.ShapeDtypeStruct(tokens.shape,...  223 us
    another operation x3, other arithmetic, shards(): jnp.stack([jnp.where(first_is_merge, full, plain), jnp.where(first_is_mer...  5.6 us

profile of v3, /device:TPU:1, one launch (start us, length us, event | category | flops | bytes accessed | tf_op | source)
XLA Modules:
  0.0 250.5 jit_solution(6401999277596478894)
XLA Ops:
  0.6 1.4 compare_reduce_fusion.1
  2.1 0.7 compare_or_fusion
  2.8 0.8 select_reduce_fusion.1
  3.5 0.6 add_subtract_fusion
  4.8 0.5 concatenate.54.table
  5.4 0.6 fusion.8
  6.0 1.0 select_reduce_fusion
  7.0 0.6 add_select_fusion
  7.9 0.8 compare_reduce_fusion
  8.7 0.6 broadcast_in_dim.134.keep_ids
  9.3 0.6 broadcast_in_dim.137.cover_ref
  9.9 0.6 broadcast_in_dim.133.send_ids
  10.7 0.8 fusion.4
  11.6 1.3 fusion.1
  12.9 223.0 %shard_map.129 = (bf16[128,512]{1,0:T(8,128)(2,1)}, bf16[3,4,128,1408]{3,2,1,0:T(8,128)(2,1)}, bf16[3,2,256,768]{3,2,1,0:T(8,128)(2,1)}, bf16[3,512,640]{2,1,0:T(8,128)(2,1)}) custom-call(s32[40]{0:T(128)} %concatenate.54.table, bf16[128,512]{1,0:T(8,128)(2,1)} %tokens.1, bf16[128,512]{1,0:T(8,128)(2,1)} %cot.1, bf16[1536,128]{1,0:T(8,128)(2,1)} %get-tuple-element.37.place, ...), custom_call_target="tpu_custom_call" | custom-call | tf_op jit(solution)/shard_map/pallas_call | solution.py:478
  235.9 1.8 fusion.12
  238.3 2.1 copy-done
  240.4 0.5 fusion.10
  240.8 2.1 bitcast_select_fusion.1
  242.9 1.3 bitcast_select_fusion.5
  244.3 1.9 pad_maximum_fusion
  246.1 1.9 pad_maximum_fusion.2
  248.0 1.9 pad_maximum_fusion.1
  249.9 0.7 copy.18
  (15 shorter events, 1.2 us)
Async XLA Ops:
  235.9 2.3 copy-start.1
  238.1 2.2 copy-start
  248.0 1.9 copy-start.2

commit v4 on v3

v4 whole, which is shorter than its diff:
```python
import jax
import jax.numpy as jnp
from jax import lax
from jax.experimental import pallas as pl
from jax.experimental.pallas import tpu as pltpu
from jax.sharding import PartitionSpec as P

BF = jnp.bfloat16
F32 = jnp.float32
MESH = pl.DeviceIdType.MESH
N_HID = 4


def silu_parts(values):
    sigma = jax.nn.sigmoid(values)
    return (values * sigma, sigma * (1.0 + values * (1.0 - sigma)))


def mm(a, b):
    return jnp.dot(a, b, preferred_element_type=F32)


def mm_nt(a, b):
    return lax.dot_general(a, b, (((1,), (1,)), ((), ())), preferred_element_type=F32)


def mm_tn(a, b):
    return lax.dot_general(a, b, (((0,), (0,)), ((), ())), preferred_element_type=F32)


def add_to(ref, other):
    ref[...] = (ref[...].astype(F32) + other[...].astype(F32)).astype(BF)


class Ring:
    def __init__(self, part, in_a, in_b, in_l, in_r, full, sends, recvs):
        self.part, self.in_a, self.in_b, self.in_l, self.in_r = part, in_a, in_b, in_l, in_r
        self.full, self.sends, self.recvs = full, sends, recvs
        self.me = lax.axis_index("hidden")
        self.right = lax.rem(self.me + 1, N_HID)
        self.left = lax.rem(self.me + 3, N_HID)
        self.across = lax.rem(self.me + 2, N_HID)
        self.chunk = part.shape[2]
        self.lo = pl.ds(0, self.chunk // 2)
        self.hi = pl.ds(self.chunk // 2, self.chunk // 2)
        self.copies = {}

    def send(self, src, dst, kind, q, peer):
        copy = pltpu.make_async_remote_copy(
            src_ref=src,
            dst_ref=dst,
            send_sem=self.sends.at[kind, q],
            recv_sem=self.recvs.at[kind, q],
            device_id={"hidden": peer},
            device_id_type=MESH,
        )
        copy.start()
        self.copies[kind, q] = copy

    def start(self, q, product):
        part = self.part
        part[q, self.across] = product(self.across).astype(BF)
        self.send(part.at[q, self.across, self.lo], self.in_a.at[q], 0, q, self.right)
        self.send(part.at[q, self.across, self.hi], self.in_b.at[q], 1, q, self.left)

    def rest(self, q, product):
        for index in (self.right, self.left, self.me):
            self.part[q, index] = product(index).astype(BF)

    def second(self, q):
        part = self.part
        self.copies[0, q].wait_recv()
        add_to(part.at[q, self.right, self.lo], self.in_a.at[q])
        self.send(part.at[q, self.right], self.in_l.at[q], 2, q, self.right)
        self.copies[1, q].wait_recv()
        add_to(part.at[q, self.left, self.hi], self.in_b.at[q])
        self.send(part.at[q, self.left], self.in_r.at[q], 3, q, self.left)

    def acts(self, cover):
        for q in range(3):
            self.copies[2, q].wait_recv()
            self.copies[3, q].wait_recv()
        step = 32

        @pl.loop(0, self.chunk // step)
        def _(tile):
            rows = pl.ds(pl.multiple_of(tile * step, step), step)

            def total(q):
                own = self.part[q, self.me, rows].astype(F32)
                return own + self.in_l[q, rows].astype(F32) + self.in_r[q, rows].astype(F32)

            g, u, dh = total(0), total(1), total(2)
            active, slope = silu_parts(g)
            values = (active * u, dh * u * slope, dh * active)
            for q in range(3):
                value = values[q] if cover is None else values[q] * cover
                self.full[q, self.me, rows] = value.astype(BF)

    def publish(self, q):
        mine = self.full.at[q, self.me]
        self.send(mine, mine, 4, q, self.right)
        self.send(mine, mine, 5, q, self.left)

    def forward(self, q):
        self.copies[4, q].wait_recv()
        half = self.full.at[q, self.left, self.lo]
        self.send(half, half, 6, q, self.right)
        self.copies[5, q].wait_recv()
        half = self.full.at[q, self.right, self.hi]
        self.send(half, half, 7, q, self.left)

    def arrived(self, q):
        self.copies[6, q].wait_recv()
        self.copies[7, q].wait_recv()

    def sent(self, kinds):
        for kind in kinds:
            for q in range(3):
                self.copies[kind, q].wait_send()


def mega_kernel(
    sources,
    targets,
    perm_ref,
    routing,
    route_w,
    tokens,
    cot,
    gate_hbm,
    up_hbm,
    down_hbm,
    mixed,
    out_p,
    out_m,
    table,
    gate,
    up,
    down,
    place,
    place_hi,
    place_lo,
    hot,
    sx_p,
    sx_m,
    rx_p,
    rx_m,
    w_send,
    w_mid_a,
    w_mid_b,
    w_got,
    w_keep,
    part_p,
    a_p,
    b_p,
    l_p,
    r_p,
    full_p,
    part_a,
    a_a,
    b_a,
    l_a,
    r_a,
    full_a,
    part_b,
    a_b,
    b_b,
    l_b,
    r_b,
    full_b,
    g_mid_a,
    g_mid_b,
    g_far_a,
    g_far_b,
    back_p,
    back_m,
    ring_sems,
    a2a_s,
    a2a_r,
    in_s,
    out_s,
):
    n = lax.axis_size("expert")
    me = lax.axis_index("expert")
    weights = (gate, up, down)
    width = tokens.shape[1]
    tok_n, top = routing.shape
    neurons = gate.shape[2]
    half = w_keep.shape[2]
    tail = neurons - half
    cols_a, cols_b = full_a.shape[3], full_b.shape[3]
    far_a = g_far_a.shape[3]
    skip = cols_a - far_a
    piece = width // n
    rows_p, rows_m = sx_p.shape[1], sx_m.shape[1]
    dp, dm = rows_p // n, rows_m // n
    log_dp = dp.bit_length() - 1
    span_a, span_b = pl.ds(0, cols_a), pl.ds(cols_a, cols_b)

    def block(index, size):
        return pl.ds(pl.multiple_of(index * size, size), size)

    loads = []
    for q, ref in enumerate((gate_hbm, up_hbm, down_hbm)):
        loads.append(pltpu.make_async_copy(ref, weights[q], in_s.at[q]))
        loads[q].start()

    def peer(step):
        nodes = n // 2
        side = 4 if nodes == 16 else nodes
        core, node = lax.rem(me, 2), lax.div(me, 2)
        flip, shift = lax.rem(step, 2), lax.div(step, 2)
        hi = lax.rem(lax.div(node, side) + lax.div(shift, side), nodes // side)
        lo = lax.rem(lax.rem(node, side) + lax.rem(shift, side), side)
        return (hi * side + lo) * 2 + lax.rem(core + flip, 2)

    ring_p = Ring(part_p, a_p, b_p, l_p, r_p, full_p, ring_sems.at[0], ring_sems.at[1])
    ring_a = Ring(part_a, a_a, b_a, l_a, r_a, full_a, ring_sems.at[2], ring_sems.at[3])
    ring_b = Ring(part_b, a_b, b_b, l_b, r_b, full_b, ring_sems.at[4], ring_sems.at[5])

    barrier = pltpu.get_barrier_semaphore()
    for other in (ring_p.left, ring_p.right):
        pl.semaphore_signal(barrier, inc=1, device_id={"hidden": other}, device_id_type=MESH)

    @pl.loop(1, n)
    def _(step):
        pl.semaphore_signal(barrier, inc=1, device_id={"expert": peer(step)}, device_id_type=MESH)

    pairs = sources.shape[0]
    wide = rows_p
    log_wide = log_dp

    def make_place(tile):
        lane = lax.broadcasted_iota(jnp.int32, (8, wide), 1)
        if tile == 0:
            device = lax.shift_right_logical(lane, log_dp)
        else:
            lane = lane + (tile - 1) * wide
            device = lax.shift_right_logical(lane, log_dp + 1)
        source = jnp.zeros((8, wide), jnp.int32)
        target = jnp.zeros((8, wide), jnp.int32)
        own = jnp.zeros((8, wide), jnp.int32)
        for m in range(pairs):
            s, t = sources[m], targets[m]
            at_s, at_t = device == lax.shift_right_logical(s, 1), device == lax.shift_right_logical(t, 1)
            source = jnp.where(at_s | at_t, s, source)
            target = jnp.where(at_s | at_t, t, target)
            own = jnp.where(at_s, s, jnp.where(at_t, t, own))
        if tile == 0:
            expert = device * 4 + 1 - own
        else:
            is_target = (lax.shift_right_logical(lane, log_dp) & 1) == 0
            expert = jnp.where(is_target, target, source)
        expert = expert[0:1, :]
        chosen = jnp.zeros((tok_n, wide), F32)
        weight = jnp.zeros((tok_n, wide), F32)
        for k in range(top):
            hit = routing[:, k : k + 1] == expert
            chosen = jnp.where(hit, 1.0, chosen)
            weight = jnp.where(hit, route_w[:, k : k + 1], weight)
        row = lax.broadcasted_iota(jnp.int32, (tok_n, tok_n), 0)
        col = lax.broadcasted_iota(jnp.int32, (tok_n, tok_n), 1)
        before = jnp.where(col < row, 1.0, 0.0).astype(BF)
        rank = mm(before, chosen.astype(BF))
        slot_of = (lane[0:1, :] & (dp - 1)).astype(F32)
        here = (rank == slot_of) & (chosen > 0.5)
        hi = weight.astype(BF).astype(F32)
        span = pl.ds(tile * wide, wide)
        place[:, span] = jnp.where(here, 1.0, 0.0).astype(BF)
        place_hi[:, span] = jnp.where(here, hi, 0.0).astype(BF)
        place_lo[:, span] = jnp.where(here, weight - hi, 0.0).astype(BF)

    def build_x(base, rows, out):
        @pl.loop(0, rows // 128)
        def _(tile):
            src = pl.ds(pl.multiple_of(base + tile * 128, 128), 128)
            out[0, block(tile, 128)] = mm_tn(place[:, src], tokens[...]).astype(BF)

    def build_dy(base, rows, out):
        @pl.loop(0, rows // 128)
        def _(tile):
            src = pl.ds(pl.multiple_of(base + tile * 128, 128), 128)
            value = mm_tn(place_hi[:, src], cot[...]) + mm_tn(place_lo[:, src], cot[...])
            out[1, block(tile, 128)] = value.astype(BF)

    def scatter(sem, src_of, dst_of):
        @pl.loop(1, n)
        def _(step):
            other = peer(step)
            pltpu.make_async_remote_copy(
                src_ref=src_of(other),
                dst_ref=dst_of(me),
                send_sem=a2a_s.at[sem],
                recv_sem=a2a_r.at[sem],
                device_id={"expert": other},
                device_id_type=MESH,
            ).start()

    def landed(sem, ref):
        pltpu.make_async_copy(ref, ref, a2a_r.at[sem]).wait()

    def left_here(sem, ref):
        pltpu.make_async_copy(ref, ref, a2a_s.at[sem]).wait()

    all_p, all_m, peers = pl.ds(0, (n - 1) * dp), pl.ds(0, (n - 1) * dm), pl.ds(0, n - 1)

    def dispatch(sem, which, size, src, dst):
        scatter(sem, lambda d: src.at[which, block(d, size)], lambda m: dst.at[which, block(m, size)])
        dst[which, block(me, size)] = src[which, block(me, size)]

    make_place(0)
    build_x(0, rows_p, sx_p)
    pl.semaphore_wait(barrier, n + 1)
    dispatch(0, 0, dp, sx_p, rx_p)
    build_dy(0, rows_p, sx_p)
    dispatch(1, 1, dp, sx_p, rx_p)

    slot, is_src = jnp.int32(0), jnp.int32(0)
    for m in range(pairs):
        s, t = sources[m], targets[m]
        at_s, at_t = lax.shift_right_logical(s, 1) == me, lax.shift_right_logical(t, 1) == me
        slot = jnp.where(at_s, s & 1, jnp.where(at_t, t & 1, slot))
        is_src = jnp.where(at_s, 1, is_src)

    def fill_table(device, carry):
        partner = jnp.int32(0)
        for m in range(pairs):
            s, t = lax.shift_right_logical(sources[m], 1), lax.shift_right_logical(targets[m], 1)
            partner = jnp.where(s == device, t, jnp.where(t == device, s, partner))
        table[device] = partner
        return carry

    perm = jnp.zeros((8, neurons), jnp.int32)
    for m in range(pairs):
        s, t = lax.shift_right_logical(sources[m], 1), lax.shift_right_logical(targets[m], 1)
        mine = jnp.where((s == me) | (t == me), 1, 0)
        perm = perm + perm_ref[m : m + 1, :] * mine
    perm = perm[0:1, :]
    lane = lax.broadcasted_iota(jnp.int32, (1, half), 1)
    send_ids = jnp.where(is_src > 0, perm[:, :half], lane + tail)
    keep_ids = jnp.where(is_src > 0, perm[:, tail:], lane)

    def ordered(ids, span, out):
        @pl.loop(0, neurons // 128)
        def _(tile):
            units = ids[:, span.start : span.start + span.size]
            rows = lax.broadcasted_iota(jnp.int32, (128, span.size), 0) + tile * 128
            hot[block(tile, 128), span] = jnp.where(rows == units, 1.0, 0.0).astype(BF)

        for q in range(3):

            @pl.loop(0, width // 128)
            def _(tile):
                rows = block(tile, 128)
                out[q, rows, span] = mm(weights[q][slot, rows, :], hot[:, span]).astype(BF)

    def first_hop(sem, span, mid):
        scatter(sem, lambda d: w_send.at[:, block(d, piece), span], lambda m: mid.at[m])
        mid[me] = w_send[:, block(me, piece), span]

    def second_hop(first, then, mid, span, dst_of):
        landed(first, mid.at[peers])
        left_here(first, mid.at[peers])

        @pl.loop(0, n)
        def _(other):
            w_send[:, block(other, piece), span] = mid[table[other]]

        scatter(then, lambda d: w_send.at[:, block(d, piece), span], dst_of)

    for load in loads:
        load.wait()
    ordered(send_ids, span_a, w_send)
    first_hop(2, span_a, w_mid_a)
    make_place(1)
    make_place(2)
    build_x(rows_p, rows_m, sx_m)
    dispatch(6, 0, dm, sx_m, rx_m)

    lefts = (0, 0, 1)

    def product_p(q):
        def product(index):
            return mm(rx_p[lefts[q], block(index, ring_p.chunk), :], weights[q][1 - slot])

        return product

    def product_m(ring, q, span):
        def product(index):
            return mm(rx_m[lefts[q], block(index, ring.chunk), :], w_keep[q, :, span])

        return product

    landed(0, rx_p.at[0, all_p])
    ring_p.start(0, product_p(0))
    ring_p.start(1, product_p(1))
    landed(1, rx_p.at[1, all_p])
    ring_p.start(2, product_p(2))
    ring_p.rest(0, product_p(0))
    ring_p.second(0)
    ring_p.rest(1, product_p(1))
    ring_p.second(1)
    ring_p.rest(2, product_p(2))
    ring_p.second(2)
    lax.fori_loop(0, n, fill_table, 0)
    build_dy(rows_p, rows_m, sx_m)
    ordered(send_ids, span_b, w_send)

    got_of = lambda span: lambda m: w_got.at[:, block(m, piece), span]
    second_hop(2, 4, w_mid_a, span_a, got_of(span_a))
    w_got[:, block(me, piece), span_a] = w_send[:, block(me, piece), span_a]
    dispatch(7, 1, dm, sx_m, rx_m)
    first_hop(3, span_b, w_mid_b)
    ordered(keep_ids, span_a, w_keep)
    ordered(keep_ids, span_b, w_keep)

    def blend(sem, span):
        landed(sem, w_got.at[:, pl.ds(0, (n - 1) * piece), span])
        for q in range(3):

            @pl.loop(0, width // 128)
            def _(tile):
                rows = block(tile, 128)
                both = w_keep[q, rows, span].astype(F32) + w_got[q, rows, span].astype(F32)
                w_keep[q, rows, span] = (0.5 * both).astype(BF)

    ring_p.acts(None)
    ring_p.publish(0)
    landed(6, rx_m.at[0, all_m])
    blend(4, span_a)
    for q in range(2):
        ring_a.start(q, product_m(ring_a, q, span_a))
    for q in range(2):
        ring_a.rest(q, product_m(ring_a, q, span_a))
    ring_a.second(0)
    ring_a.second(1)
    ring_p.forward(0)
    landed(7, rx_m.at[1, all_m])
    ring_a.start(2, product_m(ring_a, 2, span_a))
    ring_a.rest(2, product_m(ring_a, 2, span_a))
    ring_a.second(2)
    second_hop(3, 5, w_mid_b, span_b, got_of(span_b))
    w_got[:, block(me, piece), span_b] = w_send[:, block(me, piece), span_b]

    ring_p.arrived(0)
    left_here(0, sx_p.at[0, all_p])
    for index in range(N_HID):
        rows = pl.ds(index * ring_p.chunk, ring_p.chunk)
        sx_p[0, rows] = mm_nt(full_p[0, index], weights[2][1 - slot]).astype(BF)
    scatter(8, lambda d: sx_p.at[0, block(d, dp)], lambda m: back_p.at[block(m, dp)])
    back_p[block(me, dp)] = sx_p[0, block(me, dp)]

    unit = lax.broadcasted_iota(jnp.int32, (1, cols_a), 1)
    cover = jnp.where((unit < skip) & (is_src > 0), 0.0, 1.0).astype(F32)
    ring_a.acts(cover)
    ring_a.publish(0)
    ring_a.publish(1)
    ring_a.publish(2)

    blend(5, span_b)
    for q in range(3):
        ring_b.start(q, product_m(ring_b, q, span_b))
    ring_a.forward(0)
    for q in range(3):
        ring_b.rest(q, product_m(ring_b, q, span_b))
    ring_a.forward(1)
    ring_b.second(0)
    ring_b.second(1)
    ring_a.forward(2)
    ring_b.second(2)

    def gradient(left, full, rows, q, store):
        @pl.loop(0, width // 128)
        def _(tile):
            right = full[q].reshape(rows, full.shape[3])
            store(tile, mm_tn(left[:, block(tile, 128)], right).astype(BF))

    def grads_p(q, target):
        def store(tile, value):
            part_p[target, tile] = value

        gradient(rx_p.at[1 if q == 0 else 0], full_p, rows_p, q, store)
        pltpu.make_async_copy(part_p.at[target], out_p.at[target], out_s.at[target]).start()

    halves = pl.ds(0, 2)
    jobs = []

    def put(src, dst):
        copy = pltpu.make_async_copy(src, dst, out_s.at[3 + len(jobs)])
        copy.start()
        jobs.append(copy)

    def grads_m(ring, q, target, base):
        def store(tile, value):
            ring.part[target, lax.div(tile, 2), block(lax.rem(tile, 2), 128)] = value

        gradient(rx_m.at[1 if q == 0 else 0], ring.full, rows_m, q, store)
        put(ring.part.at[target, halves], out_m.at[target, :, :, pl.ds(base, ring.part.shape[3])])

    def grad_hop(ring, sem, base, size, mid):
        def src(d):
            rows = block(lax.rem(d, n // 2), piece)
            return ring.part.at[:, lax.div(d, n // 2), rows, pl.ds(base, size)]

        scatter(sem, src, lambda m: mid.at[m])
        rows = block(lax.rem(me, n // 2), piece)
        mid[me] = ring.part[:, lax.div(me, n // 2), rows, pl.ds(base, size)]

    def far_of(far):
        return lambda m: far.at[:, lax.div(m, n // 2), block(lax.rem(m, n // 2), piece), :]

    def far_own(far, span):
        rows = block(lax.rem(me, n // 2), piece)
        far[:, lax.div(me, n // 2), rows, :] = w_send[:, block(me, piece), span]

    ring_a.sent((0, 1, 2, 3))
    for q, target in ((0, 2), (1, 0), (2, 1)):
        ring_a.arrived(q)
        if q == 1:
            ring_b.acts(None)
            ring_b.publish(0)
            ring_b.publish(1)
            ring_b.publish(2)
        grads_m(ring_a, q, target, 0)
    grad_hop(ring_a, 10, skip, far_a, g_mid_a)
    ring_b.forward(0)
    ring_b.forward(1)
    ring_b.forward(2)
    ring_p.publish(1)
    ring_p.publish(2)
    ring_p.sent((0, 1, 2, 3))
    ring_b.sent((0, 1, 2, 3))
    left_here(6, sx_m.at[0, all_m])
    ring_b.arrived(0)
    grads_m(ring_b, 0, 2, cols_a)
    left_here(4, w_mid_a.at[peers])
    spare_a, spare_b = pl.ds(0, far_a), span_b
    ring_b.arrived(1)
    grads_m(ring_b, 1, 0, cols_a)
    ring_b.arrived(2)
    grads_m(ring_b, 2, 1, cols_a)
    grad_hop(ring_b, 11, 0, cols_b, g_mid_b)
    second_hop(10, 12, g_mid_a, spare_a, far_of(g_far_a))
    far_own(g_far_a, spare_a)
    ring_p.forward(1)

    for index in range(N_HID):
        rows = pl.ds(index * ring_a.chunk, ring_a.chunk)
        value = mm_nt(full_a[0, index], w_keep[2, :, span_a]) + mm_nt(full_b[0, index], w_keep[2, :, span_b])
        sx_m[0, rows] = value.astype(BF)
    scatter(9, lambda d: sx_m.at[0, block(d, dm)], lambda m: back_m.at[block(m, dm)])
    back_m[block(me, dm)] = sx_m[0, block(me, dm)]
    ring_p.forward(2)
    left_here(5, w_mid_b.at[peers])
    second_hop(11, 13, g_mid_b, spare_b, far_of(g_far_b))
    far_own(g_far_b, spare_b)
    grads_p(0, 2)
    ring_p.arrived(1)
    grads_p(1, 0)
    ring_p.arrived(2)
    grads_p(2, 1)

    far_rows = pl.ds(0, n // 2 - 1)
    all_far = g_mid_a.at[peers]
    landed(12, all_far)
    for q in range(3):
        put(g_far_a.at[q], out_m.at[q, :, :, pl.ds(half, far_a)])

    landed(8, back_p.at[all_p])
    landed(9, back_m.at[all_m])
    span_p, span_m = pl.ds(0, rows_p), pl.ds(rows_p, rows_m)
    total = mm(place_hi[:, span_p], back_p[...]) + mm(place_lo[:, span_p], back_p[...])
    total += mm(place_hi[:, span_m], back_m[...]) + mm(place_lo[:, span_m], back_m[...])
    mixed[...] = total.astype(BF)

    landed(13, g_mid_b.at[peers])
    for q in range(3):
        put(g_far_b.at[q], out_m.at[q, :, :, pl.ds(half + far_a, cols_b)])

    left_here(1, sx_p.at[1, all_p])
    left_here(7, sx_m.at[1, all_m])
    left_here(8, sx_p.at[0, all_p])
    left_here(9, sx_m.at[0, all_m])
    left_here(12, g_mid_a.at[peers])
    left_here(13, g_mid_b.at[peers])
    for ring in (ring_p, ring_a, ring_b):
        ring.sent((4, 5, 6, 7))
    for q in range(3):
        pltpu.make_async_copy(part_p.at[q], out_p.at[q], out_s.at[q]).wait()
    for job in jobs:
        job.wait()


def mega(sources, targets, perm, routing, route_w, tokens, cot, gate, up, down, n, depth):
    width, neurons = gate.shape[1], gate.shape[2]
    half = -(-neurons // 256) * 128
    far = neurons - half
    cols_a = (half * 2 // 3) // 128 * 128
    cols_b = half - cols_a
    far_a = far - cols_b
    rows_p, rows_m = n * depth, 2 * n * depth
    piece = width // n
    cp, cm = rows_p // N_HID, rows_m // N_HID
    vmem = pl.BlockSpec(memory_space=pltpu.VMEM)
    smem = pl.BlockSpec(memory_space=pltpu.SMEM)
    hbm = pl.BlockSpec(memory_space=pl.ANY)

    def ring(chunk, cols):
        return [
            pltpu.VMEM((3, N_HID, chunk, cols), BF),
            pltpu.VMEM((3, chunk // 2, cols), BF),
            pltpu.VMEM((3, chunk // 2, cols), BF),
            pltpu.VMEM((3, chunk, cols), BF),
            pltpu.VMEM((3, chunk, cols), BF),
            pltpu.VMEM((3, N_HID, chunk, cols), BF),
        ]

    return pl.pallas_call(
        mega_kernel,
        out_shape=(
            jax.ShapeDtypeStruct(tokens.shape, BF),
            jax.ShapeDtypeStruct((3, width // 128, 128, neurons), BF),
            jax.ShapeDtypeStruct((3, 2, width // 2, neurons), BF),
        ),
        in_specs=[smem] * 2 + [vmem] * 5 + [hbm] * 3,
        out_specs=(vmem, hbm, hbm),
        scratch_shapes=[
            pltpu.SMEM((n,), jnp.int32),
            *[pltpu.VMEM(gate.shape, BF)] * 3,
            *[pltpu.VMEM((tokens.shape[0], rows_p + rows_m), BF)] * 3,
            pltpu.VMEM((neurons, half), BF),
            pltpu.VMEM((2, rows_p, width), BF),
            pltpu.VMEM((2, rows_m, width), BF),
            pltpu.VMEM((2, rows_p, width), BF),
            pltpu.VMEM((2, rows_m, width), BF),
            pltpu.VMEM((3, width, half), BF),
            pltpu.VMEM((n, 3, piece, cols_a), BF),
            pltpu.VMEM((n, 3, piece, cols_b), BF),
            pltpu.VMEM((3, width, half), BF),
            pltpu.VMEM((3, width, half), BF),
            *ring(cp, neurons),
            *ring(cm, cols_a),
            *ring(cm, cols_b),
            pltpu.VMEM((n, 3, piece, far_a), BF),
            pltpu.VMEM((n, 3, piece, cols_b), BF),
            pltpu.VMEM((3, 2, width // 2, far_a), BF),
            pltpu.VMEM((3, 2, width // 2, cols_b), BF),
            pltpu.VMEM((rows_p, width), BF),
            pltpu.VMEM((rows_m, width), BF),
            pltpu.SemaphoreType.DMA((6, 8, 3)),
            pltpu.SemaphoreType.DMA((14,)),
            pltpu.SemaphoreType.DMA((14,)),
            pltpu.SemaphoreType.DMA((3,)),
            pltpu.SemaphoreType.DMA((15,)),
        ],
        compiler_params=pltpu.CompilerParams(
            collective_id=0, has_side_effects=True, vmem_limit_bytes=67_043_328
        ),
    )(sources, targets, perm, routing, route_w, tokens, cot, gate, up, down)


def shards(
    tokens,
    cotangent,
    gate_weight,
    up_weight,
    down_weight,
    routing,
    route_weight,
    merge_source,
    merge_target,
    neuron_perm,
):
    devices_n = lax.axis_size("expert")
    me = lax.axis_index("expert")
    exp_local, width, neurons = gate_weight.shape
    tok_local, top_count = routing.shape
    depth = max(2, tok_local * top_count * 4 // (3 * exp_local * devices_n))
    mixed, grads_p, grads_m = mega(
        merge_source,
        merge_target,
        neuron_perm,
        routing,
        route_weight,
        tokens,
        cotangent,
        gate_weight,
        up_weight,
        down_weight,
        devices_n,
        depth,
    )
    grads_p = grads_p.reshape(3, width, neurons)
    grads_m = grads_m.reshape(3, width, neurons)

    of_source = jnp.where(merge_source // exp_local == me, 2 + merge_source % exp_local, 0)
    of_target = jnp.where(merge_target // exp_local == me, merge_target % exp_local, 0)
    role = jnp.sum(of_source + of_target)
    place = jnp.arange(exp_local, dtype=jnp.int32)[:, None, None]
    is_merge = place == role % 2

    def final(q):
        merged = jnp.where(role >= 2, jnp.zeros((), BF), grads_m[q][None])
        return jnp.where(is_merge, merged, grads_p[q][None])

    return (mixed, final(0), final(1), final(2))


def solution(mesh):
    placed = (
        P("expert", "hidden"),
        P("expert", "hidden"),
        P("expert", "hidden", None),
        P("expert", "hidden", None),
        P("expert", "hidden", None),
        P("expert", None),
        P("expert", None),
        P(),
        P(),
        P(),
    )
    return jax.shard_map(
        shards,
        mesh=mesh,
        in_specs=placed,
        out_specs=(
            P("expert", "hidden"),
            P("expert", "hidden", None),
            P("expert", "hidden", None),
            P("expert", "hidden", None),
        ),
        check_vma=False,
    )
```

time: 251 us -> 238 us (0.948)
  other arithmetic: 17.8 us -> 8.5 us
  local copies, waits for them, and re-layouts: 8.21 us -> 4.87 us
    another operation x4 -> x0, other arithmetic: 5.61 us -> none  [the longest x3 5.6 us: shards(): jnp.stack([jnp.where(first_is_merge, full, plain), jnp.where(first_is_mer...]
    select_n x5 -> x2, other arithmetic: 6 us -> 6.66 us  [the longest x1 3.91 us: final(): return jnp.where(is_merge, merged, grads_p[q][None])]
where the time goes in v4:
time: 238 us
  Pallas kernels  221 us (93%)
  other arithmetic  8.5 us (4%)
  local copies, waits for them, and re-layouts  4.87 us (2%)
  between operations  3.28 us (1%)
    pallas_call x1, Pallas kernels, mega(): pl.pallas_call(mega_kernel, out_shape=(jax.ShapeDtypeStruct(tokens.shape,...  221 us

profile of v4, /device:TPU:1, one launch (start us, length us, event | category | flops | bytes accessed | tf_op | source)
XLA Modules:
  0.0 238.0 jit_solution(3916343419139672873)
XLA Ops:
  0.6 1.3 fusion.2
  4.6 0.5 iota_compare_fusion
  5.1 1.4 copy.14.routing
  6.5 1.4 copy.15.route_w
  7.9 221.3 %shard_map.129 = (bf16[128,512]{1,0:T(8,128)(2,1)}, bf16[3,4,128,1408]{3,2,1,0:T(8,128)(2,1)}, bf16[3,2,256,1408]{3,2,1,0:T(8,128)(2,1)}) custom-call(s32[16]{0:T(128)} %sources.1, s32[16]{0:T(128)} %targets.1, s32[16,1408]{1,0:T(8,128)} %perm_ref.1, s32[128,6]{1,0:T(8,128)} %copy.14.routing, f32[128,6]{1,0:T(8,128)} %copy.15.route_w, ...), custom_call_target="tpu_custom_call" | custom-call | tf_op jit(solution)/shard_map/pallas_call | solution.py:619
  229.3 0.0 slice-start
  229.3 0.0 slice-start.1
  229.3 2.8 %slice_select_fusion = (bf16[1,2,256,1408]{3,2,1,0:T(8,128)(2,1)S(1)}, bf16[1,2,256,1408]{3,2,1,0:T(8,128)(2,1)S(1)}, bf16[1,2,256,1408]{3,2,1,0:T(8,128)(2,1)S(1)}) fusion(bf16[3,2,256,1408]{3,2,1,0:T(8,128)(2,1)} %get-tuple-element.8, pred[]{:T(512)S(6)} %ge.2), kind=kLoop, calls=%fused_computation.3 | loop fusion | flops 2162688 | bytes 8650753 | tf_op jit(solution)/shard_map/jit(_where)/select_n | solution.py:704
  232.0 0.7 slice-done
  232.8 0.0 slice-done.1
  232.8 0.0 copy-start.1
  232.8 0.4 fusion.3
  233.1 0.3 copy-done.1
  233.4 0.0 copy-start
  233.4 3.9 %broadcast_select_fusion = (bf16[2,512,1408]{2,1,0:T(8,128)(2,1)}, bf16[2,512,1408]{2,1,0:T(8,128)(2,1)}, bf16[2,512,1408]{2,1,0:T(8,128)(2,1)}) fusion(pred[2]{0:T(512)(128)(4,1)S(1)} %copy-done.1, bf16[512,1408]{1,0:T(8,128)(2,1)S(1)} %bitcast.9, bf16[512,1408]{1,0:T(8,128)(2,1)S(1)} %bitcast.6, bf16[512,1408]{1,0:T(8,128)(2,1)S(1)} %bitcast.10, ...), kind=kLoop, calls=%fused_computation | loop fusion | flops 4325376 | bytes 17301506 | tf_op jit(solution)/shard_map/jit(_where)/select_n | solution.py:705
  237.3 0.0 copy-done
  237.3 0.7 copy.17
  (1 shorter events, 0.0 us)
Async XLA Ops:
  229.3 3.5 %slice-start = ((s8[4325376]{0:T(1024)(128)(4,1)}), s8[4194304]{0:T(1024)(128)(4,1)S(1)}, s32[]{:S(2)}) async-start(s8[4325376]{0:T(1024)(128)(4,1)} %bitcast.12), calls=%async_computation | async-start | bytes 8388608
  229.3 3.5 %slice-start.1 = ((s8[4325376]{0:T(1024)(128)(4,1)}), s8[131072]{0:T(1024)(128)(4,1)S(1)}, s32[]{:S(2)}) async-start(s8[4325376]{0:T(1024)(128)(4,1)} %bitcast.12), calls=%async_computation.1 | async-start | bytes 262144
  232.8 0.7 copy-start.1
  233.4 3.9 %copy-start = (bf16[128,512]{1,0:T(8,128)(2,1)S(1)}, bf16[128,512]{1,0:T(8,128)(2,1)}, u32[]{:S(2)}) copy-start(bf16[128,512]{1,0:T(8,128)(2,1)} %get-tuple-element.23) | copy-start | bytes 393220

commit v5 on v4

--- a/solution.py
+++ b/solution.py
@@ -9,6 +9,7 @@
 F32 = jnp.float32
 MESH = pl.DeviceIdType.MESH
 N_HID = 4
+BLOCKS = 3
 
 
 def silu_parts(values):
@@ -132,78 +133,45 @@
     up_hbm,
     down_hbm,
     mixed,
+    role,
     out_p,
     out_m,
-    table,
-    gate,
-    up,
-    down,
-    place,
-    place_hi,
-    place_lo,
-    hot,
-    sx_p,
-    sx_m,
-    rx_p,
-    rx_m,
-    w_send,
-    w_mid_a,
-    w_mid_b,
-    w_got,
-    w_keep,
-    part_p,
-    a_p,
-    b_p,
-    l_p,
-    r_p,
-    full_p,
-    part_a,
-    a_a,
-    b_a,
-    l_a,
-    r_a,
-    full_a,
-    part_b,
-    a_b,
-    b_b,
-    l_b,
-    r_b,
-    full_b,
-    g_mid_a,
-    g_mid_b,
-    g_far_a,
-    g_far_b,
-    back_p,
-    back_m,
-    ring_sems,
-    a2a_s,
-    a2a_r,
-    in_s,
-    out_s,
+    *scratch,
 ):
+    scratch = list(scratch)
+
+    def take(count):
+        got = scratch[:count]
+        del scratch[:count]
+        return got
+
+    table, weights, columns, place, place_hi, place_lo, hot, sx_p, sx_m, rx_p, rx_m = take(11)
+    w_send, w_got, w_keep, back_p, back_m = take(5)
+    w_mid, g_mid, g_far = take(BLOCKS), take(BLOCKS), take(BLOCKS)
+    scraps = [take(6) for _ in range(1 + BLOCKS)]
+    ring_sems, a2a_s, a2a_r, in_s, out_s = take(5)
     n = lax.axis_size("expert")
     me = lax.axis_index("expert")
-    weights = (gate, up, down)
     width = tokens.shape[1]
-    tok_n, top = routing.shape
-    neurons = gate.shape[2]
+    top, tok_n = routing.shape
+    neurons = weights.shape[3]
     half = w_keep.shape[2]
     tail = neurons - half
-    cols_a, cols_b = full_a.shape[3], full_b.shape[3]
-    far_a = g_far_a.shape[3]
-    skip = cols_a - far_a
+    cols = half // BLOCKS
+    skip = 2 * half - neurons
     piece = width // n
     rows_p, rows_m = sx_p.shape[1], sx_m.shape[1]
     dp, dm = rows_p // n, rows_m // n
     log_dp = dp.bit_length() - 1
-    span_a, span_b = pl.ds(0, cols_a), pl.ds(cols_a, cols_b)
+    spans = [pl.ds(i * cols, cols) for i in range(BLOCKS)]
+    cut = [skip] + [0] * (BLOCKS - 1)
 
     def block(index, size):
         return pl.ds(pl.multiple_of(index * size, size), size)
 
     loads = []
     for q, ref in enumerate((gate_hbm, up_hbm, down_hbm)):
-        loads.append(pltpu.make_async_copy(ref, weights[q], in_s.at[q]))
+        loads.append(pltpu.make_async_copy(ref, weights.at[q], in_s.at[q]))
         loads[q].start()
 
     def peer(step):
@@ -215,9 +183,9 @@
         lo = lax.rem(lax.rem(node, side) + lax.rem(shift, side), side)
         return (hi * side + lo) * 2 + lax.rem(core + flip, 2)
 
-    ring_p = Ring(part_p, a_p, b_p, l_p, r_p, full_p, ring_sems.at[0], ring_sems.at[1])
-    ring_a = Ring(part_a, a_a, b_a, l_a, r_a, full_a, ring_sems.at[2], ring_sems.at[3])
-    ring_b = Ring(part_b, a_b, b_b, l_b, r_b, full_b, ring_sems.at[4], ring_sems.at[5])
+    rings = [Ring(*scraps[i], ring_sems.at[2 * i], ring_sems.at[2 * i + 1]) for i in range(1 + BLOCKS)]
+    ring_p, blocks = rings[0], rings[1:]
+    part_p, full_p = ring_p.part, ring_p.full
 
     barrier = pltpu.get_barrier_semaphore()
     for other in (ring_p.left, ring_p.right):
@@ -226,6 +194,11 @@
     @pl.loop(1, n)
     def _(step):
         pl.semaphore_signal(barrier, inc=1, device_id={"expert": peer(step)}, device_id_type=MESH)
+
+    columns[...] = jnp.zeros_like(columns)
+    columns[0, 0:top] = routing[...].astype(F32)
+    columns[1, 0:top] = route_w[...]
+    names, shares = jnp.transpose(columns[0]), jnp.transpose(columns[1])
 
     pairs = sources.shape[0]
     wide = rows_p
@@ -255,10 +228,11 @@
         expert = expert[0:1, :]
         chosen = jnp.zeros((tok_n, wide), F32)
         weight = jnp.zeros((tok_n, wide), F32)
+        expert = expert.astype(F32)
         for k in range(top):
-            hit = routing[:, k : k + 1] == expert
+            hit = names[:, k : k + 1] == expert
             chosen = jnp.where(hit, 1.0, chosen)
-            weight = jnp.where(hit, route_w[:, k : k + 1], weight)
+            weight = jnp.where(hit, shares[:, k : k + 1], weight)
         row = lax.broadcasted_iota(jnp.int32, (tok_n, tok_n), 0)
         col = lax.broadcasted_iota(jnp.int32, (tok_n, tok_n), 1)
         before = jnp.where(col < row, 1.0, 0.0).astype(BF)
@@ -322,6 +296,7 @@
         at_s, at_t = lax.shift_right_logical(s, 1) == me, lax.shift_right_logical(t, 1) == me
         slot = jnp.where(at_s, s & 1, jnp.where(at_t, t & 1, slot))
         is_src = jnp.where(at_s, 1, is_src)
+    role[0] = is_src * 2 + slot
 
     def fill_table(device, carry):
         partner = jnp.int32(0)
@@ -342,22 +317,20 @@
     keep_ids = jnp.where(is_src > 0, perm[:, tail:], lane)
 
     def ordered(ids, span, out):
+        units = ids[:, span.start : span.start + span.size]
+
         @pl.loop(0, neurons // 128)
         def _(tile):
-            units = ids[:, span.start : span.start + span.size]
             rows = lax.broadcasted_iota(jnp.int32, (128, span.size), 0) + tile * 128
-            hot[block(tile, 128), span] = jnp.where(rows == units, 1.0, 0.0).astype(BF)
-
-        for q in range(3):
-
-            @pl.loop(0, width // 128)
-            def _(tile):
-                rows = block(tile, 128)
-                out[q, rows, span] = mm(weights[q][slot, rows, :], hot[:, span]).astype(BF)
-
-    def first_hop(sem, span, mid):
-        scatter(sem, lambda d: w_send.at[:, block(d, piece), span], lambda m: mid.at[m])
-        mid[me] = w_send[:, block(me, piece), span]
+            hot[block(tile, 128)] = jnp.where(rows == units, 1.0, 0.0).astype(BF)
+
+        @pl.loop(0, 3)
+        def _(q):
+            out[q, :, span] = mm(weights[q, slot], hot[...]).astype(BF)
+
+    def first_hop(i):
+        scatter(2 + i, lambda d: w_send.at[:, block(d, piece), spans[i]], lambda m: w_mid[i].at[m])
+        w_mid[i][me] = w_send[:, block(me, piece), spans[i]]
 
     def second_hop(first, then, mid, span, dst_of):
         landed(first, mid.at[peers])
@@ -369,222 +342,231 @@
 
         scatter(then, lambda d: w_send.at[:, block(d, piece), span], dst_of)
 
+    def weight_hop(i):
+        second_hop(2 + i, 5 + i, w_mid[i], spans[i], lambda m: w_got.at[:, block(m, piece), spans[i]])
+        w_got[:, block(me, piece), spans[i]] = w_send[:, block(me, piece), spans[i]]
+
     for load in loads:
         load.wait()
-    ordered(send_ids, span_a, w_send)
-    first_hop(2, span_a, w_mid_a)
+    ordered(send_ids, spans[0], w_send)
+    first_hop(0)
     make_place(1)
     make_place(2)
     build_x(rows_p, rows_m, sx_m)
-    dispatch(6, 0, dm, sx_m, rx_m)
+    dispatch(8, 0, dm, sx_m, rx_m)
 
     lefts = (0, 0, 1)
 
     def product_p(q):
         def product(index):
-            return mm(rx_p[lefts[q], block(index, ring_p.chunk), :], weights[q][1 - slot])
+            return mm(rx_p[lefts[q], block(index, ring_p.chunk), :], weights[q, 1 - slot])
 
         return product
 
-    def product_m(ring, q, span):
+    def product_m(i, q):
         def product(index):
-            return mm(rx_m[lefts[q], block(index, ring.chunk), :], w_keep[q, :, span])
+            return mm(rx_m[lefts[q], block(index, blocks[i].chunk), :], w_keep[q, :, spans[i]])
 
         return product
 
     landed(0, rx_p.at[0, all_p])
     ring_p.start(0, product_p(0))
     ring_p.start(1, product_p(1))
+    build_dy(rows_p, rows_m, sx_m)
+    dispatch(9, 1, dm, sx_m, rx_m)
     landed(1, rx_p.at[1, all_p])
     ring_p.start(2, product_p(2))
     ring_p.rest(0, product_p(0))
     ring_p.second(0)
     ring_p.rest(1, product_p(1))
     ring_p.second(1)
+    lax.fori_loop(0, n, fill_table, 0)
+    weight_hop(0)
     ring_p.rest(2, product_p(2))
     ring_p.second(2)
-    lax.fori_loop(0, n, fill_table, 0)
-    build_dy(rows_p, rows_m, sx_m)
-    ordered(send_ids, span_b, w_send)
-
-    got_of = lambda span: lambda m: w_got.at[:, block(m, piece), span]
-    second_hop(2, 4, w_mid_a, span_a, got_of(span_a))
-    w_got[:, block(me, piece), span_a] = w_send[:, block(me, piece), span_a]
-    dispatch(7, 1, dm, sx_m, rx_m)
-    first_hop(3, span_b, w_mid_b)
-    ordered(keep_ids, span_a, w_keep)
-    ordered(keep_ids, span_b, w_keep)
-
-    def blend(sem, span):
-        landed(sem, w_got.at[:, pl.ds(0, (n - 1) * piece), span])
+    for i in range(1, BLOCKS):
+        ordered(send_ids, spans[i], w_send)
+        first_hop(i)
+    for i in range(BLOCKS):
+        ordered(keep_ids, spans[i], w_keep)
+
+    def blend(i):
+        landed(5 + i, w_got.at[:, pl.ds(0, (n - 1) * piece), spans[i]])
+
+        @pl.loop(0, 3 * (width // 128))
+        def _(tile):
+            q, rows = lax.div(tile, width // 128), block(lax.rem(tile, width // 128), 128)
+            both = w_keep[q, rows, spans[i]].astype(F32) + w_got[q, rows, spans[i]].astype(F32)
+            w_keep[q, rows, spans[i]] = (0.5 * both).astype(BF)
+
+    def gradient(left, full, rows, q, store):
+        tile_n = 256
+
+        @pl.loop(0, width // tile_n)
+        def _(tile):
+            right = full[q].reshape(rows, full.shape[3])
+            store(tile, mm_tn(left[:, block(tile, tile_n)], right).astype(BF))
+
+    def grads_p(q, target):
+        def store(tile, value):
+            part_p[target, pl.ds(tile * 2, 2)] = value.reshape(2, 128, neurons)
+
+        gradient(rx_p.at[1 if q == 0 else 0], full_p, rows_p, q, store)
+        pltpu.make_async_copy(part_p.at[target], out_p.at[target], out_s.at[target]).start()
+
+    halves = pl.ds(0, 2)
+    jobs = []
+
+    def put(src, dst):
+        copy = pltpu.make_async_copy(src, dst, out_s.at[3 + len(jobs)])
+        copy.start()
+        jobs.append(copy)
+
+    def grads_m(i, q, target):
+        part = blocks[i].part
+
+        def store(tile, value):
+            part[target, tile] = value
+
+        gradient(rx_m.at[1 if q == 0 else 0], blocks[i].full, rows_m, q, store)
+
+    def grad_hop(i):
+        part, mid = blocks[i].part, g_mid[i]
+        size = pl.ds(cut[i], cols - cut[i])
+
+        def src(d):
+            return part.at[:, lax.div(d, n // 2), block(lax.rem(d, n // 2), piece), size]
+
+        scatter(10 + i, src, lambda m: mid.at[m])
+        mid[me] = part[:, lax.div(me, n // 2), block(lax.rem(me, n // 2), piece), size]
         for q in range(3):
-
-            @pl.loop(0, width // 128)
-            def _(tile):
-                rows = block(tile, 128)
-                both = w_keep[q, rows, span].astype(F32) + w_got[q, rows, span].astype(F32)
-                w_keep[q, rows, span] = (0.5 * both).astype(BF)
+            put(part.at[q, halves], out_m.at[q, :, :, spans[i]])
+
+    def back_hop(i):
+        far, size = g_far[i], pl.ds(i * cols, cols - cut[i])
+        left_here(5 + i, w_mid[i].at[peers])
+
+        def dst(m):
+            return far.at[:, lax.div(m, n // 2), block(lax.rem(m, n // 2), piece), :]
+
+        second_hop(10 + i, 13 + i, g_mid[i], size, dst)
+        rows = block(lax.rem(me, n // 2), piece)
+        far[:, lax.div(me, n // 2), rows, :] = w_send[:, block(me, piece), size]
+
+    unit = lax.broadcasted_iota(jnp.int32, (1, cols), 1)
+    cover = jnp.where((unit < skip) & (is_src > 0), 0.0, 1.0).astype(F32)
+
+    def mix_outputs():
+        landed(16, back_p.at[all_p])
+        landed(17, back_m.at[all_m])
+        span_p, span_m = pl.ds(0, rows_p), pl.ds(rows_p, rows_m)
+        total = mm(place_hi[:, span_p], back_p[...]) + mm(place_lo[:, span_p], back_p[...])
+        total += mm(place_hi[:, span_m], back_m[...]) + mm(place_lo[:, span_m], back_m[...])
+        mixed[...] = total.astype(BF)
+
+    def enter(i):
+        blend(i)
+        for q in range(3):
+            blocks[i].start(q, product_m(i, q))
+
+    def rest(i):
+        for q in range(3):
+            blocks[i].rest(q, product_m(i, q))
+
+    def seconds(i):
+        for q in range(3):
+            blocks[i].second(q)
+
+    def publish(i):
+        blocks[i].acts(cover if i == 0 else None)
+        for q in range(3):
+            blocks[i].publish(q)
+
+    def forwards(i):
+        for q in range(3):
+            blocks[i].forward(q)
+
+    def leave(i):
+        blocks[i].sent((0, 1, 2, 3))
+        for q, target in ((0, 2), (1, 0), (2, 1)):
+            blocks[i].arrived(q)
+            grads_m(i, q, target)
+        grad_hop(i)
 
     ring_p.acts(None)
+    landed(8, rx_m.at[0, all_m])
+    landed(9, rx_m.at[1, all_m])
+    enter(0)
     ring_p.publish(0)
-    landed(6, rx_m.at[0, all_m])
-    blend(4, span_a)
-    for q in range(2):
-        ring_a.start(q, product_m(ring_a, q, span_a))
-    for q in range(2):
-        ring_a.rest(q, product_m(ring_a, q, span_a))
-    ring_a.second(0)
-    ring_a.second(1)
+    rest(0)
+    seconds(0)
+    weight_hop(1)
     ring_p.forward(0)
-    landed(7, rx_m.at[1, all_m])
-    ring_a.start(2, product_m(ring_a, 2, span_a))
-    ring_a.rest(2, product_m(ring_a, 2, span_a))
-    ring_a.second(2)
-    second_hop(3, 5, w_mid_b, span_b, got_of(span_b))
-    w_got[:, block(me, piece), span_b] = w_send[:, block(me, piece), span_b]
+    weight_hop(2)
+    enter(1)
+    rest(1)
+    publish(0)
+    seconds(1)
+    forwards(0)
 
     ring_p.arrived(0)
     left_here(0, sx_p.at[0, all_p])
     for index in range(N_HID):
         rows = pl.ds(index * ring_p.chunk, ring_p.chunk)
-        sx_p[0, rows] = mm_nt(full_p[0, index], weights[2][1 - slot]).astype(BF)
-    scatter(8, lambda d: sx_p.at[0, block(d, dp)], lambda m: back_p.at[block(m, dp)])
+        sx_p[0, rows] = mm_nt(full_p[0, index], weights[2, 1 - slot]).astype(BF)
+    scatter(16, lambda d: sx_p.at[0, block(d, dp)], lambda m: back_p.at[block(m, dp)])
     back_p[block(me, dp)] = sx_p[0, block(me, dp)]
 
-    unit = lax.broadcasted_iota(jnp.int32, (1, cols_a), 1)
-    cover = jnp.where((unit < skip) & (is_src > 0), 0.0, 1.0).astype(F32)
-    ring_a.acts(cover)
-    ring_a.publish(0)
-    ring_a.publish(1)
-    ring_a.publish(2)
-
-    blend(5, span_b)
-    for q in range(3):
-        ring_b.start(q, product_m(ring_b, q, span_b))
-    ring_a.forward(0)
-    for q in range(3):
-        ring_b.rest(q, product_m(ring_b, q, span_b))
-    ring_a.forward(1)
-    ring_b.second(0)
-    ring_b.second(1)
-    ring_a.forward(2)
-    ring_b.second(2)
-
-    def gradient(left, full, rows, q, store):
-        @pl.loop(0, width // 128)
-        def _(tile):
-            right = full[q].reshape(rows, full.shape[3])
-            store(tile, mm_tn(left[:, block(tile, 128)], right).astype(BF))
-
-    def grads_p(q, target):
-        def store(tile, value):
-            part_p[target, tile] = value
-
-        gradient(rx_p.at[1 if q == 0 else 0], full_p, rows_p, q, store)
-        pltpu.make_async_copy(part_p.at[target], out_p.at[target], out_s.at[target]).start()
-
-    halves = pl.ds(0, 2)
-    jobs = []
-
-    def put(src, dst):
-        copy = pltpu.make_async_copy(src, dst, out_s.at[3 + len(jobs)])
-        copy.start()
-        jobs.append(copy)
-
-    def grads_m(ring, q, target, base):
-        def store(tile, value):
-            ring.part[target, lax.div(tile, 2), block(lax.rem(tile, 2), 128)] = value
-
-        gradient(rx_m.at[1 if q == 0 else 0], ring.full, rows_m, q, store)
-        put(ring.part.at[target, halves], out_m.at[target, :, :, pl.ds(base, ring.part.shape[3])])
-
-    def grad_hop(ring, sem, base, size, mid):
-        def src(d):
-            rows = block(lax.rem(d, n // 2), piece)
-            return ring.part.at[:, lax.div(d, n // 2), rows, pl.ds(base, size)]
-
-        scatter(sem, src, lambda m: mid.at[m])
-        rows = block(lax.rem(me, n // 2), piece)
-        mid[me] = ring.part[:, lax.div(me, n // 2), rows, pl.ds(base, size)]
-
-    def far_of(far):
-        return lambda m: far.at[:, lax.div(m, n // 2), block(lax.rem(m, n // 2), piece), :]
-
-    def far_own(far, span):
-        rows = block(lax.rem(me, n // 2), piece)
-        far[:, lax.div(me, n // 2), rows, :] = w_send[:, block(me, piece), span]
-
-    ring_a.sent((0, 1, 2, 3))
-    for q, target in ((0, 2), (1, 0), (2, 1)):
-        ring_a.arrived(q)
-        if q == 1:
-            ring_b.acts(None)
-            ring_b.publish(0)
-            ring_b.publish(1)
-            ring_b.publish(2)
-        grads_m(ring_a, q, target, 0)
-    grad_hop(ring_a, 10, skip, far_a, g_mid_a)
-    ring_b.forward(0)
-    ring_b.forward(1)
-    ring_b.forward(2)
+    enter(2)
+    rest(2)
+    publish(1)
+    seconds(2)
+    leave(0)
+    forwards(1)
+    back_hop(0)
+    publish(2)
+    leave(1)
+    forwards(2)
     ring_p.publish(1)
     ring_p.publish(2)
     ring_p.sent((0, 1, 2, 3))
-    ring_b.sent((0, 1, 2, 3))
-    left_here(6, sx_m.at[0, all_m])
-    ring_b.arrived(0)
-    grads_m(ring_b, 0, 2, cols_a)
-    left_here(4, w_mid_a.at[peers])
-    spare_a, spare_b = pl.ds(0, far_a), span_b
-    ring_b.arrived(1)
-    grads_m(ring_b, 1, 0, cols_a)
-    ring_b.arrived(2)
-    grads_m(ring_b, 2, 1, cols_a)
-    grad_hop(ring_b, 11, 0, cols_b, g_mid_b)
-    second_hop(10, 12, g_mid_a, spare_a, far_of(g_far_a))
-    far_own(g_far_a, spare_a)
+    left_here(8, sx_m.at[0, all_m])
+    back_hop(1)
+    leave(2)
     ring_p.forward(1)
 
     for index in range(N_HID):
-        rows = pl.ds(index * ring_a.chunk, ring_a.chunk)
-        value = mm_nt(full_a[0, index], w_keep[2, :, span_a]) + mm_nt(full_b[0, index], w_keep[2, :, span_b])
+        rows = pl.ds(index * blocks[0].chunk, blocks[0].chunk)
+        value = mm_nt(blocks[0].full[0, index], w_keep[2, :, spans[0]])
+        for i in range(1, BLOCKS):
+            value += mm_nt(blocks[i].full[0, index], w_keep[2, :, spans[i]])
         sx_m[0, rows] = value.astype(BF)
-    scatter(9, lambda d: sx_m.at[0, block(d, dm)], lambda m: back_m.at[block(m, dm)])
+    scatter(17, lambda d: sx_m.at[0, block(d, dm)], lambda m: back_m.at[block(m, dm)])
     back_m[block(me, dm)] = sx_m[0, block(me, dm)]
     ring_p.forward(2)
-    left_here(5, w_mid_b.at[peers])
-    second_hop(11, 13, g_mid_b, spare_b, far_of(g_far_b))
-    far_own(g_far_b, spare_b)
+    back_hop(2)
     grads_p(0, 2)
     ring_p.arrived(1)
     grads_p(1, 0)
     ring_p.arrived(2)
     grads_p(2, 1)
 
-    far_rows = pl.ds(0, n // 2 - 1)
-    all_far = g_mid_a.at[peers]
-    landed(12, all_far)
-    for q in range(3):
-        put(g_far_a.at[q], out_m.at[q, :, :, pl.ds(half, far_a)])
-
-    landed(8, back_p.at[all_p])
-    landed(9, back_m.at[all_m])
-    span_p, span_m = pl.ds(0, rows_p), pl.ds(rows_p, rows_m)
-    total = mm(place_hi[:, span_p], back_p[...]) + mm(place_lo[:, span_p], back_p[...])
-    total += mm(place_hi[:, span_m], back_m[...]) + mm(place_lo[:, span_m], back_m[...])
-    mixed[...] = total.astype(BF)
-
-    landed(13, g_mid_b.at[peers])
-    for q in range(3):
-        put(g_far_b.at[q], out_m.at[q, :, :, pl.ds(half + far_a, cols_b)])
+    base = half
+    for i in range(BLOCKS):
+        if i == BLOCKS - 1:
+            mix_outputs()
+        landed(13 + i, g_mid[i].at[peers])
+        for q in range(3):
+            put(g_far[i].at[q], out_m.at[q, :, :, pl.ds(base, cols - cut[i])])
+        base += cols - cut[i]
 
     left_here(1, sx_p.at[1, all_p])
-    left_here(7, sx_m.at[1, all_m])
-    left_here(8, sx_p.at[0, all_p])
-    left_here(9, sx_m.at[0, all_m])
-    left_here(12, g_mid_a.at[peers])
-    left_here(13, g_mid_b.at[peers])
-    for ring in (ring_p, ring_a, ring_b):
+    left_here(9, sx_m.at[1, all_m])
+    left_here(16, sx_p.at[0, all_p])
+    left_here(17, sx_m.at[0, all_m])
+    for i in range(BLOCKS):
+        left_here(13 + i, g_mid[i].at[peers])
+    for ring in rings:
         ring.sent((4, 5, 6, 7))
     for q in range(3):
         pltpu.make_async_copy(part_p.at[q], out_p.at[q], out_s.at[q]).wait()
@@ -596,9 +578,8 @@
     width, neurons = gate.shape[1], gate.shape[2]
     half = -(-neurons // 256) * 128
     far = neurons - half
-    cols_a = (half * 2 // 3) // 128 * 128
-    cols_b = half - cols_a
-    far_a = far - cols_b
+    cols = half // BLOCKS
+    fars = [far - (BLOCKS - 1) * cols] + [cols] * (BLOCKS - 1)
     rows_p, rows_m = n * depth, 2 * n * depth
     piece = width // n
     cp, cm = rows_p // N_HID, rows_m // N_HID
@@ -620,39 +601,35 @@
         mega_kernel,
         out_shape=(
             jax.ShapeDtypeStruct(tokens.shape, BF),
+            jax.ShapeDtypeStruct((1,), jnp.int32),
             jax.ShapeDtypeStruct((3, width // 128, 128, neurons), BF),
             jax.ShapeDtypeStruct((3, 2, width // 2, neurons), BF),
         ),
         in_specs=[smem] * 2 + [vmem] * 5 + [hbm] * 3,
-        out_specs=(vmem, hbm, hbm),
+        out_specs=(vmem, smem, hbm, hbm),
         scratch_shapes=[
             pltpu.SMEM((n,), jnp.int32),
-            *[pltpu.VMEM(gate.shape, BF)] * 3,
+            pltpu.VMEM((3, *gate.shape), BF),
+            pltpu.VMEM((2, 8, tokens.shape[0]), F32),
             *[pltpu.VMEM((tokens.shape[0], rows_p + rows_m), BF)] * 3,
-            pltpu.VMEM((neurons, half), BF),
+            pltpu.VMEM((neurons, cols), BF),
             pltpu.VMEM((2, rows_p, width), BF),
             pltpu.VMEM((2, rows_m, width), BF),
             pltpu.VMEM((2, rows_p, width), BF),
             pltpu.VMEM((2, rows_m, width), BF),
-            pltpu.VMEM((3, width, half), BF),
-            pltpu.VMEM((n, 3, piece, cols_a), BF),
-            pltpu.VMEM((n, 3, piece, cols_b), BF),
-            pltpu.VMEM((3, width, half), BF),
-            pltpu.VMEM((3, width, half), BF),
-            *ring(cp, neurons),
-            *ring(cm, cols_a),
-            *ring(cm, cols_b),
-            pltpu.VMEM((n, 3, piece, far_a), BF),
-            pltpu.VMEM((n, 3, piece, cols_b), BF),
-            pltpu.VMEM((3, 2, width // 2, far_a), BF),
-            pltpu.VMEM((3, 2, width // 2, cols_b), BF),
+            *[pltpu.VMEM((3, width, half), BF)] * 3,
             pltpu.VMEM((rows_p, width), BF),
             pltpu.VMEM((rows_m, width), BF),
-            pltpu.SemaphoreType.DMA((6, 8, 3)),
-            pltpu.SemaphoreType.DMA((14,)),
-            pltpu.SemaphoreType.DMA((14,)),
+            *[pltpu.VMEM((n, 3, piece, cols), BF)] * BLOCKS,
+            *[pltpu.VMEM((n, 3, piece, size), BF) for size in fars],
+            *[pltpu.VMEM((3, 2, width // 2, size), BF) for size in fars],
+            *ring(cp, neurons),
+            *(ring(cm, cols) * BLOCKS),
+            pltpu.SemaphoreType.DMA((2 + 2 * BLOCKS, 8, 3)),
+            pltpu.SemaphoreType.DMA((18,)),
+            pltpu.SemaphoreType.DMA((18,)),
             pltpu.SemaphoreType.DMA((3,)),
-            pltpu.SemaphoreType.DMA((15,)),
+            pltpu.SemaphoreType.DMA((3 + 6 * BLOCKS,)),
         ],
         compiler_params=pltpu.CompilerParams(
             collective_id=0, has_side_effects=True, vmem_limit_bytes=67_043_328
@@ -673,16 +650,15 @@
     neuron_perm,
 ):
     devices_n = lax.axis_size("expert")
-    me = lax.axis_index("expert")
     exp_local, width, neurons = gate_weight.shape
     tok_local, top_count = routing.shape
     depth = max(2, tok_local * top_count * 4 // (3 * exp_local * devices_n))
-    mixed, grads_p, grads_m = mega(
+    mixed, role, grads_p, grads_m = mega(
         merge_source,
         merge_target,
         neuron_perm,
-        routing,
-        route_weight,
+        routing.T,
+        route_weight.T,
         tokens,
         cotangent,
         gate_weight,
@@ -694,9 +670,7 @@
     grads_p = grads_p.reshape(3, width, neurons)
     grads_m = grads_m.reshape(3, width, neurons)
 
-    of_source = jnp.where(merge_source // exp_local == me, 2 + merge_source % exp_local, 0)
-    of_target = jnp.where(merge_target // exp_local == me, merge_target % exp_local, 0)
-    role = jnp.sum(of_source + of_target)
+    role = role[0]
     place = jnp.arange(exp_local, dtype=jnp.int32)[:, None, None]
     is_merge = place == role % 2
 

time: 238 us -> 217 us (0.912)
  Pallas kernels: 221 us -> 205 us
  local copies, waits for them, and re-layouts: 4.87 us -> 1.74 us
    pallas_call x1, Pallas kernels: 221 us -> 205 us  [mega(): pl.pallas_call(mega_kernel, out_shape=(jax.ShapeDtypeStruct(tokens.shape,...]
    unnamed x11 -> x7, local copies, waits for them, and re-layouts: 4.51 us -> 1.38 us
where the time goes in v5:
time: 217 us
  Pallas kernels  205 us (94%)
  other arithmetic  6.69 us (3%)
  between operations  3.2 us (1%)
    pallas_call x1, Pallas kernels, mega(): pl.pallas_call(mega_kernel, out_shape=(jax.ShapeDtypeStruct(tokens.shape,...  205 us

profile of v5, /device:TPU:1, one launch (start us, length us, event | category | flops | bytes accessed | tf_op | source)
XLA Modules:
  0.0 216.9 jit_solution(16690807354116562722)
XLA Ops:
  0.6 205.3 %shard_map.129 = (bf16[128,512]{1,0:T(8,128)(2,1)}, s32[1]{0:T(128)}, bf16[3,4,128,1408]{3,2,1,0:T(8,128)(2,1)}, bf16[3,2,256,1408]{3,2,1,0:T(8,128)(2,1)}) custom-call(s32[16]{0:T(128)} %sources.1, s32[16]{0:T(128)} %targets.1, s32[16,1408]{1,0:T(8,128)} %perm_ref.1, s32[6,128]{1,0:T(8,128)} %bitcast.17, f32[6,128]{1,0:T(8,128)} %bitcast.18, ...), custom_call_target="tpu_custom_call" | custom-call | tf_op jit(solution)/shard_map/pallas_call | solution.py:600
  208.5 0.0 slice-start
  208.5 0.0 slice-start.1
  208.5 2.8 %slice_select_fusion = (bf16[1,2,256,1408]{3,2,1,0:T(8,128)(2,1)S(1)}, bf16[1,2,256,1408]{3,2,1,0:T(8,128)(2,1)S(1)}, bf16[1,2,256,1408]{3,2,1,0:T(8,128)(2,1)S(1)}) fusion(bf16[3,2,256,1408]{3,2,1,0:T(8,128)(2,1)} %get-tuple-element.10, pred[]{:T(512)S(6)} %ge.2), kind=kLoop, calls=%fused_computation.3 | loop fusion | flops 2162688 | bytes 8650753 | tf_op jit(solution)/shard_map/jit(_where)/select_n | solution.py:678
  211.3 0.7 slice-done
  212.0 0.0 slice-done.1
  212.0 0.4 fusion
  212.3 0.0 copy-start
  212.4 3.9 %broadcast_select_fusion = (bf16[2,512,1408]{2,1,0:T(8,128)(2,1)}, bf16[2,512,1408]{2,1,0:T(8,128)(2,1)}, bf16[2,512,1408]{2,1,0:T(8,128)(2,1)}) fusion(pred[2]{0:T(512)(128)(4,1)S(1)} %iota_compare_fusion, bf16[512,1408]{1,0:T(8,128)(2,1)S(1)} %bitcast.12, bf16[512,1408]{1,0:T(8,128)(2,1)S(1)} %bitcast.9, bf16[512,1408]{1,0:T(8,128)(2,1)S(1)} %bitcast.13, ...), kind=kLoop, calls=%fused_computation | loop fusion | flops 4325376 | bytes 17301506 | tf_op jit(solution)/shard_map/jit(_where)/select_n | solution.py:679
  216.3 0.0 copy-done
  216.3 0.7 copy.15
  (2 shorter events, 0.0 us)
Async XLA Ops:
  208.5 3.5 %slice-start = ((s8[4325376]{0:T(1024)(128)(4,1)}), s8[4194304]{0:T(1024)(128)(4,1)S(1)}, s32[]{:S(2)}) async-start(s8[4325376]{0:T(1024)(128)(4,1)} %bitcast.15), calls=%async_computation | async-start | bytes 8388608
  208.5 3.5 %slice-start.1 = ((s8[4325376]{0:T(1024)(128)(4,1)}), s8[131072]{0:T(1024)(128)(4,1)S(1)}, s32[]{:S(2)}) async-start(s8[4325376]{0:T(1024)(128)(4,1)} %bitcast.15), calls=%async_computation.1 | async-start | bytes 262144
  212.3 3.9 %copy-start = (bf16[128,512]{1,0:T(8,128)(2,1)S(1)}, bf16[128,512]{1,0:T(8,128)(2,1)}, u32[]{:S(2)}) copy-start(bf16[128,512]{1,0:T(8,128)(2,1)} %get-tuple-element.25) | copy-start | bytes 393220

commit v6 on v5

--- a/solution.py
+++ b/solution.py
@@ -45,6 +45,7 @@
         self.lo = pl.ds(0, self.chunk // 2)
         self.hi = pl.ds(self.chunk // 2, self.chunk // 2)
         self.copies = {}
+        self.seen = set()
 
     def send(self, src, dst, kind, q, peer):
         copy = pltpu.make_async_remote_copy(
@@ -112,8 +113,10 @@
         self.send(half, half, 7, q, self.left)
 
     def arrived(self, q):
-        self.copies[6, q].wait_recv()
-        self.copies[7, q].wait_recv()
+        for kind in (6, 7):
+            if (kind, q) not in self.seen:
+                self.seen.add((kind, q))
+                self.copies[kind, q].wait_recv()
 
     def sent(self, kinds):
         for kind in kinds:
@@ -163,8 +166,8 @@
     rows_p, rows_m = sx_p.shape[1], sx_m.shape[1]
     dp, dm = rows_p // n, rows_m // n
     log_dp = dp.bit_length() - 1
-    spans = [pl.ds(i * cols, cols) for i in range(BLOCKS)]
-    cut = [skip] + [0] * (BLOCKS - 1)
+    spans = [pl.ds((i + 1) % BLOCKS * cols, cols) for i in range(BLOCKS)]
+    cut = [0] * (BLOCKS - 1) + [skip]
 
     def block(index, size):
         return pl.ds(pl.multiple_of(index * size, size), size)
@@ -373,7 +376,6 @@
     ring_p.start(0, product_p(0))
     ring_p.start(1, product_p(1))
     build_dy(rows_p, rows_m, sx_m)
-    dispatch(9, 1, dm, sx_m, rx_m)
     landed(1, rx_p.at[1, all_p])
     ring_p.start(2, product_p(2))
     ring_p.rest(0, product_p(0))
@@ -382,6 +384,7 @@
     ring_p.second(1)
     lax.fori_loop(0, n, fill_table, 0)
     weight_hop(0)
+    dispatch(9, 1, dm, sx_m, rx_m)
     ring_p.rest(2, product_p(2))
     ring_p.second(2)
     for i in range(1, BLOCKS):
@@ -443,7 +446,7 @@
             put(part.at[q, halves], out_m.at[q, :, :, spans[i]])
 
     def back_hop(i):
-        far, size = g_far[i], pl.ds(i * cols, cols - cut[i])
+        far, size = g_far[i], pl.ds(spans[i].start, cols - cut[i])
         left_here(5 + i, w_mid[i].at[peers])
 
         def dst(m):
@@ -478,7 +481,7 @@
             blocks[i].second(q)
 
     def publish(i):
-        blocks[i].acts(cover if i == 0 else None)
+        blocks[i].acts(cover if cut[i] else None)
         for q in range(3):
             blocks[i].publish(q)
 
@@ -493,72 +496,82 @@
             grads_m(i, q, target)
         grad_hop(i)
 
+    def outputs_p():
+        ring_p.arrived(0)
+        left_here(0, sx_p.at[0, all_p])
+        for index in range(N_HID):
+            rows = pl.ds(index * ring_p.chunk, ring_p.chunk)
+            sx_p[0, rows] = mm_nt(full_p[0, index], weights[2, 1 - slot]).astype(BF)
+        scatter(16, lambda d: sx_p.at[0, block(d, dp)], lambda m: back_p.at[block(m, dp)])
+        back_p[block(me, dp)] = sx_p[0, block(me, dp)]
+
+    def outputs_m():
+        for i in range(BLOCKS):
+            blocks[i].arrived(0)
+        left_here(8, sx_m.at[0, all_m])
+        for index in range(N_HID):
+            rows = pl.ds(index * blocks[0].chunk, blocks[0].chunk)
+            value = mm_nt(blocks[0].full[0, index], w_keep[2, :, spans[0]])
+            for i in range(1, BLOCKS):
+                value += mm_nt(blocks[i].full[0, index], w_keep[2, :, spans[i]])
+            sx_m[0, rows] = value.astype(BF)
+        scatter(17, lambda d: sx_m.at[0, block(d, dm)], lambda m: back_m.at[block(m, dm)])
+        back_m[block(me, dm)] = sx_m[0, block(me, dm)]
+
+    landed(8, rx_m.at[0, all_m])
+    blend(0)
+    blocks[0].start(0, product_m(0, 0))
+    blocks[0].start(1, product_m(0, 1))
     ring_p.acts(None)
-    landed(8, rx_m.at[0, all_m])
+    ring_p.publish(0)
+    blocks[0].rest(0, product_m(0, 0))
+    blocks[0].second(0)
+    blocks[0].rest(1, product_m(0, 1))
+    blocks[0].second(1)
     landed(9, rx_m.at[1, all_m])
-    enter(0)
-    ring_p.publish(0)
-    rest(0)
-    seconds(0)
+    blocks[0].start(2, product_m(0, 2))
+    blocks[0].rest(2, product_m(0, 2))
     weight_hop(1)
+    blocks[0].second(2)
     ring_p.forward(0)
+    publish(0)
     weight_hop(2)
     enter(1)
     rest(1)
-    publish(0)
+    forwards(0)
+    outputs_p()
+    enter(2)
     seconds(1)
-    forwards(0)
-
-    ring_p.arrived(0)
-    left_here(0, sx_p.at[0, all_p])
-    for index in range(N_HID):
-        rows = pl.ds(index * ring_p.chunk, ring_p.chunk)
-        sx_p[0, rows] = mm_nt(full_p[0, index], weights[2, 1 - slot]).astype(BF)
-    scatter(16, lambda d: sx_p.at[0, block(d, dp)], lambda m: back_p.at[block(m, dp)])
-    back_p[block(me, dp)] = sx_p[0, block(me, dp)]
-
-    enter(2)
     rest(2)
+    leave(0)
     publish(1)
     seconds(2)
-    leave(0)
+    back_hop(0)
     forwards(1)
-    back_hop(0)
     publish(2)
     leave(1)
     forwards(2)
     ring_p.publish(1)
     ring_p.publish(2)
     ring_p.sent((0, 1, 2, 3))
-    left_here(8, sx_m.at[0, all_m])
+    leave(2)
     back_hop(1)
-    leave(2)
+    outputs_m()
     ring_p.forward(1)
-
-    for index in range(N_HID):
-        rows = pl.ds(index * blocks[0].chunk, blocks[0].chunk)
-        value = mm_nt(blocks[0].full[0, index], w_keep[2, :, spans[0]])
-        for i in range(1, BLOCKS):
-            value += mm_nt(blocks[i].full[0, index], w_keep[2, :, spans[i]])
-        sx_m[0, rows] = value.astype(BF)
-    scatter(17, lambda d: sx_m.at[0, block(d, dm)], lambda m: back_m.at[block(m, dm)])
-    back_m[block(me, dm)] = sx_m[0, block(me, dm)]
+    back_hop(2)
     ring_p.forward(2)
-    back_hop(2)
     grads_p(0, 2)
     ring_p.arrived(1)
     grads_p(1, 0)
     ring_p.arrived(2)
     grads_p(2, 1)
 
-    base = half
     for i in range(BLOCKS):
         if i == BLOCKS - 1:
             mix_outputs()
         landed(13 + i, g_mid[i].at[peers])
         for q in range(3):
-            put(g_far[i].at[q], out_m.at[q, :, :, pl.ds(base, cols - cut[i])])
-        base += cols - cut[i]
+            put(g_far[i].at[q], out_m.at[q, :, :, pl.ds(tail + spans[i].start + cut[i], cols - cut[i])])
 
     left_here(1, sx_p.at[1, all_p])
     left_here(9, sx_m.at[1, all_m])
@@ -579,7 +592,7 @@
     half = -(-neurons // 256) * 128
     far = neurons - half
     cols = half // BLOCKS
-    fars = [far - (BLOCKS - 1) * cols] + [cols] * (BLOCKS - 1)
+    fars = [cols] * (BLOCKS - 1) + [far - (BLOCKS - 1) * cols]
     rows_p, rows_m = n * depth, 2 * n * depth
     piece = width // n
     cp, cm = rows_p // N_HID, rows_m // N_HID

time: 217 us -> 204 us (0.940)
  Pallas kernels: 205 us -> 192 us
    pallas_call x1, Pallas kernels: 205 us -> 192 us  [mega(): pl.pallas_call(mega_kernel, out_shape=(jax.ShapeDtypeStruct(tokens.shape,...]
where the time goes in v6:
time: 204 us
  Pallas kernels  192 us (94%)
  other arithmetic  6.69 us (3%)
  between operations  3.2 us (2%)
    pallas_call x1, Pallas kernels, mega(): pl.pallas_call(mega_kernel, out_shape=(jax.ShapeDtypeStruct(tokens.shape,...  192 us

profile of v6, /device:TPU:1, one launch (start us, length us, event | category | flops | bytes accessed | tf_op | source)
XLA Modules:
  0.0 203.6 jit_solution(10530396398309476060)
XLA Ops:
  0.6 191.9 %shard_map.129 = (bf16[128,512]{1,0:T(8,128)(2,1)}, s32[1]{0:T(128)}, bf16[3,4,128,1408]{3,2,1,0:T(8,128)(2,1)}, bf16[3,2,256,1408]{3,2,1,0:T(8,128)(2,1)}) custom-call(s32[16]{0:T(128)} %sources.1, s32[16]{0:T(128)} %targets.1, s32[16,1408]{1,0:T(8,128)} %perm_ref.1, s32[6,128]{1,0:T(8,128)} %bitcast.17, f32[6,128]{1,0:T(8,128)} %bitcast.18, ...), custom_call_target="tpu_custom_call" | custom-call | tf_op jit(solution)/shard_map/pallas_call | solution.py:613
  195.1 0.0 slice-start
  195.1 0.0 slice-start.1
  195.1 2.8 %slice_select_fusion = (bf16[1,2,256,1408]{3,2,1,0:T(8,128)(2,1)S(1)}, bf16[1,2,256,1408]{3,2,1,0:T(8,128)(2,1)S(1)}, bf16[1,2,256,1408]{3,2,1,0:T(8,128)(2,1)S(1)}) fusion(bf16[3,2,256,1408]{3,2,1,0:T(8,128)(2,1)} %get-tuple-element.10, pred[]{:T(512)S(6)} %ge.2), kind=kLoop, calls=%fused_computation.3 | loop fusion | flops 2162688 | bytes 8650753 | tf_op jit(solution)/shard_map/jit(_where)/select_n | solution.py:691
  197.9 0.7 slice-done
  198.6 0.0 slice-done.1
  198.6 0.4 fusion
  199.0 0.0 copy-start
  199.0 3.9 %broadcast_select_fusion = (bf16[2,512,1408]{2,1,0:T(8,128)(2,1)}, bf16[2,512,1408]{2,1,0:T(8,128)(2,1)}, bf16[2,512,1408]{2,1,0:T(8,128)(2,1)}) fusion(pred[2]{0:T(512)(128)(4,1)S(1)} %iota_compare_fusion, bf16[512,1408]{1,0:T(8,128)(2,1)S(1)} %bitcast.12, bf16[512,1408]{1,0:T(8,128)(2,1)S(1)} %bitcast.9, bf16[512,1408]{1,0:T(8,128)(2,1)S(1)} %bitcast.13, ...), kind=kLoop, calls=%fused_computation | loop fusion | flops 4325376 | bytes 17301506 | tf_op jit(solution)/shard_map/jit(_where)/select_n | solution.py:692
  202.9 0.0 copy-done
  202.9 0.7 copy.15
  (2 shorter events, 0.0 us)
Async XLA Ops:
  195.1 3.5 %slice-start = ((s8[4325376]{0:T(1024)(128)(4,1)}), s8[4194304]{0:T(1024)(128)(4,1)S(1)}, s32[]{:S(2)}) async-start(s8[4325376]{0:T(1024)(128)(4,1)} %bitcast.15), calls=%async_computation | async-start | bytes 8388608
  195.1 3.5 %slice-start.1 = ((s8[4325376]{0:T(1024)(128)(4,1)}), s8[131072]{0:T(1024)(128)(4,1)S(1)}, s32[]{:S(2)}) async-start(s8[4325376]{0:T(1024)(128)(4,1)} %bitcast.15), calls=%async_computation.1 | async-start | bytes 262144
  199.0 3.9 %copy-start = (bf16[128,512]{1,0:T(8,128)(2,1)S(1)}, bf16[128,512]{1,0:T(8,128)(2,1)}, u32[]{:S(2)}) copy-start(bf16[128,512]{1,0:T(8,128)(2,1)} %get-tuple-element.25) | copy-start | bytes 393220

commit v7 on v6

--- a/solution.py
+++ b/solution.py
@@ -136,12 +136,10 @@
     up_hbm,
     down_hbm,
     mixed,
-    role,
-    out_p,
-    out_m,
-    *scratch,
+    marks,
+    *rest_refs,
 ):
-    scratch = list(scratch)
+    out_p, out_m, scratch = rest_refs[:3], rest_refs[3:6], list(rest_refs[6:])
 
     def take(count):
         got = scratch[:count]
@@ -264,7 +262,7 @@
     def scatter(sem, src_of, dst_of):
         @pl.loop(1, n)
         def _(step):
-            other = peer(step)
+            other = peer(lax.rem(step * 5, n))
             pltpu.make_async_remote_copy(
                 src_ref=src_of(other),
                 dst_ref=dst_of(me),
@@ -299,7 +297,8 @@
         at_s, at_t = lax.shift_right_logical(s, 1) == me, lax.shift_right_logical(t, 1) == me
         slot = jnp.where(at_s, s & 1, jnp.where(at_t, t & 1, slot))
         is_src = jnp.where(at_s, 1, is_src)
-    role[0] = is_src * 2 + slot
+    marks[0:8, :] = jnp.zeros((8, neurons), jnp.int32) + slot
+    marks[8:16, :] = jnp.zeros((8, neurons), jnp.int32) + is_src
 
     def fill_table(device, carry):
         partner = jnp.int32(0)
@@ -415,7 +414,7 @@
             part_p[target, pl.ds(tile * 2, 2)] = value.reshape(2, 128, neurons)
 
         gradient(rx_p.at[1 if q == 0 else 0], full_p, rows_p, q, store)
-        pltpu.make_async_copy(part_p.at[target], out_p.at[target], out_s.at[target]).start()
+        pltpu.make_async_copy(part_p.at[target], out_p[target], out_s.at[target]).start()
 
     halves = pl.ds(0, 2)
     jobs = []
@@ -443,7 +442,7 @@
         scatter(10 + i, src, lambda m: mid.at[m])
         mid[me] = part[:, lax.div(me, n // 2), block(lax.rem(me, n // 2), piece), size]
         for q in range(3):
-            put(part.at[q, halves], out_m.at[q, :, :, spans[i]])
+            put(part.at[q, halves], out_m[q].at[:, :, spans[i]])
 
     def back_hop(i):
         far, size = g_far[i], pl.ds(spans[i].start, cols - cut[i])
@@ -571,7 +570,7 @@
             mix_outputs()
         landed(13 + i, g_mid[i].at[peers])
         for q in range(3):
-            put(g_far[i].at[q], out_m.at[q, :, :, pl.ds(tail + spans[i].start + cut[i], cols - cut[i])])
+            put(g_far[i].at[q], out_m[q].at[:, :, pl.ds(tail + spans[i].start + cut[i], cols - cut[i])])
 
     left_here(1, sx_p.at[1, all_p])
     left_here(9, sx_m.at[1, all_m])
@@ -582,7 +581,7 @@
     for ring in rings:
         ring.sent((4, 5, 6, 7))
     for q in range(3):
-        pltpu.make_async_copy(part_p.at[q], out_p.at[q], out_s.at[q]).wait()
+        pltpu.make_async_copy(part_p.at[q], out_p[q], out_s.at[q]).wait()
     for job in jobs:
         job.wait()
 
@@ -614,12 +613,12 @@
         mega_kernel,
         out_shape=(
             jax.ShapeDtypeStruct(tokens.shape, BF),
-            jax.ShapeDtypeStruct((1,), jnp.int32),
-            jax.ShapeDtypeStruct((3, width // 128, 128, neurons), BF),
-            jax.ShapeDtypeStruct((3, 2, width // 2, neurons), BF),
+            jax.ShapeDtypeStruct((16, neurons), jnp.int32),
+            *[jax.ShapeDtypeStruct((width // 128, 128, neurons), BF)] * 3,
+            *[jax.ShapeDtypeStruct((2, width // 2, neurons), BF)] * 3,
         ),
         in_specs=[smem] * 2 + [vmem] * 5 + [hbm] * 3,
-        out_specs=(vmem, smem, hbm, hbm),
+        out_specs=(vmem, vmem, *[hbm] * 6),
         scratch_shapes=[
             pltpu.SMEM((n,), jnp.int32),
             pltpu.VMEM((3, *gate.shape), BF),
@@ -666,7 +665,7 @@
     exp_local, width, neurons = gate_weight.shape
     tok_local, top_count = routing.shape
     depth = max(2, tok_local * top_count * 4 // (3 * exp_local * devices_n))
-    mixed, role, grads_p, grads_m = mega(
+    mixed, marks, *grads = mega(
         merge_source,
         merge_target,
         neuron_perm,
@@ -680,16 +679,14 @@
         devices_n,
         depth,
     )
-    grads_p = grads_p.reshape(3, width, neurons)
-    grads_m = grads_m.reshape(3, width, neurons)
-
-    role = role[0]
-    place = jnp.arange(exp_local, dtype=jnp.int32)[:, None, None]
-    is_merge = place == role % 2
+    slot, is_source = marks[0][None, None, :], marks[8][None, None, :] > 0
+    is_merge = jnp.arange(exp_local, dtype=jnp.int32)[:, None, None] == slot
 
     def final(q):
-        merged = jnp.where(role >= 2, jnp.zeros((), BF), grads_m[q][None])
-        return jnp.where(is_merge, merged, grads_p[q][None])
+        plain = grads[q].reshape(1, width, neurons)
+        merged = grads[3 + q].reshape(1, width, neurons)
+        rest = jnp.where(is_merge, jnp.zeros((), BF), plain)
+        return jnp.where(is_merge & ~is_source, merged, rest)
 
     return (mixed, final(0), final(1), final(2))
 

time: 204 us -> 193 us (0.946)
  Pallas kernels: 192 us -> 184 us
  between operations: 3.2 us -> 0.67 us
    pallas_call x1, Pallas kernels: 192 us -> 184 us  [mega(): pl.pallas_call(mega_kernel, out_shape=(jax.ShapeDtypeStruct(tokens.shape,...]
    select_n x2 -> x1, other arithmetic: 6.69 us -> 6.26 us  [final(): return jnp.where(is_merge & ~is_source, merged, rest)]
where the time goes in v7:
time: 193 us
  Pallas kernels  184 us (95%)
  other arithmetic  7.1 us (4%)
    pallas_call x1, Pallas kernels, mega(): pl.pallas_call(mega_kernel, out_shape=(jax.ShapeDtypeStruct(tokens.shape,...  184 us
    select_n x1, other arithmetic, final(): return jnp.where(is_merge & ~is_source, merged, rest)  6.26 us

profile of v7, /device:TPU:1, one launch (start us, length us, event | category | flops | bytes accessed | tf_op | source)
XLA Modules:
  0.0 193.2 jit_solution(4975187693413830901)
XLA Ops:
  0.6 184.0 %shard_map.129 = (bf16[128,512]{1,0:T(8,128)(2,1)}, s32[16,1408]{1,0:T(8,128)}, bf16[4,128,1408]{2,1,0:T(8,128)(2,1)}, bf16[4,128,1408]{2,1,0:T(8,128)(2,1)}, bf...) custom-call(s32[16]{0:T(128)} %sources.1, ...), custom_call_target="tpu_custom_call" | custom-call | tf_op jit(solution)/shard_map/pallas_call | solution.py:612
  184.6 0.8 not_reduce_fusion
  185.4 0.8 slice_reduce_fusion
  186.3 0.0 copy-start
  186.3 6.3 %select_select_fusion = (bf16[2,512,1408]{2,1,0:T(8,128)(2,1)}, bf16[2,512,1408]{2,1,0:T(8,128)(2,1)}, bf16[2,512,1408]{2,1,0:T(8,128)(2,1)}) fusion(pred[2,1408]{1,0:T(4,128)(4,1)S(1)} %get-tuple-element.21, pred[2,1408]{1,0:T(4,128)(4,1)S(1)} %get-tuple-element.20, bf16[512,1408]{1,0:T(8,128)(2,1)} %bitcast.10, bf16[512,1408]{1,0:T(8,128)(2,1)} %bitcast.13, ...), kind=kLoop, calls=%fused_computation | loop fusion | flops 8650752 | bytes 17307136 | tf_op jit(solution)/shard_map/jit(_where)/select_n | solution.py:689
  192.5 0.0 copy-done
  192.5 0.7 copy.15
  (1 shorter events, 0.0 us)
Async XLA Ops:
  186.3 6.3 %copy-start = (bf16[128,512]{1,0:T(8,128)(2,1)S(1)}, bf16[128,512]{1,0:T(8,128)(2,1)}, u32[]{:S(2)}) copy-start(bf16[128,512]{1,0:T(8,128)(2,1)} %get-tuple-element.29) | copy-start | bytes 393220

commit v8 on v7

--- a/solution.py
+++ b/solution.py
@@ -297,8 +297,8 @@
         at_s, at_t = lax.shift_right_logical(s, 1) == me, lax.shift_right_logical(t, 1) == me
         slot = jnp.where(at_s, s & 1, jnp.where(at_t, t & 1, slot))
         is_src = jnp.where(at_s, 1, is_src)
-    marks[0:8, :] = jnp.zeros((8, neurons), jnp.int32) + slot
-    marks[8:16, :] = jnp.zeros((8, neurons), jnp.int32) + is_src
+    held = lax.broadcasted_iota(jnp.int32, marks.shape, 0)
+    marks[...] = jnp.where(held == slot, 1 + is_src, 0)
 
     def fill_table(device, carry):
         partner = jnp.int32(0)
@@ -613,7 +613,7 @@
         mega_kernel,
         out_shape=(
             jax.ShapeDtypeStruct(tokens.shape, BF),
-            jax.ShapeDtypeStruct((16, neurons), jnp.int32),
+            jax.ShapeDtypeStruct((gate.shape[0], neurons), jnp.int32),
             *[jax.ShapeDtypeStruct((width // 128, 128, neurons), BF)] * 3,
             *[jax.ShapeDtypeStruct((2, width // 2, neurons), BF)] * 3,
         ),
@@ -679,14 +679,13 @@
         devices_n,
         depth,
     )
-    slot, is_source = marks[0][None, None, :], marks[8][None, None, :] > 0
-    is_merge = jnp.arange(exp_local, dtype=jnp.int32)[:, None, None] == slot
+    marks = marks[:, None, :]
 
     def final(q):
         plain = grads[q].reshape(1, width, neurons)
         merged = grads[3 + q].reshape(1, width, neurons)
-        rest = jnp.where(is_merge, jnp.zeros((), BF), plain)
-        return jnp.where(is_merge & ~is_source, merged, rest)
+        rest = jnp.where(marks == 2, jnp.zeros((), BF), plain)
+        return jnp.where(marks == 1, merged, rest)
 
     return (mixed, final(0), final(1), final(2))
 

time: 193 us -> 192 us (level)
  no operation moved by 1% of the time
where the time goes in v8:
time: 192 us
  Pallas kernels  184 us (96%)
  other arithmetic  6.98 us (4%)
    pallas_call x1, Pallas kernels, mega(): pl.pallas_call(mega_kernel, out_shape=(jax.ShapeDtypeStruct(tokens.shape,...  184 us
    select_n x1, other arithmetic, final(): return jnp.where(marks == 1, merged, rest)  6.26 us

profile of v8, /device:TPU:1, one launch (start us, length us, event | category | flops | bytes accessed | tf_op | source)
XLA Modules:
  0.0 192.3 jit_solution(5787558327409519224)
XLA Ops:
  0.6 184.0 %shard_map.129 = (bf16[128,512]{1,0:T(8,128)(2,1)}, s32[2,1408]{1,0:T(2,128)}, bf16[4,128,1408]{2,1,0:T(8,128)(2,1)}, bf16[4,128,1408]{2,1,0:T(8,128)(2,1)}, bf1...) custom-call(s32[16]{0:T(128)} %sources.1, ...), custom_call_target="tpu_custom_call" | custom-call | tf_op jit(solution)/shard_map/pallas_call | solution.py:612
  184.6 0.7 broadcast_compare_fusion.1
  185.3 0.0 copy-start
  185.3 6.3 %select_select_fusion = (bf16[2,512,1408]{2,1,0:T(8,128)(2,1)}, bf16[2,512,1408]{2,1,0:T(8,128)(2,1)}, bf16[2,512,1408]{2,1,0:T(8,128)(2,1)}) fusion(pred[2,1408]{1,0:T(4,128)(4,1)S(1)} %get-tuple-element.24, pred[2,1408]{1,0:T(4,128)(4,1)S(1)} %get-tuple-element.23, bf16[512,1408]{1,0:T(8,128)(2,1)} %bitcast.10, bf16[512,1408]{1,0:T(8,128)(2,1)} %bitcast.13, ...), kind=kLoop, calls=%fused_computation | loop fusion | flops 8650752 | bytes 17307136 | tf_op jit(solution)/shard_map/jit(_where)/select_n | solution.py:688
  191.6 0.0 copy-done
  191.6 0.7 copy.15
Async XLA Ops:
  185.3 6.3 %copy-start = (bf16[128,512]{1,0:T(8,128)(2,1)S(1)}, bf16[128,512]{1,0:T(8,128)(2,1)}, u32[]{:S(2)}) copy-start(bf16[128,512]{1,0:T(8,128)(2,1)} %get-tuple-element.29) | copy-start | bytes 393220
